TPU v7x, 128 devices: a whole 4x4x4 slice. The times are simulated.
128 devices in a mesh: grp: 16 (over x, y), chan: 8 (over z, core).
Axes of the slice: x: 4, y: 4, z: 4, core: 2. Of those that a mesh axis runs over, the one named last changes fastest.
Arguments:
- spectra: bfloat16 [2048, 2, 2, 8192], P(('grp', 'chan')), may hold values from -45 to 45
- pair_blocks: int32 [16, 8, 18, 2], P('grp', 'chan'), may hold values from 0 to 63
- owners: int32 [16, 8, 18, 1], P('grp', 'chan'), may hold values from 0 to 15; in each aligned block of 18 rows (0 to 17, 18 to 35, ..., all dimensions but the last counted through in order) at most 3 rows name the same one
Outputs:
- stacks: float32 [16, 8, 48, 4, 1024], P('grp', 'chan')
Inputs may be any that keep to these rules, and one draw needn't show every extreme that they name: `owners`: at most 3 of one device's 18 pair blocks name the same owner.
All inputs are finite; a program needn't handle non-finite values.
Results may differ from a plain program's by a relative error of at most 0.011.
Values may be sent and summed in bfloat16 or wider, within the bound.
A program may use at most 128 MiB of HBM per device.

v0:
```python
import jax
import jax.numpy as jnp
from jax import lax
from jax.experimental import pallas as pl
from jax.experimental.pallas import tpu as pltpu
from jax.sharding import PartitionSpec as P

F = 8192
LAGS = 1024
BLK = 2
NB_SRC = 18
MOST = 3
WINDOWS = 2
FINE = 128


def phase_angle(bins, lag_index):
    phase = bins[:, None] * lag_index[None, :] % (2 * F)
    return phase.astype(jnp.float32) * (jnp.pi / F)


def table_slice(start, count):
    lag_index = jnp.arange(LAGS, dtype=jnp.int32) - LAGS // 2
    coarse = phase_angle(start + FINE * jnp.arange(count // FINE, dtype=jnp.int32), lag_index)
    fine = phase_angle(jnp.arange(FINE, dtype=jnp.int32), lag_index)
    cos_a, sin_a = jnp.cos(coarse)[:, None, :], jnp.sin(coarse)[:, None, :]
    cos_b, sin_b = jnp.cos(fine)[None, :, :], jnp.sin(fine)[None, :, :]
    cos_ab = (cos_a * cos_b - sin_a * sin_b).reshape(count, LAGS)
    sin_ab = (sin_a * cos_b + cos_a * sin_b).reshape(count, LAGS)
    bins = start + jnp.arange(count, dtype=jnp.int32)
    weight = (jnp.where(bins == 0, 1.0, 2.0).astype(jnp.float32) / jnp.sqrt(jnp.float32(F)))[:, None]
    cos_part = (cos_ab * weight).astype(jnp.bfloat16)
    sin_part = (-sin_ab * weight).astype(jnp.bfloat16)
    return cos_part, sin_part


def whiten(spectra):
    values = spectra.astype(jnp.float32)
    power = values[:, :, 0] ** 2 + values[:, :, 1] ** 2
    level = jnp.mean(power, axis=-1, keepdims=True) + 1e-05
    scale = lax.rsqrt(power + 0.1 * level)
    return (values * scale[:, :, None, :]).astype(jnp.bfloat16)


def pair_kernel(left_hot, right_hot, panel, cos_ref, sin_ref, out_ref, left_rows, right_rows):
    part = cos_ref.shape[0]
    kinds = BLK * WINDOWS * 2
    for kind in range(kinds):
        cols = panel[:, kind * part:(kind + 1) * part]
        left_rows[kind] = jnp.dot(left_hot[...], cols, preferred_element_type=jnp.float32)
        right_rows[kind] = jnp.dot(right_hot[...], cols, preferred_element_type=jnp.float32)

    def one_pair(pq, carry):
        p = pq // BLK
        q = pq % BLK
        real_sum = None
        imag_sum = None
        for window in range(WINDOWS):
            ra = left_rows[(p * WINDOWS + window) * 2]
            ia = left_rows[(p * WINDOWS + window) * 2 + 1]
            rb = right_rows[(q * WINDOWS + window) * 2]
            ib = right_rows[(q * WINDOWS + window) * 2 + 1]
            real = (ra * rb + ia * ib).astype(jnp.bfloat16).astype(jnp.float32)
            imag = (ia * rb - ra * ib).astype(jnp.bfloat16).astype(jnp.float32)
            real_sum = real if real_sum is None else real_sum + real
            imag_sum = imag if imag_sum is None else imag_sum + imag
        real_stack = (real_sum / WINDOWS).astype(jnp.bfloat16)
        imag_stack = (imag_sum / WINDOWS).astype(jnp.bfloat16)
        total = jnp.dot(real_stack, cos_ref[...], preferred_element_type=jnp.float32)
        total = total + jnp.dot(imag_stack, sin_ref[...], preferred_element_type=jnp.float32)
        listed = out_ref.shape[2]
        for chan in range(out_ref.shape[0]):
            out_ref[chan, pq] = total[chan * listed:(chan + 1) * listed]
        return carry

    lax.fori_loop(0, BLK * BLK, one_pair, 0)


def pair_correlations(left_hot, right_hot, panel, cos_part, sin_part, chan_count):
    count = left_hot.shape[0]
    part = cos_part.shape[0]
    kinds = BLK * WINDOWS * 2
    vmem = pl.BlockSpec(memory_space=pltpu.VMEM)
    flops = 2 * count * panel.shape[0] * panel.shape[1] * 2 + 2 * 2 * BLK * BLK * count * part * LAGS
    return pl.pallas_call(
        pair_kernel,
        out_shape=jax.ShapeDtypeStruct((chan_count, BLK * BLK, count // chan_count, LAGS), jnp.float32),
        in_specs=[vmem] * 5,
        out_specs=vmem,
        scratch_shapes=[
            pltpu.VMEM((kinds, count, part), jnp.float32),
            pltpu.VMEM((kinds, count, part), jnp.float32),
        ],
        compiler_params=pltpu.CompilerParams(vmem_limit_bytes=56 * 1024 * 1024),
        cost_estimate=pl.CostEstimate(
            flops=flops,
            transcendentals=0,
            bytes_accessed=panel.size * 2 + 4 * part * LAGS + BLK * BLK * count * LAGS * 4,
        ),
    )(left_hot, right_hot, panel, cos_part, sin_part)


def local(spectra, pair_blocks, owners):
    groups_count = lax.axis_size("grp")
    chan_count = lax.axis_size("chan")
    slot_count = groups_count * MOST
    pairs = BLK * BLK
    part = F // chan_count
    me = lax.axis_index("chan")

    white = whiten(spectra)
    channels = white.shape[0]
    chunks = white.reshape(channels, WINDOWS, 2, chan_count, part).transpose(3, 0, 1, 2, 4)
    chunks = chunks.reshape(chan_count, channels * WINDOWS * 2, part)
    listed = pair_blocks[0, 0].reshape(-1).astype(jnp.bfloat16)
    extra = jnp.zeros((part,), jnp.bfloat16).at[: listed.shape[0]].set(listed)
    extra = jnp.broadcast_to(extra[None, None, :], (chan_count, 1, part))
    sent = jnp.concatenate([chunks, extra], axis=1)
    got = lax.all_to_all(sent, "chan", split_axis=0, concat_axis=0, tiled=True)
    rows_per = channels * WINDOWS * 2
    blocks_count = chan_count * channels // BLK
    panel = got[:, :rows_per].reshape(blocks_count, BLK * WINDOWS * 2 * part)
    all_blocks = got[:, rows_per, : NB_SRC * 2].astype(jnp.float32).astype(jnp.int32)
    all_blocks = all_blocks.reshape(chan_count * NB_SRC, 2)
    block_ids = jnp.arange(blocks_count, dtype=jnp.int32)[None, :]
    left_hot = (all_blocks[:, 0][:, None] == block_ids).astype(jnp.bfloat16)
    right_hot = (all_blocks[:, 1][:, None] == block_ids).astype(jnp.bfloat16)

    cos_part, sin_part = table_slice(me * part, part)
    partial = pair_correlations(left_hot, right_hot, panel, cos_part, sin_part, chan_count)
    partial = partial.reshape(chan_count, pairs * NB_SRC, LAGS)
    corr = lax.psum_scatter(partial, "chan", scatter_dimension=0, tiled=True)
    corr = corr.reshape(pairs, NB_SRC, LAGS).transpose(1, 0, 2).reshape(NB_SRC, pairs * LAGS)

    owner_list = owners[0, 0, :, 0]
    same = owner_list[:, None] == owner_list[None, :]
    earlier = jnp.arange(NB_SRC)[None, :] < jnp.arange(NB_SRC)[:, None]
    order_rank = jnp.sum(jnp.logical_and(same, earlier), axis=1)
    slot_ids = owner_list * MOST + order_rank
    chooser = slot_ids[None, :] == jnp.arange(slot_count, dtype=jnp.int32)[:, None]
    source = jnp.argmax(chooser, axis=1)
    filled = jnp.any(chooser, axis=1)
    placed = jnp.where(filled[:, None], jnp.take(corr, source, axis=0), 0.0)
    placed = placed.reshape(groups_count, MOST, pairs, LAGS)
    received = lax.all_to_all(placed, "grp", split_axis=0, concat_axis=0, tiled=True)
    return received.reshape(1, 1, slot_count, pairs, LAGS)


def solution(mesh):
    return jax.shard_map(
        local,
        mesh=mesh,
        in_specs=(
            P(("grp", "chan"), None, None, None),
            P("grp", "chan", None, None),
            P("grp", "chan", None, None),
        ),
        out_specs=P("grp", "chan", None, None, None),
        check_vma=False,
    )
```

profile of v0, /device:TPU:0, one launch (start us, length us, event | category | flops | bytes accessed | tf_op | source)
XLA Modules:
  0.0 118.5 jit_solution(1375576141269606950)
XLA Ops:
  6.5 1.8 %copy_convert_fusion = f32[16,2,2,8192]{3,0,2,1:T(8,128)S(1)} fusion(bf16[16,2,2,8192]{3,2,1,0:T(2,128)(2,1)} %param.5), kind=kLoop, calls=%fused_computation.12 | loop fusion | flops 524288 | bytes 3145728 | tf_op jit(solution)/shard_map/convert_element_type | solution.py:38
  8.4 0.0 copy-start
  8.4 0.2 fusion.11
  8.6 0.3 rsqrt_bitcast_fusion
  8.9 0.7 copy-done
  9.6 0.6 multiply_convert_fusion
  10.2 0.6 copy.25
  10.8 0.0 copy-start.1
  10.9 1.1 copy.20
  11.9 0.4 reshape.245
  12.4 0.0 copy-done.1
  12.4 0.1 copy.21
  12.5 0.1 convert_element_type.70
  12.7 1.2 pad_maximum_fusion
  13.8 5.4 %all-to-all-start = ((bf16[8,65,1024]{2,1,0:T(8,128)(2,1)}), bf16[8,65,1024]{2,1,0:T(8,128)(2,1)S(1)}, u32[]{:S(2)}, u32[]{:S(2)}) async-start(bf16[8,65,1024]{2,1,0:T(8,128)(2,1)} %pad_maximum_fusion), calls=%async_computation | async-start | bytes 2359296 | tf_op jit(solution)/shard_map/all_to_all | solution.py:119
  19.2 0.2 reduce-scatter.2.cloned.1.call-start
  19.5 2.0 %fusion.10 = (f32[128,1024]{1,0:T(8,128)S(1)}, f32[128,1024]{1,0:T(8,128)S(1)}) fusion(s32[1024]{0:T(1024)S(1)} %iota_add_fusion), kind=kLoop, calls=%fused_computation.25 | loop fusion | flops 1835008 | bytes 1052672 | tf_op jit(solution)/shard_map/cos | solution.py:27
  21.5 0.2 fusion.18
  21.7 1.2 add_negate_fusion
  22.9 2.5 %fusion = (bf16[1024,1024]{1,0:T(8,128)(2,1)}, bf16[1024,1024]{1,0:T(8,128)(2,1)}) fusion(f32[8,128,1024]{2,1,0:T(8,128)S(1)} %get-tuple-element.21, f32[1024]{0:T(1024)S(1)} %select_multiply_fusion, f32[8,128,1024]{2,1,0:T(8,128)S(1)} %get-tuple-element.22), kind=kLoop, calls=%fused_computation.2 | loop fusion | flops 4194304 | bytes 12587008 | tf_op jit(solution)/shard_map/convert_element_type | solution.py:33
  25.5 11.1 %all-to-all-done = bf16[8,65,1024]{2,1,0:T(8,128)(2,1)S(1)} async-done(((bf16[8,65,1024]{2,1,0:T(8,128)(2,1)}), bf16[8,65,1024]{2,1,0:T(8,128)(2,1)S(1)}, u32[]{:S(2)}, u32[]{:S(2)}) %all-to-all-start) | async-done | bytes 1064992 | tf_op jit(solution)/shard_map/all_to_all | solution.py:119
  36.6 0.1 convert_element_type.73
  36.7 0.2 slice_reduce_fusion
  36.9 0.1 slice.42
  37.0 1.3 %reshape.246.panel = bf16[64,8192]{1,0:T(8,128)(2,1)} reshape(bf16[8,64,1024]{2,1,0:T(8,128)(2,1)S(1)} %slice.42) | data formatting | bytes 2097152 | tf_op jit(solution)/shard_map/reshape | solution.py:122
  38.4 0.7 fusion.12
  39.1 10.4 %shard_map.37 = f32[8,4,18,1024]{3,2,1,0:T(8,128)} custom-call(bf16[144,64]{1,0:T(8,128)(2,1)} %get-tuple-element.29.left_hot, bf16[144,64]{1,0:T(8,128)(2,1)} %get-tuple-element.30.right_hot, bf16[64,8192]{1,0:T(8,128)(2,1)} %reshape.246.panel, bf16[1024,1024]{1,0:T(8,128)(2,1)} %get-tuple-element.26.cos_ref, bf16[1024,1024]{1,0:T(8,128)(2,1)} %get-tuple-element.25.sin_ref), custom_call_target="tpu_custom_call" | custom-call | flops 2717908992 | bytes 7602176 | tf_op jit(solution)/shard_map/pallas_call | solution.py:85
  49.5 3.3 %copy.22 = f32[8,4,18,1024]{3,0,2,1:T(8,128)S(1)} copy(f32[8,4,18,1024]{3,2,1,0:T(8,128)} %shard_map.37) | data formatting | bytes 4718592 | tf_op jit(solution)/shard_map/pallas_call | solution.py:85
  52.8 2.8 %copy.23 = f32[8,72,1024]{2,1,0:T(8,128)} copy(f32[8,72,1024]{2,0,1:T(8,128)S(1)} %bitcast.28) | data formatting | bytes 4718592 | tf_op jit(solution)/shard_map/reshape | solution.py:131
  55.6 0.0 copy-start.2
  55.6 0.0 reduce-scatter.2.cloned.1.call-update
  55.6 0.6 copy-done.2
  56.2 0.2 convert_reduce_fusion
  56.4 0.6 iota_reduce_fusion
  57.0 0.1 broadcast_in_dim.62
  57.1 0.1 fusion.19
  57.2 0.1 broadcast_in_dim.34
  57.3 32.3 %reduce-scatter.2.cloned.1.call-done = f32[1,72,1024]{2,1,0:T(8,128)} async-done(((f32[8,72,1024]{2,1,0:T(8,128)}), f32[1,72,1024]{2,1,0:T(8,128)}) %reduce-scatter.2.cloned.1.call-update) | async-done | bytes 294928 | tf_op jit(solution)/shard_map/reduce_scatter | solution.py:132
  89.7 1.0 reshape.248
  90.7 0.2 copy.24
  90.9 0.1 pad.6
  91.0 0.2 copy.26
  91.2 0.8 gather_fusion
  92.0 0.5 gather.7
  92.6 0.3 select_select_fusion
  92.9 17.9 %all_to_all.10 = f32[16,3,4,1024]{3,2,1,0:T(4,128)S(1)} all-to-all(f32[16,3,4,1024]{3,2,1,0:T(4,128)S(1)} %select_select_fusion), channel_id=1, replica_groups=mesh['grp'=16,'chan'=8] {'grp'}, dimensions={0} | all-to-all | bytes 1572864 | tf_op jit(solution)/shard_map/all_to_all | solution.py:145
  110.7 0.9 copy.31
  (12 shorter events, 0.1 us)
Async XLA Ops:
  8.4 1.2 %copy-start = (bf16[16,2,2,8192]{3,2,1,0:T(2,128)(2,1)S(1)}, bf16[16,2,2,8192]{3,2,1,0:T(2,128)(2,1)}, u32[]{:S(2)}) copy-start(bf16[16,2,2,8192]{3,2,1,0:T(2,128)(2,1)} %param.5) | copy-start | bytes 3145732
  10.8 1.5 %copy-start.1 = (s32[1,1,18,2]{2,3,1,0:T(2,128)S(1)}, s32[1,1,18,2]{2,3,1,0:T(2,128)}, u32[]{:S(2)}) copy-start(s32[1,1,18,2]{2,3,1,0:T(2,128)} %param.6) | copy-start | bytes 436
  13.8 22.8 %all-to-all-start = ((bf16[8,65,1024]{2,1,0:T(8,128)(2,1)}), bf16[8,65,1024]{2,1,0:T(8,128)(2,1)S(1)}, u32[]{:S(2)}, u32[]{:S(2)}) async-start(bf16[8,65,1024]{2,1,0:T(8,128)(2,1)} %pad_maximum_fusion), calls=%async_computation | async-start | bytes 2359296 | tf_op jit(solution)/shard_map/all_to_all | solution.py:119
  19.2 70.5 %reduce-scatter.2.cloned.1.call-start = ((), (), s32[]{:S(2)}) async-start(), calls=%async_computation.3 | async-start | bytes 2654208 | tf_op jit(solution)/shard_map/reduce_scatter | solution.py:132
  55.6 0.7 copy-start.2
Sparse Core Ops, SparseCore 0:
  55.7 33.9 reduce-scatter.1
where the time goes:
time: 119 us; the launch traced here: 118 us
  waiting for transfers between devices  43.5 us (37%)
  blocking collectives  17.9 us (15%)
  local copies, waits for them, and re-layouts  15.4 us (13%)
  between operations  13.6 us (11%)
  other arithmetic  12.1 us (10%)
  Pallas kernels  10.4 us (9%)
  starting transfers between devices  5.61 us (5%)
    reduce_scatter x1, waiting for transfers between devices, local(): corr = lax.psum_scatter(partial, 'chan', scatter_dimension=0, tiled=True)  32.3 us
    all_to_all x1, blocking collectives, local(): lax.all_to_all(placed, 'grp', split_axis=0, concat_axis=0, tiled=True)  17.9 us
    all_to_all x1, waiting for transfers between devices, local(): got = lax.all_to_all(sent, 'chan', split_axis=0, concat_axis=0, tiled=True)  11.1 us
    pallas_call x1, Pallas kernels, pair_correlations(): pl.pallas_call(pair_kernel, out_shape=jax.ShapeDtypeStruct((chan_count, B...  10.4 us
    all_to_all x1, starting transfers between devices, local(): got = lax.all_to_all(sent, 'chan', split_axis=0, concat_axis=0, tiled=True)  5.4 us
    pallas_call x1, local copies, waits for them, and re-layouts, pair_correlations(): pl.pallas_call(pair_kernel, out_shape=jax.ShapeDtypeStruct((chan_count, B...  3.26 us
    unnamed x10, local copies, waits for them, and re-layouts  3.12 us
    reshape x1, local copies, waits for them, and re-layouts, local(): partial = partial.reshape(chan_count, pairs * NB_SRC, LAGS)  2.78 us
  transfers between devices with their start and end apart: 2, of which 2 were waited for; matrix products, arithmetic and copies ran while one was open for 6% of the time, Pallas kernels for 0%

commit v1 on v0

--- a/solution.py
+++ b/solution.py
@@ -12,6 +12,7 @@
 MOST = 3
 WINDOWS = 2
 FINE = 128
+ROW_CHUNK = 144
 
 
 def phase_angle(bins, lag_index):
@@ -42,24 +43,25 @@
     return (values * scale[:, :, None, :]).astype(jnp.bfloat16)
 
 
-def pair_kernel(left_hot, right_hot, panel, cos_ref, sin_ref, out_ref, left_rows, right_rows):
+def pair_kernel(left_hot, right_hot, panel, cos_ref, sin_ref, out_ref):
     part = cos_ref.shape[0]
-    kinds = BLK * WINDOWS * 2
-    for kind in range(kinds):
-        cols = panel[:, kind * part:(kind + 1) * part]
-        left_rows[kind] = jnp.dot(left_hot[...], cols, preferred_element_type=jnp.float32)
-        right_rows[kind] = jnp.dot(right_hot[...], cols, preferred_element_type=jnp.float32)
+    chunk = ROW_CHUNK
 
-    def one_pair(pq, carry):
-        p = pq // BLK
-        q = pq % BLK
+    def rows_of(hot, window, kind):
+        col = (window * 2 + kind) * part
+        return jnp.dot(hot, panel[:, col:col + part], preferred_element_type=jnp.float32)
+
+    def one_chunk(step, carry):
+        at = pl.multiple_of(step * chunk, chunk)
+        left = left_hot[pl.ds(at, chunk), :]
+        right = right_hot[pl.ds(at, chunk), :]
         real_sum = None
         imag_sum = None
         for window in range(WINDOWS):
-            ra = left_rows[(p * WINDOWS + window) * 2]
-            ia = left_rows[(p * WINDOWS + window) * 2 + 1]
-            rb = right_rows[(q * WINDOWS + window) * 2]
-            ib = right_rows[(q * WINDOWS + window) * 2 + 1]
+            ra = rows_of(left, window, 0)
+            ia = rows_of(left, window, 1)
+            rb = rows_of(right, window, 0)
+            ib = rows_of(right, window, 1)
             real = (ra * rb + ia * ib).astype(jnp.bfloat16).astype(jnp.float32)
             imag = (ia * rb - ra * ib).astype(jnp.bfloat16).astype(jnp.float32)
             real_sum = real if real_sum is None else real_sum + real
@@ -68,34 +70,27 @@
         imag_stack = (imag_sum / WINDOWS).astype(jnp.bfloat16)
         total = jnp.dot(real_stack, cos_ref[...], preferred_element_type=jnp.float32)
         total = total + jnp.dot(imag_stack, sin_ref[...], preferred_element_type=jnp.float32)
-        listed = out_ref.shape[2]
-        for chan in range(out_ref.shape[0]):
-            out_ref[chan, pq] = total[chan * listed:(chan + 1) * listed]
+        out_ref[pl.ds(at, chunk), :] = total.astype(out_ref.dtype)
         return carry
 
-    lax.fori_loop(0, BLK * BLK, one_pair, 0)
+    lax.fori_loop(0, out_ref.shape[0] // chunk, one_chunk, 0)
 
 
-def pair_correlations(left_hot, right_hot, panel, cos_part, sin_part, chan_count):
-    count = left_hot.shape[0]
+def pair_correlations(left_hot, right_hot, panel, cos_part, sin_part):
+    rows = left_hot.shape[0]
     part = cos_part.shape[0]
-    kinds = BLK * WINDOWS * 2
     vmem = pl.BlockSpec(memory_space=pltpu.VMEM)
-    flops = 2 * count * panel.shape[0] * panel.shape[1] * 2 + 2 * 2 * BLK * BLK * count * part * LAGS
+    flops = 2 * 2 * rows * panel.shape[0] * panel.shape[1] + 2 * 2 * rows * part * LAGS
     return pl.pallas_call(
         pair_kernel,
-        out_shape=jax.ShapeDtypeStruct((chan_count, BLK * BLK, count // chan_count, LAGS), jnp.float32),
+        out_shape=jax.ShapeDtypeStruct((rows, LAGS), jnp.bfloat16),
         in_specs=[vmem] * 5,
         out_specs=vmem,
-        scratch_shapes=[
-            pltpu.VMEM((kinds, count, part), jnp.float32),
-            pltpu.VMEM((kinds, count, part), jnp.float32),
-        ],
         compiler_params=pltpu.CompilerParams(vmem_limit_bytes=56 * 1024 * 1024),
         cost_estimate=pl.CostEstimate(
             flops=flops,
             transcendentals=0,
-            bytes_accessed=panel.size * 2 + 4 * part * LAGS + BLK * BLK * count * LAGS * 4,
+            bytes_accessed=panel.size * 2 + 4 * part * LAGS + rows * LAGS * 2,
         ),
     )(left_hot, right_hot, panel, cos_part, sin_part)
 
@@ -118,19 +113,22 @@
     sent = jnp.concatenate([chunks, extra], axis=1)
     got = lax.all_to_all(sent, "chan", split_axis=0, concat_axis=0, tiled=True)
     rows_per = channels * WINDOWS * 2
-    blocks_count = chan_count * channels // BLK
-    panel = got[:, :rows_per].reshape(blocks_count, BLK * WINDOWS * 2 * part)
+    group_channels = chan_count * channels
+    panel = got[:, :rows_per].reshape(group_channels, WINDOWS * 2 * part)
     all_blocks = got[:, rows_per, : NB_SRC * 2].astype(jnp.float32).astype(jnp.int32)
-    all_blocks = all_blocks.reshape(chan_count * NB_SRC, 2)
-    block_ids = jnp.arange(blocks_count, dtype=jnp.int32)[None, :]
-    left_hot = (all_blocks[:, 0][:, None] == block_ids).astype(jnp.bfloat16)
-    right_hot = (all_blocks[:, 1][:, None] == block_ids).astype(jnp.bfloat16)
+    all_blocks = all_blocks.reshape(chan_count * NB_SRC, 1, 2)
+    offsets = jnp.arange(BLK, dtype=jnp.int32)
+    left_ch = (all_blocks[:, :, 0] * BLK + offsets[None, :])[:, :, None] + jnp.zeros((1, 1, BLK), jnp.int32)
+    right_ch = (all_blocks[:, :, 1] * BLK + offsets[None, :])[:, None, :] + jnp.zeros((1, BLK, 1), jnp.int32)
+    channel_ids = jnp.arange(group_channels, dtype=jnp.int32)[None, :]
+    left_hot = (left_ch.reshape(-1, 1) == channel_ids).astype(jnp.bfloat16)
+    right_hot = (right_ch.reshape(-1, 1) == channel_ids).astype(jnp.bfloat16)
 
     cos_part, sin_part = table_slice(me * part, part)
-    partial = pair_correlations(left_hot, right_hot, panel, cos_part, sin_part, chan_count)
-    partial = partial.reshape(chan_count, pairs * NB_SRC, LAGS)
+    partial = pair_correlations(left_hot, right_hot, panel, cos_part, sin_part)
+    partial = partial.reshape(chan_count, NB_SRC * pairs, LAGS)
     corr = lax.psum_scatter(partial, "chan", scatter_dimension=0, tiled=True)
-    corr = corr.reshape(pairs, NB_SRC, LAGS).transpose(1, 0, 2).reshape(NB_SRC, pairs * LAGS)
+    corr = corr.reshape(NB_SRC, pairs * LAGS).astype(jnp.float32)
 
     owner_list = owners[0, 0, :, 0]
     same = owner_list[:, None] == owner_list[None, :]

time: 119 us -> 112 us (0.941)
  local copies, waits for them, and re-layouts: 15.4 us -> 8.75 us
  waiting for transfers between devices: 43.5 us -> 42.1 us
    reshape x3 -> x1, local copies, waits for them, and re-layouts: 5.11 us -> 1.45 us  [local(): panel = got[:, :rows_per].reshape(group_channels, WINDOWS * 2 * part)]
    pallas_call x1 -> x0, local copies, waits for them, and re-layouts: 3.26 us -> none  [pair_correlations(): pl.pallas_call(pair_kernel, out_shape=jax.ShapeDtypeStruct((chan_count, B...]
    reduce_scatter x1, waiting for transfers between devices: 32.3 us -> 30.8 us  [local(): corr = lax.psum_scatter(partial, 'chan', scatter_dimension=0, tiled=True)]
    unnamed x10 -> x8, local copies, waits for them, and re-layouts: 3.12 us -> 2.19 us
where the time goes in v1:
time: 112 us
  waiting for transfers between devices  42.1 us (38%)
  blocking collectives  17.9 us (16%)
  between operations  13.6 us (12%)
  other arithmetic  13.2 us (12%)
  Pallas kernels  10.8 us (10%)
  local copies, waits for them, and re-layouts  8.75 us (8%)
  starting transfers between devices  5.61 us (5%)
    reduce_scatter x1, waiting for transfers between devices, local(): corr = lax.psum_scatter(partial, 'chan', scatter_dimension=0, tiled=True)  30.8 us
    all_to_all x1, blocking collectives, local(): lax.all_to_all(placed, 'grp', split_axis=0, concat_axis=0, tiled=True)  17.9 us
    all_to_all x1, waiting for transfers between devices, local(): got = lax.all_to_all(sent, 'chan', split_axis=0, concat_axis=0, tiled=True)  11.2 us
    pallas_call x1, Pallas kernels, pair_correlations(): pl.pallas_call(pair_kernel, out_shape=jax.ShapeDtypeStruct((rows, LAGS),...  10.8 us
    all_to_all x1, starting transfers between devices, local(): got = lax.all_to_all(sent, 'chan', split_axis=0, concat_axis=0, tiled=True)  5.4 us
    convert_element_type x1, other arithmetic, table_slice(): sin_part = (-sin_ab * weight).astype(jnp.bfloat16)  2.45 us
  transfers between devices with their start and end apart: 2, of which 2 were waited for; matrix products, arithmetic and copies ran while one was open for 6% of the time, Pallas kernels for 0%

profile of v1, /device:TPU:0, one launch (start us, length us, event | category | flops | bytes accessed | tf_op | source)
XLA Modules:
  0.0 112.0 jit_solution(16091188549288055961)
XLA Ops:
  6.5 1.8 %copy_convert_fusion = f32[16,2,2,8192]{3,0,2,1:T(8,128)S(1)} fusion(bf16[16,2,2,8192]{3,2,1,0:T(2,128)(2,1)} %param.5), kind=kLoop, calls=%fused_computation.12 | loop fusion | flops 524288 | bytes 3145728 | tf_op jit(solution)/shard_map/convert_element_type | solution.py:39
  8.4 0.0 copy-start
  8.4 0.2 fusion.13
  8.6 0.3 rsqrt_bitcast_fusion
  8.9 0.7 copy-done
  9.6 0.6 multiply_convert_fusion
  10.2 0.6 copy.16
  10.8 0.0 copy-start.1
  10.9 1.1 copy.14
  11.9 0.4 reshape.313
  12.4 0.0 copy-done.1
  12.4 0.1 copy.15
  12.5 0.1 convert_element_type.88
  12.7 1.1 %pad_maximum_fusion = bf16[8,65,1024]{2,1,0:T(8,128)(2,1)} fusion(bf16[8,1,1024]{2,1,0:T(2,128)(2,1)S(1)} %broadcast_in_dim.38, bf16[8,64,1024]{2,1,0:T(8,128)(2,1)S(1)} %reshape.313), kind=kLoop, calls=%fused_computation.8 | loop fusion | flops 2129920 | bytes 2129920 | tf_op jit(solution)/shard_map/concatenate | solution.py:113
  13.8 5.4 %all-to-all-start = ((bf16[8,65,1024]{2,1,0:T(8,128)(2,1)}), bf16[8,65,1024]{2,1,0:T(8,128)(2,1)S(1)}, u32[]{:S(2)}, u32[]{:S(2)}) async-start(bf16[8,65,1024]{2,1,0:T(8,128)(2,1)} %pad_maximum_fusion), calls=%async_computation | async-start | bytes 2359296 | tf_op jit(solution)/shard_map/all_to_all | solution.py:114
  19.2 0.2 reduce-scatter.2.cloned.1.call-start
  19.5 2.0 %fusion.12 = (f32[128,1024]{1,0:T(8,128)S(1)}, f32[128,1024]{1,0:T(8,128)S(1)}) fusion(s32[1024]{0:T(1024)S(1)} %iota_add_fusion.2), kind=kLoop, calls=%fused_computation.29 | loop fusion | flops 1835008 | bytes 1052672 | tf_op jit(solution)/shard_map/cos | solution.py:28
  21.5 0.2 fusion.20
  21.7 1.2 %add_negate_fusion = (f32[8,128,1024]{2,1,0:T(8,128)S(1)}, f32[8,128,1024]{2,1,0:T(8,128)S(1)}) fusion(f32[128,1024]{1,0:T(8,128)S(1)} %get-tuple-element.28, f32[8,1024]{1,0:T(8,128)S(1)} %get-tuple-element.24, f32[128,1024]{1,0:T(8,128)S(1)} %get-tuple-element.27, f32[8,1024]{1,0:T(8,128)S(1)} %get-tuple-element.23), kind=kLoop, calls=%fused_computation.5 | loop fusion | flops 7340032 | bytes 9502720 | tf_op jit(solution)/shard_map/neg | solution.py:34
  22.9 2.4 %fusion = (bf16[1024,1024]{1,0:T(8,128)(2,1)}, bf16[1024,1024]{1,0:T(8,128)(2,1)}) fusion(f32[8,128,1024]{2,1,0:T(8,128)S(1)} %get-tuple-element.21, f32[1024]{0:T(1024)S(1)} %select_multiply_fusion, f32[8,128,1024]{2,1,0:T(8,128)S(1)} %get-tuple-element.22), kind=kLoop, calls=%fused_computation.2 | loop fusion | flops 4194304 | bytes 12587008 | tf_op jit(solution)/shard_map/convert_element_type | solution.py:34
  25.4 11.2 %all-to-all-done = bf16[8,65,1024]{2,1,0:T(8,128)(2,1)S(1)} async-done(((bf16[8,65,1024]{2,1,0:T(8,128)(2,1)}), bf16[8,65,1024]{2,1,0:T(8,128)(2,1)S(1)}, u32[]{:S(2)}, u32[]{:S(2)}) %all-to-all-start) | async-done | bytes 1064992 | tf_op jit(solution)/shard_map/all_to_all | solution.py:114
  36.6 0.1 convert_element_type.91
  36.7 0.2 fusion.14
  36.9 0.1 iota_add_fusion
  37.0 0.1 add.167
  37.1 0.2 eq.82
  37.3 0.8 fusion.10.right_hot
  38.1 0.2 add.163
  38.3 0.2 eq.78
  38.5 0.8 fusion.9.left_hot
  39.3 0.1 slice.42
  39.4 1.4 %reshape.314.panel = bf16[128,4096]{1,0:T(8,128)(2,1)} reshape(bf16[8,64,1024]{2,1,0:T(8,128)(2,1)S(1)} %slice.42) | data formatting | bytes 2097152 | tf_op jit(solution)/shard_map/reshape | solution.py:117
  40.9 0.0 copy-start.2
  40.9 10.8 %shard_map.37 = bf16[576,1024]{1,0:T(8,128)(2,1)} custom-call(bf16[576,128]{1,0:T(8,128)(2,1)} %fusion.9.left_hot, bf16[576,128]{1,0:T(8,128)(2,1)} %fusion.10.right_hot, bf16[128,4096]{1,0:T(8,128)(2,1)} %reshape.314.panel, bf16[1024,1024]{1,0:T(8,128)(2,1)} %get-tuple-element.26.cos_ref, bf16[1024,1024]{1,0:T(8,128)(2,1)} %get-tuple-element.25.sin_ref), custom_call_target="tpu_custom_call" | custom-call | flops 3623878656 | bytes 6422528 | tf_op jit(solution)/shard_map/pallas_call | solution.py:84
  51.7 0.0 reduce-scatter.2.cloned.1.call-update
  51.7 0.0 copy-done.2
  51.7 0.2 convert_reduce_fusion
  51.9 0.6 iota_reduce_fusion
  52.5 0.1 broadcast_in_dim.36
  52.6 0.1 fusion.21
  52.7 0.1 broadcast_in_dim.31
  52.8 30.8 %reduce-scatter.2.cloned.1.call-done = bf16[1,72,1024]{2,1,0:T(8,128)(2,1)} async-done(((bf16[8,72,1024]{2,1,0:T(8,128)(2,1)}), bf16[1,72,1024]{2,1,0:T(8,128)(2,1)}) %reduce-scatter.2.cloned.1.call-update) | async-done | bytes 147472 | tf_op jit(solution)/shard_map/reduce_scatter | solution.py:130
  83.7 1.0 reshape.317
  84.7 0.8 gather_fusion
  85.5 0.5 gather.7
  86.1 0.3 select_select_fusion
  86.4 17.9 %all_to_all.10 = f32[16,3,4,1024]{3,2,1,0:T(4,128)S(1)} all-to-all(f32[16,3,4,1024]{3,2,1,0:T(4,128)S(1)} %select_select_fusion), channel_id=1, replica_groups=mesh['grp'=16,'chan'=8] {'grp'}, dimensions={0} | all-to-all | bytes 1572864 | tf_op jit(solution)/shard_map/all_to_all | solution.py:143
  104.3 0.9 copy.21
  (12 shorter events, 0.1 us)
Async XLA Ops:
  8.4 1.2 %copy-start = (bf16[16,2,2,8192]{3,2,1,0:T(2,128)(2,1)S(1)}, bf16[16,2,2,8192]{3,2,1,0:T(2,128)(2,1)}, u32[]{:S(2)}) copy-start(bf16[16,2,2,8192]{3,2,1,0:T(2,128)(2,1)} %param.5) | copy-start | bytes 3145732
  10.8 1.5 %copy-start.1 = (s32[1,1,18,2]{2,3,1,0:T(2,128)S(1)}, s32[1,1,18,2]{2,3,1,0:T(2,128)}, u32[]{:S(2)}) copy-start(s32[1,1,18,2]{2,3,1,0:T(2,128)} %param.6) | copy-start | bytes 436
  13.8 22.8 %all-to-all-start = ((bf16[8,65,1024]{2,1,0:T(8,128)(2,1)}), bf16[8,65,1024]{2,1,0:T(8,128)(2,1)S(1)}, u32[]{:S(2)}, u32[]{:S(2)}) async-start(bf16[8,65,1024]{2,1,0:T(8,128)(2,1)} %pad_maximum_fusion), calls=%async_computation | async-start | bytes 2359296 | tf_op jit(solution)/shard_map/all_to_all | solution.py:114
  19.2 64.5 %reduce-scatter.2.cloned.1.call-start = ((), (), s32[]{:S(2)}) async-start(), calls=%async_computation.3 | async-start | bytes 1327104 | tf_op jit(solution)/shard_map/reduce_scatter | solution.py:130
  40.9 10.8 %copy-start.2 = (s32[1,1,18,1]{2,3,1,0:T(1,128)S(1)}, s32[1,1,18,1]{2,3,1,0:T(1,128)}, u32[]{:S(2)}) copy-start(s32[1,1,18,1]{2,3,1,0:T(1,128)} %param.7) | copy-start | bytes 220
Sparse Core Ops, SparseCore 0:
  51.8 31.8 reduce-scatter.1

commit v2 on v1

--- a/solution.py
+++ b/solution.py
@@ -1,3 +1,5 @@
+import functools
+
 import jax
 import jax.numpy as jnp
 from jax import lax
@@ -83,16 +85,77 @@
     flops = 2 * 2 * rows * panel.shape[0] * panel.shape[1] + 2 * 2 * rows * part * LAGS
     return pl.pallas_call(
         pair_kernel,
-        out_shape=jax.ShapeDtypeStruct((rows, LAGS), jnp.bfloat16),
+        out_shape=jax.ShapeDtypeStruct((rows, LAGS), jnp.float32),
         in_specs=[vmem] * 5,
         out_specs=vmem,
         compiler_params=pltpu.CompilerParams(vmem_limit_bytes=56 * 1024 * 1024),
         cost_estimate=pl.CostEstimate(
             flops=flops,
             transcendentals=0,
-            bytes_accessed=panel.size * 2 + 4 * part * LAGS + rows * LAGS * 2,
+            bytes_accessed=panel.size * 2 + 4 * part * LAGS + rows * LAGS * 4,
         ),
     )(left_hot, right_hot, panel, cos_part, sin_part)
+
+
+def exchange_kernel(axis, other_axis, axis_first, collective, x_ref, out_ref, local_sem, send_sem, recv_sem):
+    n = x_ref.shape[0]
+    me = lax.axis_index(axis)
+    other = lax.axis_index(other_axis)
+
+    def device(j):
+        return (j, other) if axis_first else (other, j)
+
+    barrier = pltpu.get_barrier_semaphore()
+    for step in range(1, n):
+        pl.semaphore_signal(barrier, inc=1, device_id=device(lax.rem(me + step, n)),
+                            device_id_type=pl.DeviceIdType.MESH)
+    pl.semaphore_wait(barrier, n - 1)
+
+    own = pltpu.make_async_copy(x_ref.at[me], out_ref.at[me], local_sem)
+    own.start()
+    copies = []
+    for step in range(1, n):
+        target = lax.rem(me + step, n)
+        copy = pltpu.make_async_remote_copy(
+            src_ref=x_ref.at[target],
+            dst_ref=out_ref.at[me],
+            send_sem=send_sem.at[step],
+            recv_sem=recv_sem.at[step],
+            device_id=device(target),
+            device_id_type=pl.DeviceIdType.MESH,
+        )
+        copy.start()
+        copies.append(copy)
+    own.wait()
+    for step in range(1, n):
+        source = lax.rem(me + n - step, n)
+        copies[step - 1].wait_send()
+        incoming = pltpu.make_async_remote_copy(
+            src_ref=x_ref.at[source],
+            dst_ref=out_ref.at[source],
+            send_sem=send_sem.at[step],
+            recv_sem=recv_sem.at[step],
+            device_id=device(source),
+            device_id_type=pl.DeviceIdType.MESH,
+        )
+        incoming.wait_recv()
+
+
+def exchange(x, axis, other_axis, axis_first, collective):
+    n = x.shape[0]
+    anywhere = pl.BlockSpec(memory_space=pl.ANY)
+    return pl.pallas_call(
+        functools.partial(exchange_kernel, axis, other_axis, axis_first, collective),
+        out_shape=jax.ShapeDtypeStruct(x.shape, x.dtype),
+        in_specs=[anywhere],
+        out_specs=anywhere,
+        scratch_shapes=[
+            pltpu.SemaphoreType.DMA(()),
+            pltpu.SemaphoreType.DMA((n,)),
+            pltpu.SemaphoreType.DMA((n,)),
+        ],
+        compiler_params=pltpu.CompilerParams(collective_id=collective, has_side_effects=True),
+    )(x)
 
 
 def local(spectra, pair_blocks, owners):
@@ -127,8 +190,8 @@
     cos_part, sin_part = table_slice(me * part, part)
     partial = pair_correlations(left_hot, right_hot, panel, cos_part, sin_part)
     partial = partial.reshape(chan_count, NB_SRC * pairs, LAGS)
-    corr = lax.psum_scatter(partial, "chan", scatter_dimension=0, tiled=True)
-    corr = corr.reshape(NB_SRC, pairs * LAGS).astype(jnp.float32)
+    gathered = exchange(partial, "chan", "grp", False, 0)
+    corr = jnp.sum(gathered, axis=0).reshape(NB_SRC, pairs * LAGS)
 
     owner_list = owners[0, 0, :, 0]
     same = owner_list[:, None] == owner_list[None, :]
@@ -140,7 +203,7 @@
     filled = jnp.any(chooser, axis=1)
     placed = jnp.where(filled[:, None], jnp.take(corr, source, axis=0), 0.0)
     placed = placed.reshape(groups_count, MOST, pairs, LAGS)
-    received = lax.all_to_all(placed, "grp", split_axis=0, concat_axis=0, tiled=True)
+    received = exchange(placed, "grp", "chan", True, 1)
     return received.reshape(1, 1, slot_count, pairs, LAGS)
 
 

time: 112 us -> 98.6 us (0.88)
  the two profiles are of different devices: /device:TPU:0 before, /device:TPU:1 now
where the time goes in v2:
time: 98.6 us; the launch traced here: 97.7 us
  Pallas kernels  56.2 us (57%)
  other arithmetic  16.1 us (16%)
  waiting for transfers between devices  9.35 us (9%)
  local copies, waits for them, and re-layouts  9.08 us (9%)
  starting transfers between devices  6.81 us (7%)
    pallas_call x2, Pallas kernels, exchange(): pl.pallas_call(functools.partial(exchange_kernel, axis, other_axis, axis_...  45 us
    pallas_call x1, Pallas kernels, pair_correlations(): pl.pallas_call(pair_kernel, out_shape=jax.ShapeDtypeStruct((rows, LAGS),...  11.2 us
    all_to_all x1, waiting for transfers between devices, local(): got = lax.all_to_all(sent, 'chan', split_axis=0, concat_axis=0, tiled=True)  9.35 us
    all_to_all x1, starting transfers between devices, local(): got = lax.all_to_all(sent, 'chan', split_axis=0, concat_axis=0, tiled=True)  6.81 us
    unnamed x8, local copies, waits for them, and re-layouts  3.38 us
    convert_element_type x1, other arithmetic, table_slice(): sin_part = (-sin_ab * weight).astype(jnp.bfloat16)  2.55 us
    cos x1, other arithmetic, table_slice(): cos_b, sin_b = (jnp.cos(fine)[None, :, :], jnp.sin(fine)[None, :, :])  2.04 us
  transfers between devices with their start and end apart: 1, of which 1 were waited for; matrix products, arithmetic and copies ran while one was open for 7% of the time, Pallas kernels for 0%

profile of v2, /device:TPU:1, one launch (start us, length us, event | category | flops | bytes accessed | tf_op | source)
XLA Modules:
  0.0 97.7 jit_solution(6440388298843632449)
XLA Ops:
  0.0 1.8 %copy_convert_fusion = f32[16,2,2,8192]{3,0,2,1:T(8,128)S(1)} fusion(bf16[16,2,2,8192]{3,2,1,0:T(2,128)(2,1)} %param.5), kind=kLoop, calls=%fused_computation.12 | loop fusion | flops 524288 | bytes 3145728 | tf_op jit(solution)/shard_map/convert_element_type | solution.py:41
  1.8 0.0 copy-start
  1.9 0.2 fusion.13
  2.1 0.3 rsqrt_bitcast_fusion
  2.4 0.7 copy-done
  3.1 0.6 multiply_convert_fusion
  3.7 0.6 copy.16
  4.3 0.0 copy-start.1
  4.3 1.1 %copy.14 = bf16[8,16,2,2,1024]{4,3,2,1,0:T(2,128)(2,1)S(1)} copy(bf16[8,16,2,2,1024]{4,0,1,3,2:T(8,128)(2,1)S(1)} %bitcast.24) | data formatting | bytes 2097152 | tf_op jit(solution)/shard_map/transpose | solution.py:171
  5.4 0.4 reshape.313
  5.9 0.0 copy-done.1
  5.9 0.0 copy-start.2
  5.9 0.1 copy.15
  6.0 0.1 convert_element_type.82
  6.1 1.2 %pad_maximum_fusion = bf16[8,65,1024]{2,1,0:T(8,128)(2,1)} fusion(bf16[8,1,1024]{2,1,0:T(2,128)(2,1)S(1)} %broadcast_in_dim.38, bf16[8,64,1024]{2,1,0:T(8,128)(2,1)S(1)} %reshape.313), kind=kLoop, calls=%fused_computation.8 | loop fusion | flops 2129920 | bytes 2129920 | tf_op jit(solution)/shard_map/concatenate | solution.py:176
  7.3 6.8 %all-to-all-start = ((bf16[8,65,1024]{2,1,0:T(8,128)(2,1)}), bf16[8,65,1024]{2,1,0:T(8,128)(2,1)S(1)}, u32[]{:S(2)}, u32[]{:S(2)}) async-start(bf16[8,65,1024]{2,1,0:T(8,128)(2,1)} %pad_maximum_fusion), calls=%async_computation | async-start | bytes 2359296 | tf_op jit(solution)/shard_map/all_to_all | solution.py:177
  14.1 0.0 copy-done.2
  14.1 0.2 convert_reduce_fusion
  14.3 0.6 iota_reduce_fusion
  14.9 0.1 fusion.21
  15.0 2.0 %fusion.12 = (f32[128,1024]{1,0:T(8,128)S(1)}, f32[128,1024]{1,0:T(8,128)S(1)}) fusion(s32[1024]{0:T(1024)S(1)} %iota_add_fusion.2), kind=kLoop, calls=%fused_computation.29 | loop fusion | flops 1835008 | bytes 1052672 | tf_op jit(solution)/shard_map/cos | solution.py:30
  17.1 0.2 fusion.20
  17.3 0.1 broadcast_in_dim.36
  17.4 0.1 broadcast_in_dim.31
  17.5 1.2 %add_negate_fusion = (f32[8,128,1024]{2,1,0:T(8,128)S(1)}, f32[8,128,1024]{2,1,0:T(8,128)S(1)}) fusion(f32[128,1024]{1,0:T(8,128)S(1)} %get-tuple-element.28, f32[8,1024]{1,0:T(8,128)S(1)} %get-tuple-element.24, f32[128,1024]{1,0:T(8,128)S(1)} %get-tuple-element.27, f32[8,1024]{1,0:T(8,128)S(1)} %get-tuple-element.23), kind=kLoop, calls=%fused_computation.5 | loop fusion | flops 7340032 | bytes 9502720 | tf_op jit(solution)/shard_map/neg | solution.py:36
  18.7 2.6 %fusion = (bf16[1024,1024]{1,0:T(8,128)(2,1)}, bf16[1024,1024]{1,0:T(8,128)(2,1)}) fusion(f32[8,128,1024]{2,1,0:T(8,128)S(1)} %get-tuple-element.21, f32[1024]{0:T(1024)S(1)} %select_multiply_fusion, f32[8,128,1024]{2,1,0:T(8,128)S(1)} %get-tuple-element.22), kind=kLoop, calls=%fused_computation.2 | loop fusion | flops 4194304 | bytes 12587008 | tf_op jit(solution)/shard_map/convert_element_type | solution.py:36
  21.3 9.3 %all-to-all-done = bf16[8,65,1024]{2,1,0:T(8,128)(2,1)S(1)} async-done(((bf16[8,65,1024]{2,1,0:T(8,128)(2,1)}), bf16[8,65,1024]{2,1,0:T(8,128)(2,1)S(1)}, u32[]{:S(2)}, u32[]{:S(2)}) %all-to-all-start) | async-done | bytes 1064992 | tf_op jit(solution)/shard_map/all_to_all | solution.py:177
  30.6 0.1 convert_element_type.85
  30.7 0.2 fusion.14
  31.0 0.1 iota_add_fusion
  31.1 0.1 add.165
  31.1 0.2 eq.82
  31.3 0.8 fusion.10.right_hot
  32.1 0.2 add.161
  32.4 0.2 eq.78
  32.6 0.8 fusion.9.left_hot
  33.4 0.1 slice.42
  33.5 1.5 %reshape.314.panel = bf16[128,4096]{1,0:T(8,128)(2,1)} reshape(bf16[8,64,1024]{2,1,0:T(8,128)(2,1)S(1)} %slice.42) | data formatting | bytes 2097152 | tf_op jit(solution)/shard_map/reshape | solution.py:180
  34.9 11.2 %shard_map.37 = f32[576,1024]{1,0:T(8,128)} custom-call(bf16[576,128]{1,0:T(8,128)(2,1)} %fusion.9.left_hot, bf16[576,128]{1,0:T(8,128)(2,1)} %fusion.10.right_hot, bf16[128,4096]{1,0:T(8,128)(2,1)} %reshape.314.panel, bf16[1024,1024]{1,0:T(8,128)(2,1)} %get-tuple-element.26.cos_ref, bf16[1024,1024]{1,0:T(8,128)(2,1)} %get-tuple-element.25.sin_ref), custom_call_target="tpu_custom_call" | custom-call | flops 3623878656 | bytes 7602176 | tf_op jit(solution)/shard_map/pallas_call | solution.py:86
  46.1 30.5 %shard_map.38 = f32[8,72,1024]{2,1,0:T(8,128)} custom-call(f32[8,72,1024]{2,1,0:T(8,128)} %bitcast.26), custom_call_target="tpu_custom_call" | custom-call | tf_op jit(solution)/shard_map/pallas_call | solution.py:147
  76.6 1.8 %reduce_sum.29 = f32[72,1024]{1,0:T(8,128)S(1)} reduce(f32[8,72,1024]{2,1,0:T(8,128)} %shard_map.38, f32[]{:T(128)} %constant.91.clone.1), dimensions={0}, to_apply=%region_4.5 | reduce | flops 516096 | bytes 2654212 | tf_op jit(solution)/shard_map/reduce_sum | solution.py:194
  78.4 0.1 reshape.316
  78.6 0.8 gather_fusion
  79.4 0.5 gather.7
  79.9 1.2 %select_select_fusion.x_ref = f32[16,3,4,1024]{3,2,1,0:T(4,128)} fusion(f32[16,3,4,1024]{3,2,1,0:T(4,128)S(1)} %gather.7, pred[16,3]{1,0:T(8,128)(4,1)S(1)} %broadcast_in_dim.36, pred[16,3]{1,0:T(8,128)(4,1)S(1)} %broadcast_in_dim.31), kind=kLoop, calls=%fused_computation.14 | loop fusion | flops 393216 | bytes 1572960 | tf_op jit(solution)/shard_map/jit(_where)/select_n | solution.py:204
  81.1 14.5 %shard_map.39 = f32[16,3,4,1024]{3,2,1,0:T(4,128)} custom-call(f32[16,3,4,1024]{3,2,1,0:T(4,128)} %select_select_fusion.x_ref), custom_call_target="tpu_custom_call" | custom-call | tf_op jit(solution)/shard_map/pallas_call | solution.py:147
  95.7 2.1 %copy.21 = f32[1,1,48,4,1024]{4,3,2,1,0:T(4,128)} copy(f32[1,1,48,4,1024]{4,3,2,1,0:T(4,128)} %bitcast.25) | data formatting | bytes 1572864
  (12 shorter events, 0.1 us)
Async XLA Ops:
  1.8 1.2 %copy-start = (bf16[16,2,2,8192]{3,2,1,0:T(2,128)(2,1)S(1)}, bf16[16,2,2,8192]{3,2,1,0:T(2,128)(2,1)}, u32[]{:S(2)}) copy-start(bf16[16,2,2,8192]{3,2,1,0:T(2,128)(2,1)} %param.5) | copy-start | bytes 3145732
  4.3 1.5 %copy-start.1 = (s32[1,1,18,2]{2,3,1,0:T(2,128)S(1)}, s32[1,1,18,2]{2,3,1,0:T(2,128)}, u32[]{:S(2)}) copy-start(s32[1,1,18,2]{2,3,1,0:T(2,128)} %param.6) | copy-start | bytes 436
  5.9 8.3 %copy-start.2 = (s32[1,1,18,1]{2,3,1,0:T(1,128)S(1)}, s32[1,1,18,1]{2,3,1,0:T(1,128)}, u32[]{:S(2)}) copy-start(s32[1,1,18,1]{2,3,1,0:T(1,128)} %param.7) | copy-start | bytes 220
  7.3 23.3 %all-to-all-start = ((bf16[8,65,1024]{2,1,0:T(8,128)(2,1)}), bf16[8,65,1024]{2,1,0:T(8,128)(2,1)S(1)}, u32[]{:S(2)}, u32[]{:S(2)}) async-start(bf16[8,65,1024]{2,1,0:T(8,128)(2,1)} %pad_maximum_fusion), calls=%async_computation | async-start | bytes 2359296 | tf_op jit(solution)/shard_map/all_to_all | solution.py:177

commit v3 on v2

--- a/solution.py
+++ b/solution.py
@@ -15,6 +15,7 @@
 WINDOWS = 2
 FINE = 128
 ROW_CHUNK = 144
+CORES = 2
 
 
 def phase_angle(bins, lag_index):
@@ -97,13 +98,16 @@
     )(left_hot, right_hot, panel, cos_part, sin_part)
 
 
-def exchange_kernel(axis, other_axis, axis_first, collective, x_ref, out_ref, local_sem, send_sem, recv_sem):
+def exchange_kernel(axis, other_axis, axis_first, stride, x_ref, out_ref, local_sem, send_sem, recv_sem):
     n = x_ref.shape[0]
-    me = lax.axis_index(axis)
+    index = lax.axis_index(axis)
+    me = lax.rem(index // stride, n)
+    base = index - me * stride
     other = lax.axis_index(other_axis)
 
     def device(j):
-        return (j, other) if axis_first else (other, j)
+        coord = base + stride * j
+        return (coord, other) if axis_first else (other, coord)
 
     barrier = pltpu.get_barrier_semaphore()
     for step in range(1, n):
@@ -141,11 +145,11 @@
         incoming.wait_recv()
 
 
-def exchange(x, axis, other_axis, axis_first, collective):
+def exchange(x, axis, other_axis, axis_first, stride, collective):
     n = x.shape[0]
     anywhere = pl.BlockSpec(memory_space=pl.ANY)
     return pl.pallas_call(
-        functools.partial(exchange_kernel, axis, other_axis, axis_first, collective),
+        functools.partial(exchange_kernel, axis, other_axis, axis_first, stride),
         out_shape=jax.ShapeDtypeStruct(x.shape, x.dtype),
         in_specs=[anywhere],
         out_specs=anywhere,
@@ -179,6 +183,7 @@
     group_channels = chan_count * channels
     panel = got[:, :rows_per].reshape(group_channels, WINDOWS * 2 * part)
     all_blocks = got[:, rows_per, : NB_SRC * 2].astype(jnp.float32).astype(jnp.int32)
+    all_blocks = all_blocks.reshape(chan_count // CORES, CORES, NB_SRC, 2).transpose(1, 0, 2, 3)
     all_blocks = all_blocks.reshape(chan_count * NB_SRC, 1, 2)
     offsets = jnp.arange(BLK, dtype=jnp.int32)
     left_ch = (all_blocks[:, :, 0] * BLK + offsets[None, :])[:, :, None] + jnp.zeros((1, 1, BLK), jnp.int32)
@@ -189,9 +194,11 @@
 
     cos_part, sin_part = table_slice(me * part, part)
     partial = pair_correlations(left_hot, right_hot, panel, cos_part, sin_part)
-    partial = partial.reshape(chan_count, NB_SRC * pairs, LAGS)
-    gathered = exchange(partial, "chan", "grp", False, 0)
-    corr = jnp.sum(gathered, axis=0).reshape(NB_SRC, pairs * LAGS)
+    partial = partial.reshape(CORES, chan_count // CORES * NB_SRC * pairs, LAGS)
+    on_chip = exchange(partial, "chan", "grp", False, 1, 0)
+    chip_sum = (on_chip[0] + on_chip[1]).reshape(chan_count // CORES, NB_SRC * pairs, LAGS)
+    across = exchange(chip_sum, "chan", "grp", False, CORES, 1)
+    corr = jnp.sum(across, axis=0).reshape(NB_SRC, pairs * LAGS)
 
     owner_list = owners[0, 0, :, 0]
     same = owner_list[:, None] == owner_list[None, :]
@@ -202,8 +209,8 @@
     source = jnp.argmax(chooser, axis=1)
     filled = jnp.any(chooser, axis=1)
     placed = jnp.where(filled[:, None], jnp.take(corr, source, axis=0), 0.0)
-    placed = placed.reshape(groups_count, MOST, pairs, LAGS)
-    received = exchange(placed, "grp", "chan", True, 1)
+    placed = placed.reshape(groups_count, MOST, pairs, LAGS).astype(jnp.bfloat16)
+    received = exchange(placed, "grp", "chan", True, 1, 2).astype(jnp.float32)
     return received.reshape(1, 1, slot_count, pairs, LAGS)
 
 

time: 98.6 us -> 120 us (1.22)
  Pallas kernels: 56.2 us -> 76.2 us
  other arithmetic: 16.1 us -> 18.4 us
  local copies, waits for them, and re-layouts: 9.08 us -> 7.45 us
    pallas_call x2 -> x3, Pallas kernels: 45 us -> 65 us  [exchange(): pl.pallas_call(functools.partial(exchange_kernel, axis, other_axis, axis_...]
    add x0 -> x2, other arithmetic: none -> 2.95 us  [the longest x1 2.86 us: local(): on_chip[0] + on_chip[1]]
    reshape x0 -> x1, other arithmetic: none -> 1.98 us  [local(): return received.reshape(1, 1, slot_count, pairs, LAGS)]
    unnamed x8 -> x7, local copies, waits for them, and re-layouts: 3.38 us -> 1.57 us
    concatenate x0 -> x1, local copies, waits for them, and re-layouts: none -> 1.61 us  [local(): sent = jnp.concatenate([chunks, extra], axis=1)]
  transfers between devices with their start and end apart: 1 -> 1, of which waited for: 1 -> 1; matrix products, arithmetic and copies ran while one was open for 7% -> 6% of each run, Pallas kernels for 0% -> 0%
where the time goes in v3:
time: 120 us; the launch traced here: 118 us
  Pallas kernels  76.2 us (64%)
  other arithmetic  18.4 us (15%)
  waiting for transfers between devices  9.35 us (8%)
  local copies, waits for them, and re-layouts  7.45 us (6%)
  starting transfers between devices  6.81 us (6%)
    pallas_call x3, Pallas kernels, exchange(): pl.pallas_call(functools.partial(exchange_kernel, axis, other_axis, axis_...  65 us
    pallas_call x1, Pallas kernels, pair_correlations(): pl.pallas_call(pair_kernel, out_shape=jax.ShapeDtypeStruct((rows, LAGS),...  11.2 us
    all_to_all x1, waiting for transfers between devices, local(): got = lax.all_to_all(sent, 'chan', split_axis=0, concat_axis=0, tiled=True)  9.35 us
    all_to_all x1, starting transfers between devices, local(): got = lax.all_to_all(sent, 'chan', split_axis=0, concat_axis=0, tiled=True)  6.81 us
    add x1, other arithmetic, local(): on_chip[0] + on_chip[1]  2.86 us
    convert_element_type x1, other arithmetic, table_slice(): sin_part = (-sin_ab * weight).astype(jnp.bfloat16)  2.55 us
  transfers between devices with their start and end apart: 1, of which 1 were waited for; matrix products, arithmetic and copies ran while one was open for 6% of the time, Pallas kernels for 0%

profile of v3, /device:TPU:1, one launch (start us, length us, event | category | flops | bytes accessed | tf_op | source)
XLA Modules:
  0.0 118.5 jit_solution(2885666158664317894)
XLA Ops:
  0.0 1.8 %copy_convert_fusion = f32[16,2,2,8192]{3,0,2,1:T(8,128)S(1)} fusion(bf16[16,2,2,8192]{3,2,1,0:T(2,128)(2,1)} %param.5), kind=kLoop, calls=%fused_computation.13 | loop fusion | flops 524288 | bytes 3145728 | tf_op jit(solution)/shard_map/convert_element_type | solution.py:42
  1.8 0.2 fusion.13
  2.1 0.3 rsqrt_bitcast_fusion
  2.4 1.0 copy-done
  3.3 0.6 multiply_convert_fusion
  3.9 0.0 copy-start.1
  4.0 0.6 copy.31
  4.6 0.1 copy.24
  4.7 0.1 copy.25
  4.8 0.1 convert_element_type.74
  4.9 0.1 pad_maximum_fusion
  5.0 0.0 copy-start.2
  5.0 1.6 %copy.26 = bf16[8,65,1024]{2,1,0:T(8,128)(2,1)} copy(bf16[8,65,1024]{2,0,1:T(8,128)(2,1)S(1)} %pad_maximum_fusion) | data formatting | bytes 2129920 | tf_op jit(solution)/shard_map/concatenate | solution.py:180
  6.6 6.8 %all-to-all-start = ((bf16[8,65,1024]{2,1,0:T(8,128)(2,1)}), bf16[8,65,1024]{2,1,0:T(8,128)(2,1)S(1)}, u32[]{:S(2)}, u32[]{:S(2)}) async-start(bf16[8,65,1024]{2,1,0:T(8,128)(2,1)} %copy.26), calls=%async_computation | async-start | bytes 2359296 | tf_op jit(solution)/shard_map/all_to_all | solution.py:181
  13.5 0.2 convert_reduce_fusion
  13.7 0.6 iota_reduce_fusion
  14.3 0.1 fusion.19
  14.4 2.0 %fusion.12 = (f32[128,1024]{1,0:T(8,128)S(1)}, f32[128,1024]{1,0:T(8,128)S(1)}) fusion(s32[1024]{0:T(1024)S(1)} %iota_add_fusion.2), kind=kLoop, calls=%fused_computation.30 | loop fusion | flops 1835008 | bytes 1052672 | tf_op jit(solution)/shard_map/cos | solution.py:31
  16.4 0.2 fusion.18
  16.7 0.1 broadcast_in_dim.36
  16.8 0.1 broadcast_in_dim.31
  16.9 1.2 %add_negate_fusion = (f32[8,128,1024]{2,1,0:T(8,128)S(1)}, f32[8,128,1024]{2,1,0:T(8,128)S(1)}) fusion(f32[128,1024]{1,0:T(8,128)S(1)} %get-tuple-element.26, f32[8,1024]{1,0:T(8,128)S(1)} %get-tuple-element.22, f32[128,1024]{1,0:T(8,128)S(1)} %get-tuple-element.25, f32[8,1024]{1,0:T(8,128)S(1)} %get-tuple-element.21), kind=kLoop, calls=%fused_computation.5 | loop fusion | flops 7340032 | bytes 9502720 | tf_op jit(solution)/shard_map/neg | solution.py:37
  18.1 2.6 %fusion = (bf16[1024,1024]{1,0:T(8,128)(2,1)}, bf16[1024,1024]{1,0:T(8,128)(2,1)}) fusion(f32[8,128,1024]{2,1,0:T(8,128)S(1)} %get-tuple-element.19, f32[1024]{0:T(1024)S(1)} %select_multiply_fusion, f32[8,128,1024]{2,1,0:T(8,128)S(1)} %get-tuple-element.20), kind=kLoop, calls=%fused_computation.2 | loop fusion | flops 4194304 | bytes 12587008 | tf_op jit(solution)/shard_map/convert_element_type | solution.py:37
  20.6 9.3 %all-to-all-done = bf16[8,65,1024]{2,1,0:T(8,128)(2,1)S(1)} async-done(((bf16[8,65,1024]{2,1,0:T(8,128)(2,1)}), bf16[8,65,1024]{2,1,0:T(8,128)(2,1)S(1)}, u32[]{:S(2)}, u32[]{:S(2)}) %all-to-all-start) | async-done | bytes 1064992 | tf_op jit(solution)/shard_map/all_to_all | solution.py:181
  30.0 0.1 copy.28
  30.1 0.1 convert_element_type.77
  30.2 0.1 copy.29
  30.3 0.1 reshape.312
  30.4 0.1 iota_add_fusion.1
  30.5 0.2 add.168
  30.7 0.2 eq.78
  30.9 0.1 iota_add_fusion
  31.0 0.1 add.172
  31.1 0.2 eq.82
  31.3 0.1 slice.50
  31.4 1.5 %reshape.313.panel = bf16[128,4096]{1,0:T(8,128)(2,1)} reshape(bf16[8,64,1024]{2,1,0:T(8,128)(2,1)S(1)} %slice.50) | data formatting | bytes 2097152 | tf_op jit(solution)/shard_map/reshape | solution.py:184
  32.8 0.9 fusion.9
  33.7 11.2 %shard_map.37 = f32[576,1024]{1,0:T(8,128)} custom-call(bf16[576,128]{1,0:T(8,128)(2,1)} %get-tuple-element.29.left_hot, bf16[576,128]{1,0:T(8,128)(2,1)} %get-tuple-element.30.right_hot, bf16[128,4096]{1,0:T(8,128)(2,1)} %reshape.313.panel, bf16[1024,1024]{1,0:T(8,128)(2,1)} %get-tuple-element.24.cos_ref, bf16[1024,1024]{1,0:T(8,128)(2,1)} %get-tuple-element.23.sin_ref), custom_call_target="tpu_custom_call" | custom-call | flops 3623878656 | bytes 7602176 | tf_op jit(solution)/shard_map/pallas_call | solution.py:87
  45.0 37.7 %shard_map.38 = f32[2,288,1024]{2,1,0:T(8,128)} custom-call(f32[2,288,1024]{2,1,0:T(8,128)} %bitcast.37), custom_call_target="tpu_custom_call" | custom-call | tf_op jit(solution)/shard_map/pallas_call | solution.py:151
  82.7 2.9 %slice_add_fusion = f32[1,288,1024]{2,1,0:T(8,128)} fusion(f32[2,288,1024]{2,1,0:T(8,128)} %shard_map.38), kind=kLoop, calls=%fused_computation.8 | loop fusion | flops 294912 | bytes 3538944 | tf_op jit(solution)/shard_map/add | solution.py:199
  85.6 16.9 %shard_map.39 = f32[4,72,1024]{2,1,0:T(8,128)} custom-call(f32[4,72,1024]{2,1,0:T(8,128)} %bitcast.33), custom_call_target="tpu_custom_call" | custom-call | tf_op jit(solution)/shard_map/pallas_call | solution.py:151
  102.4 1.4 %reduce_sum.29 = bf16[72,1024]{1,0:T(8,128)(2,1)S(1)} reduce(f32[4,72,1024]{2,1,0:T(8,128)} %shard_map.39, f32[]{:T(128)} %constant.91.clone.1), dimensions={0}, to_apply=%region_4.5 | reduce | flops 221184 | bytes 1327108 | tf_op jit(solution)/shard_map/reduce_sum | solution.py:201
  103.8 0.1 reshape.315
  103.9 0.8 gather_fusion
  104.7 0.3 gather.7
  105.0 1.1 select_convert_fusion.x_ref
  106.1 10.4 %shard_map.40 = bf16[16,3,4,1024]{3,2,1,0:T(4,128)(2,1)} custom-call(bf16[16,3,4,1024]{3,2,1,0:T(4,128)(2,1)} %select_convert_fusion.x_ref), custom_call_target="tpu_custom_call" | custom-call | tf_op jit(solution)/shard_map/pallas_call | solution.py:151
  116.5 2.0 %convert.1 = f32[1,1,48,4,1024]{4,3,2,1,0:T(4,128)} convert(bf16[1,1,48,4,1024]{4,3,2,1,0:T(4,128)(2,1)} %bitcast.38) | non-fusion elementwise | flops 196608 | bytes 1179648 | tf_op jit(solution)/shard_map/reshape | solution.py:214
  (17 shorter events, 0.1 us)
Async XLA Ops:
  2.1 1.2 %copy-start = (bf16[16,2,2,8192]{3,2,1,0:T(2,128)(2,1)S(1)}, bf16[16,2,2,8192]{3,2,1,0:T(2,128)(2,1)}, u32[]{:S(2)}) copy-start(bf16[16,2,2,8192]{3,2,1,0:T(2,128)(2,1)} %param.5) | copy-start | bytes 3145732
  3.9 0.7 copy-start.1
  5.0 8.5 %copy-start.2 = (s32[1,1,18,1]{2,3,1,0:T(1,128)S(1)}, s32[1,1,18,1]{2,3,1,0:T(1,128)}, u32[]{:S(2)}) copy-start(s32[1,1,18,1]{2,3,1,0:T(1,128)} %param.7) | copy-start | bytes 220
  6.6 23.3 %all-to-all-start = ((bf16[8,65,1024]{2,1,0:T(8,128)(2,1)}), bf16[8,65,1024]{2,1,0:T(8,128)(2,1)S(1)}, u32[]{:S(2)}, u32[]{:S(2)}) async-start(bf16[8,65,1024]{2,1,0:T(8,128)(2,1)} %copy.26), calls=%async_computation | async-start | bytes 2359296 | tf_op jit(solution)/shard_map/all_to_all | solution.py:181

commit v4 on v3

--- a/solution.py
+++ b/solution.py
@@ -16,6 +16,8 @@
 FINE = 128
 ROW_CHUNK = 144
 CORES = 2
+PARTNER_PIECES = 8
+CHIP_PIECES = 4
 
 
 def phase_angle(bins, lag_index):
@@ -115,34 +117,37 @@
                             device_id_type=pl.DeviceIdType.MESH)
     pl.semaphore_wait(barrier, n - 1)
 
+    pieces = x_ref.shape[1]
     own = pltpu.make_async_copy(x_ref.at[me], out_ref.at[me], local_sem)
     own.start()
     copies = []
     for step in range(1, n):
         target = lax.rem(me + step, n)
-        copy = pltpu.make_async_remote_copy(
-            src_ref=x_ref.at[target],
-            dst_ref=out_ref.at[me],
-            send_sem=send_sem.at[step],
-            recv_sem=recv_sem.at[step],
-            device_id=device(target),
-            device_id_type=pl.DeviceIdType.MESH,
-        )
-        copy.start()
-        copies.append(copy)
+        for piece in range(pieces):
+            copy = pltpu.make_async_remote_copy(
+                src_ref=x_ref.at[target, piece],
+                dst_ref=out_ref.at[me, piece],
+                send_sem=send_sem.at[step, piece],
+                recv_sem=recv_sem.at[step, piece],
+                device_id=device(target),
+                device_id_type=pl.DeviceIdType.MESH,
+            )
+            copy.start()
+            copies.append(copy)
     own.wait()
     for step in range(1, n):
         source = lax.rem(me + n - step, n)
-        copies[step - 1].wait_send()
-        incoming = pltpu.make_async_remote_copy(
-            src_ref=x_ref.at[source],
-            dst_ref=out_ref.at[source],
-            send_sem=send_sem.at[step],
-            recv_sem=recv_sem.at[step],
-            device_id=device(source),
-            device_id_type=pl.DeviceIdType.MESH,
-        )
-        incoming.wait_recv()
+        for piece in range(pieces):
+            copies[(step - 1) * pieces + piece].wait_send()
+            incoming = pltpu.make_async_remote_copy(
+                src_ref=x_ref.at[source, piece],
+                dst_ref=out_ref.at[source, piece],
+                send_sem=send_sem.at[step, piece],
+                recv_sem=recv_sem.at[step, piece],
+                device_id=device(source),
+                device_id_type=pl.DeviceIdType.MESH,
+            )
+            incoming.wait_recv()
 
 
 def exchange(x, axis, other_axis, axis_first, stride, collective):
@@ -155,8 +160,8 @@
         out_specs=anywhere,
         scratch_shapes=[
             pltpu.SemaphoreType.DMA(()),
-            pltpu.SemaphoreType.DMA((n,)),
-            pltpu.SemaphoreType.DMA((n,)),
+            pltpu.SemaphoreType.DMA((n, x.shape[1])),
+            pltpu.SemaphoreType.DMA((n, x.shape[1])),
         ],
         compiler_params=pltpu.CompilerParams(collective_id=collective, has_side_effects=True),
     )(x)
@@ -194,9 +199,9 @@
 
     cos_part, sin_part = table_slice(me * part, part)
     partial = pair_correlations(left_hot, right_hot, panel, cos_part, sin_part)
-    partial = partial.reshape(CORES, chan_count // CORES * NB_SRC * pairs, LAGS)
+    partial = partial.reshape(CORES, PARTNER_PIECES, -1, LAGS)
     on_chip = exchange(partial, "chan", "grp", False, 1, 0)
-    chip_sum = (on_chip[0] + on_chip[1]).reshape(chan_count // CORES, NB_SRC * pairs, LAGS)
+    chip_sum = (on_chip[0] + on_chip[1]).reshape(chan_count // CORES, CHIP_PIECES, -1, LAGS)
     across = exchange(chip_sum, "chan", "grp", False, CORES, 1)
     corr = jnp.sum(across, axis=0).reshape(NB_SRC, pairs * LAGS)
 
@@ -209,7 +214,7 @@
     source = jnp.argmax(chooser, axis=1)
     filled = jnp.any(chooser, axis=1)
     placed = jnp.where(filled[:, None], jnp.take(corr, source, axis=0), 0.0)
-    placed = placed.reshape(groups_count, MOST, pairs, LAGS).astype(jnp.bfloat16)
+    placed = placed.reshape(groups_count, 1, MOST, pairs, LAGS).astype(jnp.bfloat16)
     received = exchange(placed, "grp", "chan", True, 1, 2).astype(jnp.float32)
     return received.reshape(1, 1, slot_count, pairs, LAGS)
 

time: 120 us -> 132 us (1.10)
  Pallas kernels: 76.2 us -> 84.9 us
  local copies, waits for them, and re-layouts: 7.45 us -> 11.7 us
    pallas_call x3, Pallas kernels: 65 us -> 73.7 us  [exchange(): pl.pallas_call(functools.partial(exchange_kernel, axis, other_axis, axis_...]
    reshape x0 -> x1, local copies, waits for them, and re-layouts: none -> 2.89 us  [local(): partial = partial.reshape(CORES, PARTNER_PIECES, -1, LAGS)]
  transfers between devices with their start and end apart: 1 -> 1, of which waited for: 1 -> 1; matrix products, arithmetic and copies ran while one was open for 6% -> 5% of each run, Pallas kernels for 0% -> 0%
where the time goes in v4:
time: 132 us; the launch traced here: 131 us
  Pallas kernels  84.9 us (64%)
  other arithmetic  17.7 us (13%)
  local copies, waits for them, and re-layouts  11.7 us (9%)
  waiting for transfers between devices  9.35 us (7%)
  starting transfers between devices  6.81 us (5%)
    pallas_call x3, Pallas kernels, exchange(): pl.pallas_call(functools.partial(exchange_kernel, axis, other_axis, axis_...  73.7 us
    pallas_call x1, Pallas kernels, pair_correlations(): pl.pallas_call(pair_kernel, out_shape=jax.ShapeDtypeStruct((rows, LAGS),...  11.2 us
    all_to_all x1, waiting for transfers between devices, local(): got = lax.all_to_all(sent, 'chan', split_axis=0, concat_axis=0, tiled=True)  9.35 us
    all_to_all x1, starting transfers between devices, local(): got = lax.all_to_all(sent, 'chan', split_axis=0, concat_axis=0, tiled=True)  6.81 us
    reshape x1, local copies, waits for them, and re-layouts, local(): partial = partial.reshape(CORES, PARTNER_PIECES, -1, LAGS)  2.89 us
  transfers between devices with their start and end apart: 1, of which 1 were waited for; matrix products, arithmetic and copies ran while one was open for 5% of the time, Pallas kernels for 0%

profile of v4, /device:TPU:1, one launch (start us, length us, event | category | flops | bytes accessed | tf_op | source)
XLA Modules:
  0.0 130.6 jit_solution(15290506275514210854)
XLA Ops:
  0.0 1.8 %copy_convert_fusion = f32[16,2,2,8192]{3,0,2,1:T(8,128)S(1)} fusion(bf16[16,2,2,8192]{3,2,1,0:T(2,128)(2,1)} %param.5), kind=kLoop, calls=%fused_computation.13 | loop fusion | flops 524288 | bytes 3145728 | tf_op jit(solution)/shard_map/convert_element_type | solution.py:44
  1.8 0.2 fusion.13
  2.1 0.3 rsqrt_bitcast_fusion
  2.4 1.0 copy-done
  3.3 0.6 multiply_convert_fusion
  4.0 0.6 copy.31
  4.6 0.1 copy.24
  4.7 0.1 copy.25
  4.8 0.1 convert_element_type.74
  4.9 0.1 pad_maximum_fusion
  5.0 1.6 %copy.26 = bf16[8,65,1024]{2,1,0:T(8,128)(2,1)} copy(bf16[8,65,1024]{2,0,1:T(8,128)(2,1)S(1)} %pad_maximum_fusion) | data formatting | bytes 2129920 | tf_op jit(solution)/shard_map/concatenate | solution.py:185
  6.6 6.8 %all-to-all-start = ((bf16[8,65,1024]{2,1,0:T(8,128)(2,1)}), bf16[8,65,1024]{2,1,0:T(8,128)(2,1)S(1)}, u32[]{:S(2)}, u32[]{:S(2)}) async-start(bf16[8,65,1024]{2,1,0:T(8,128)(2,1)} %copy.26), calls=%async_computation | async-start | bytes 2359296 | tf_op jit(solution)/shard_map/all_to_all | solution.py:186
  13.5 0.2 convert_reduce_fusion
  13.7 0.6 iota_reduce_fusion
  14.3 0.1 fusion.19
  14.4 2.0 %fusion.12 = (f32[128,1024]{1,0:T(8,128)S(1)}, f32[128,1024]{1,0:T(8,128)S(1)}) fusion(s32[1024]{0:T(1024)S(1)} %iota_add_fusion.2), kind=kLoop, calls=%fused_computation.30 | loop fusion | flops 1835008 | bytes 1052672 | tf_op jit(solution)/shard_map/cos | solution.py:33
  16.4 0.2 fusion.18
  16.7 0.1 broadcast_in_dim.36
  16.8 0.1 broadcast_in_dim.31
  16.9 1.2 add_negate_fusion
  18.1 2.6 %fusion = (bf16[1024,1024]{1,0:T(8,128)(2,1)}, bf16[1024,1024]{1,0:T(8,128)(2,1)}) fusion(f32[8,128,1024]{2,1,0:T(8,128)S(1)} %get-tuple-element.19, f32[1024]{0:T(1024)S(1)} %select_multiply_fusion, f32[8,128,1024]{2,1,0:T(8,128)S(1)} %get-tuple-element.20), kind=kLoop, calls=%fused_computation.2 | loop fusion | flops 4194304 | bytes 12587008 | tf_op jit(solution)/shard_map/convert_element_type | solution.py:39
  20.6 9.3 %all-to-all-done = bf16[8,65,1024]{2,1,0:T(8,128)(2,1)S(1)} async-done(((bf16[8,65,1024]{2,1,0:T(8,128)(2,1)}), bf16[8,65,1024]{2,1,0:T(8,128)(2,1)S(1)}, u32[]{:S(2)}, u32[]{:S(2)}) %all-to-all-start) | async-done | bytes 1064992 | tf_op jit(solution)/shard_map/all_to_all | solution.py:186
  30.0 0.1 copy.28
  30.1 0.1 convert_element_type.77
  30.2 0.1 copy.29
  30.3 0.1 reshape.330
  30.4 0.1 iota_add_fusion.1
  30.5 0.2 add.168
  30.7 0.2 eq.78
  30.9 0.1 iota_add_fusion
  31.0 0.1 add.172
  31.1 0.2 eq.82
  31.3 0.1 slice.50
  31.4 1.5 %reshape.331.panel = bf16[128,4096]{1,0:T(8,128)(2,1)} reshape(bf16[8,64,1024]{2,1,0:T(8,128)(2,1)S(1)} %slice.50) | data formatting | bytes 2097152 | tf_op jit(solution)/shard_map/reshape | solution.py:189
  32.8 0.9 fusion.9
  33.7 11.2 %shard_map.37 = f32[576,1024]{1,0:T(8,128)} custom-call(bf16[576,128]{1,0:T(8,128)(2,1)} %get-tuple-element.29.left_hot, bf16[576,128]{1,0:T(8,128)(2,1)} %get-tuple-element.30.right_hot, bf16[128,4096]{1,0:T(8,128)(2,1)} %reshape.331.panel, bf16[1024,1024]{1,0:T(8,128)(2,1)} %get-tuple-element.24.cos_ref, bf16[1024,1024]{1,0:T(8,128)(2,1)} %get-tuple-element.23.sin_ref), custom_call_target="tpu_custom_call" | custom-call | flops 3623878656 | bytes 7602176 | tf_op jit(solution)/shard_map/pallas_call | solution.py:89
  45.0 2.9 %reshape.332.x_ref = f32[2,8,36,1024]{3,2,1,0:T(8,128)} reshape(f32[576,1024]{1,0:T(8,128)} %shard_map.37) | data formatting | bytes 4718592 | tf_op jit(solution)/shard_map/reshape | solution.py:202
  47.8 42.0 %shard_map.38 = f32[2,8,36,1024]{3,2,1,0:T(8,128)} custom-call(f32[2,8,36,1024]{3,2,1,0:T(8,128)} %reshape.332.x_ref), custom_call_target="tpu_custom_call" | custom-call | tf_op jit(solution)/shard_map/pallas_call | solution.py:156
  89.8 1.9 %slice_add_fusion = f32[1,8,36,1024]{3,2,1,0:T(8,128)S(1)} fusion(f32[2,8,36,1024]{3,2,1,0:T(8,128)} %shard_map.38), kind=kLoop, calls=%fused_computation.8 | loop fusion | flops 294912 | bytes 3538944 | tf_op jit(solution)/shard_map/add | solution.py:204
  91.7 1.3 add.181.x_ref
  93.0 21.3 %shard_map.39 = f32[4,4,18,1024]{3,2,1,0:T(8,128)} custom-call(f32[4,4,18,1024]{3,2,1,0:T(8,128)} %add.181.x_ref), custom_call_target="tpu_custom_call" | custom-call | tf_op jit(solution)/shard_map/pallas_call | solution.py:156
  114.3 1.6 %reduce_sum.29 = bf16[4,18,1024]{2,1,0:T(8,128)(2,1)S(1)} reduce(f32[4,4,18,1024]{3,2,1,0:T(8,128)} %shard_map.39, f32[]{:T(128)} %constant.91.clone.1), dimensions={0}, to_apply=%region_4.5 | reduce | flops 221184 | bytes 1327108 | tf_op jit(solution)/shard_map/reduce_sum | solution.py:206
  115.9 0.1 reshape.333
  116.1 0.8 gather_fusion
  116.9 0.3 gather.7
  117.1 1.1 select_convert_fusion.x_ref
  118.2 10.4 %shard_map.40 = bf16[16,1,3,4,1024]{4,3,2,1,0:T(4,128)(2,1)} custom-call(bf16[16,1,3,4,1024]{4,3,2,1,0:T(4,128)(2,1)} %select_convert_fusion.x_ref), custom_call_target="tpu_custom_call" | custom-call | tf_op jit(solution)/shard_map/pallas_call | solution.py:156
  128.6 2.0 %convert.1 = f32[1,1,48,4,1024]{4,3,2,1,0:T(4,128)} convert(bf16[1,1,48,4,1024]{4,3,2,1,0:T(4,128)(2,1)} %bitcast.34) | non-fusion elementwise | flops 196608 | bytes 1179648 | tf_op jit(solution)/shard_map/reshape | solution.py:219
  (19 shorter events, 0.1 us)
Async XLA Ops:
  2.1 1.2 copy-start
  3.9 0.7 copy-start.1
  5.0 8.5 %copy-start.2 = (s32[1,1,18,1]{2,3,1,0:T(1,128)S(1)}, s32[1,1,18,1]{2,3,1,0:T(1,128)}, u32[]{:S(2)}) copy-start(s32[1,1,18,1]{2,3,1,0:T(1,128)} %param.7) | copy-start | bytes 220
  6.6 23.3 %all-to-all-start = ((bf16[8,65,1024]{2,1,0:T(8,128)(2,1)}), bf16[8,65,1024]{2,1,0:T(8,128)(2,1)S(1)}, u32[]{:S(2)}, u32[]{:S(2)}) async-start(bf16[8,65,1024]{2,1,0:T(8,128)(2,1)} %copy.26), calls=%async_computation | async-start | bytes 2359296 | tf_op jit(solution)/shard_map/all_to_all | solution.py:186

commit v5 on v4

--- a/solution.py
+++ b/solution.py
@@ -15,9 +15,6 @@
 WINDOWS = 2
 FINE = 128
 ROW_CHUNK = 144
-CORES = 2
-PARTNER_PIECES = 8
-CHIP_PIECES = 4
 
 
 def phase_angle(bins, lag_index):
@@ -152,12 +149,12 @@
 
 def exchange(x, axis, other_axis, axis_first, stride, collective):
     n = x.shape[0]
-    anywhere = pl.BlockSpec(memory_space=pl.ANY)
+    vmem = pl.BlockSpec(memory_space=pltpu.VMEM)
     return pl.pallas_call(
         functools.partial(exchange_kernel, axis, other_axis, axis_first, stride),
         out_shape=jax.ShapeDtypeStruct(x.shape, x.dtype),
-        in_specs=[anywhere],
-        out_specs=anywhere,
+        in_specs=[vmem],
+        out_specs=vmem,
         scratch_shapes=[
             pltpu.SemaphoreType.DMA(()),
             pltpu.SemaphoreType.DMA((n, x.shape[1])),
@@ -188,7 +185,6 @@
     group_channels = chan_count * channels
     panel = got[:, :rows_per].reshape(group_channels, WINDOWS * 2 * part)
     all_blocks = got[:, rows_per, : NB_SRC * 2].astype(jnp.float32).astype(jnp.int32)
-    all_blocks = all_blocks.reshape(chan_count // CORES, CORES, NB_SRC, 2).transpose(1, 0, 2, 3)
     all_blocks = all_blocks.reshape(chan_count * NB_SRC, 1, 2)
     offsets = jnp.arange(BLK, dtype=jnp.int32)
     left_ch = (all_blocks[:, :, 0] * BLK + offsets[None, :])[:, :, None] + jnp.zeros((1, 1, BLK), jnp.int32)
@@ -199,11 +195,9 @@
 
     cos_part, sin_part = table_slice(me * part, part)
     partial = pair_correlations(left_hot, right_hot, panel, cos_part, sin_part)
-    partial = partial.reshape(CORES, PARTNER_PIECES, -1, LAGS)
-    on_chip = exchange(partial, "chan", "grp", False, 1, 0)
-    chip_sum = (on_chip[0] + on_chip[1]).reshape(chan_count // CORES, CHIP_PIECES, -1, LAGS)
-    across = exchange(chip_sum, "chan", "grp", False, CORES, 1)
-    corr = jnp.sum(across, axis=0).reshape(NB_SRC, pairs * LAGS)
+    partial = partial.reshape(chan_count, 1, NB_SRC * pairs, LAGS)
+    gathered = exchange(partial, "chan", "grp", False, 1, 0)
+    corr = jnp.sum(gathered, axis=0).reshape(NB_SRC, pairs * LAGS)
 
     owner_list = owners[0, 0, :, 0]
     same = owner_list[:, None] == owner_list[None, :]
@@ -215,7 +209,7 @@
     filled = jnp.any(chooser, axis=1)
     placed = jnp.where(filled[:, None], jnp.take(corr, source, axis=0), 0.0)
     placed = placed.reshape(groups_count, 1, MOST, pairs, LAGS).astype(jnp.bfloat16)
-    received = exchange(placed, "grp", "chan", True, 1, 2).astype(jnp.float32)
+    received = exchange(placed, "grp", "chan", True, 1, 1).astype(jnp.float32)
     return received.reshape(1, 1, slot_count, pairs, LAGS)
 
 

time: 132 us -> 97.9 us (0.74)
  Pallas kernels: 84.9 us -> 56.4 us
  local copies, waits for them, and re-layouts: 11.7 us -> 6.69 us
    pallas_call x3 -> x2, Pallas kernels: 73.7 us -> 45.2 us  [exchange(): pl.pallas_call(functools.partial(exchange_kernel, axis, other_axis, axis_...]
    reshape x3 -> x2, local copies, waits for them, and re-layouts: 3.11 us -> 0.54 us  [the longest x1 0.44 us: local(): chunks = chunks.reshape(chan_count, channels * WINDOWS * 2, part)]
    add x2 -> x0, other arithmetic: 1.99 us -> none  [the longest x1 1.9 us: local(): on_chip[0] + on_chip[1]]
    concatenate x1 -> x0, local copies, waits for them, and re-layouts: 1.61 us -> none  [local(): sent = jnp.concatenate([chunks, extra], axis=1)]
  transfers between devices with their start and end apart: 1 -> 1, of which waited for: 1 -> 1; matrix products, arithmetic and copies ran while one was open for 5% -> 7% of each run, Pallas kernels for 0% -> 0%
where the time goes in v5:
time: 97.9 us; the launch traced here: 97.5 us
  Pallas kernels  56.4 us (58%)
  other arithmetic  18 us (18%)
  waiting for transfers between devices  9.35 us (10%)
  starting transfers between devices  6.81 us (7%)
  local copies, waits for them, and re-layouts  6.69 us (7%)
    pallas_call x2, Pallas kernels, exchange(): pl.pallas_call(functools.partial(exchange_kernel, axis, other_axis, axis_...  45.2 us
    pallas_call x1, Pallas kernels, pair_correlations(): pl.pallas_call(pair_kernel, out_shape=jax.ShapeDtypeStruct((rows, LAGS),...  11.2 us
    all_to_all x1, waiting for transfers between devices, local(): got = lax.all_to_all(sent, 'chan', split_axis=0, concat_axis=0, tiled=True)  9.35 us
    all_to_all x1, starting transfers between devices, local(): got = lax.all_to_all(sent, 'chan', split_axis=0, concat_axis=0, tiled=True)  6.81 us
    convert_element_type x1, other arithmetic, table_slice(): sin_part = (-sin_ab * weight).astype(jnp.bfloat16)  2.55 us
    cos x1, other arithmetic, table_slice(): cos_b, sin_b = (jnp.cos(fine)[None, :, :], jnp.sin(fine)[None, :, :])  2.04 us
    reshape x1, other arithmetic, local(): return received.reshape(1, 1, slot_count, pairs, LAGS)  1.98 us
  transfers between devices with their start and end apart: 1, of which 1 were waited for; matrix products, arithmetic and copies ran while one was open for 7% of the time, Pallas kernels for 0%

profile of v5, /device:TPU:1, one launch (start us, length us, event | category | flops | bytes accessed | tf_op | source)
XLA Modules:
  0.0 97.5 jit_solution(15137964450051809321)
XLA Ops:
  0.0 1.8 %copy_convert_fusion = f32[16,2,2,8192]{3,0,2,1:T(8,128)S(1)} fusion(bf16[16,2,2,8192]{3,2,1,0:T(2,128)(2,1)} %param.5), kind=kLoop, calls=%fused_computation.12 | loop fusion | flops 524288 | bytes 3145728 | tf_op jit(solution)/shard_map/convert_element_type | solution.py:41
  1.8 0.0 copy-start
  1.9 0.2 fusion.13
  2.1 0.3 rsqrt_bitcast_fusion
  2.4 0.7 copy-done
  3.1 0.6 multiply_convert_fusion
  3.7 0.6 copy.16
  4.3 0.0 copy-start.1
  4.3 1.1 %copy.14 = bf16[8,16,2,2,1024]{4,3,2,1,0:T(2,128)(2,1)S(1)} copy(bf16[8,16,2,2,1024]{4,0,1,3,2:T(8,128)(2,1)S(1)} %bitcast.25) | data formatting | bytes 2097152 | tf_op jit(solution)/shard_map/transpose | solution.py:177
  5.4 0.4 reshape.336
  5.9 0.0 copy-done.1
  5.9 0.0 copy-start.2
  5.9 0.1 copy.15
  6.0 0.1 convert_element_type.86
  6.1 1.2 %pad_maximum_fusion = bf16[8,65,1024]{2,1,0:T(8,128)(2,1)} fusion(bf16[8,1,1024]{2,1,0:T(2,128)(2,1)S(1)} %broadcast_in_dim.38, bf16[8,64,1024]{2,1,0:T(8,128)(2,1)S(1)} %reshape.336), kind=kLoop, calls=%fused_computation.8 | loop fusion | flops 2129920 | bytes 2129920 | tf_op jit(solution)/shard_map/concatenate | solution.py:182
  7.3 6.8 %all-to-all-start = ((bf16[8,65,1024]{2,1,0:T(8,128)(2,1)}), bf16[8,65,1024]{2,1,0:T(8,128)(2,1)S(1)}, u32[]{:S(2)}, u32[]{:S(2)}) async-start(bf16[8,65,1024]{2,1,0:T(8,128)(2,1)} %pad_maximum_fusion), calls=%async_computation | async-start | bytes 2359296 | tf_op jit(solution)/shard_map/all_to_all | solution.py:183
  14.1 0.0 copy-done.2
  14.1 0.2 convert_reduce_fusion
  14.3 0.6 iota_reduce_fusion
  14.9 0.1 fusion.21
  15.0 2.0 %fusion.12 = (f32[128,1024]{1,0:T(8,128)S(1)}, f32[128,1024]{1,0:T(8,128)S(1)}) fusion(s32[1024]{0:T(1024)S(1)} %iota_add_fusion.2), kind=kLoop, calls=%fused_computation.29 | loop fusion | flops 1835008 | bytes 1052672 | tf_op jit(solution)/shard_map/cos | solution.py:30
  17.1 0.2 fusion.20
  17.3 0.1 broadcast_in_dim.36
  17.4 0.1 broadcast_in_dim.31
  17.5 1.2 %add_negate_fusion = (f32[8,128,1024]{2,1,0:T(8,128)S(1)}, f32[8,128,1024]{2,1,0:T(8,128)S(1)}) fusion(f32[128,1024]{1,0:T(8,128)S(1)} %get-tuple-element.28, f32[8,1024]{1,0:T(8,128)S(1)} %get-tuple-element.24, f32[128,1024]{1,0:T(8,128)S(1)} %get-tuple-element.27, f32[8,1024]{1,0:T(8,128)S(1)} %get-tuple-element.23), kind=kLoop, calls=%fused_computation.5 | loop fusion | flops 7340032 | bytes 9502720 | tf_op jit(solution)/shard_map/neg | solution.py:36
  18.7 2.6 %fusion = (bf16[1024,1024]{1,0:T(8,128)(2,1)}, bf16[1024,1024]{1,0:T(8,128)(2,1)}) fusion(f32[8,128,1024]{2,1,0:T(8,128)S(1)} %get-tuple-element.21, f32[1024]{0:T(1024)S(1)} %select_multiply_fusion, f32[8,128,1024]{2,1,0:T(8,128)S(1)} %get-tuple-element.22), kind=kLoop, calls=%fused_computation.2 | loop fusion | flops 4194304 | bytes 12587008 | tf_op jit(solution)/shard_map/convert_element_type | solution.py:36
  21.3 9.3 %all-to-all-done = bf16[8,65,1024]{2,1,0:T(8,128)(2,1)S(1)} async-done(((bf16[8,65,1024]{2,1,0:T(8,128)(2,1)}), bf16[8,65,1024]{2,1,0:T(8,128)(2,1)S(1)}, u32[]{:S(2)}, u32[]{:S(2)}) %all-to-all-start) | async-done | bytes 1064992 | tf_op jit(solution)/shard_map/all_to_all | solution.py:183
  30.6 0.1 convert_element_type.89
  30.7 0.2 fusion.14
  31.0 0.1 iota_add_fusion
  31.1 0.1 add.165
  31.1 0.2 eq.82
  31.3 0.8 fusion.10.right_hot
  32.1 0.2 add.161
  32.4 0.2 eq.78
  32.6 0.8 fusion.9.left_hot
  33.4 0.1 slice.42
  33.5 1.5 %reshape.337.panel = bf16[128,4096]{1,0:T(8,128)(2,1)} reshape(bf16[8,64,1024]{2,1,0:T(8,128)(2,1)S(1)} %slice.42) | data formatting | bytes 2097152 | tf_op jit(solution)/shard_map/reshape | solution.py:186
  34.9 11.2 %shard_map.37 = f32[576,1024]{1,0:T(8,128)} custom-call(bf16[576,128]{1,0:T(8,128)(2,1)} %fusion.9.left_hot, bf16[576,128]{1,0:T(8,128)(2,1)} %fusion.10.right_hot, bf16[128,4096]{1,0:T(8,128)(2,1)} %reshape.337.panel, bf16[1024,1024]{1,0:T(8,128)(2,1)} %get-tuple-element.26.cos_ref, bf16[1024,1024]{1,0:T(8,128)(2,1)} %get-tuple-element.25.sin_ref), custom_call_target="tpu_custom_call" | custom-call | flops 3623878656 | bytes 7602176 | tf_op jit(solution)/shard_map/pallas_call | solution.py:86
  46.1 33.3 %shard_map.38 = f32[8,1,72,1024]{3,2,1,0:T(8,128)} custom-call(f32[8,1,72,1024]{3,2,1,0:T(8,128)} %bitcast.26), custom_call_target="tpu_custom_call" | custom-call | tf_op jit(solution)/shard_map/pallas_call | solution.py:153
  79.4 1.9 %reduce_sum.29 = bf16[72,1024]{1,0:T(8,128)(2,1)S(1)} reduce(f32[8,1,72,1024]{3,2,1,0:T(8,128)} %shard_map.38, f32[]{:T(128)} %constant.91.clone.1), dimensions={0,1}, to_apply=%region_4.5 | reduce | flops 516096 | bytes 2506756 | tf_op jit(solution)/shard_map/reduce_sum | solution.py:200
  81.3 0.1 reshape.339
  81.4 0.8 gather_fusion
  82.2 0.3 gather.7
  82.5 1.1 %select_convert_fusion.x_ref = bf16[16,1,3,4,1024]{4,3,2,1,0:T(4,128)(2,1)} fusion(bf16[16,1,3,4,1024]{4,3,2,1,0:T(4,128)(2,1)S(1)} %gather.7, pred[16,3]{1,0:T(8,128)(4,1)S(1)} %broadcast_in_dim.36, pred[16,3]{1,0:T(8,128)(4,1)S(1)} %broadcast_in_dim.31), kind=kLoop, calls=%fused_computation.14 | loop fusion | flops 393216 | bytes 786528 | tf_op jit(solution)/shard_map/convert_element_type | solution.py:211
  83.5 12.0 %shard_map.39 = bf16[16,1,3,4,1024]{4,3,2,1,0:T(4,128)(2,1)} custom-call(bf16[16,1,3,4,1024]{4,3,2,1,0:T(4,128)(2,1)} %select_convert_fusion.x_ref), custom_call_target="tpu_custom_call" | custom-call | tf_op jit(solution)/shard_map/pallas_call | solution.py:153
  95.5 2.0 %convert.1 = f32[1,1,48,4,1024]{4,3,2,1,0:T(4,128)} convert(bf16[1,1,48,4,1024]{4,3,2,1,0:T(4,128)(2,1)} %bitcast.27) | non-fusion elementwise | flops 196608 | bytes 1179648 | tf_op jit(solution)/shard_map/reshape | solution.py:213
  (12 shorter events, 0.1 us)
Async XLA Ops:
  1.8 1.2 %copy-start = (bf16[16,2,2,8192]{3,2,1,0:T(2,128)(2,1)S(1)}, bf16[16,2,2,8192]{3,2,1,0:T(2,128)(2,1)}, u32[]{:S(2)}) copy-start(bf16[16,2,2,8192]{3,2,1,0:T(2,128)(2,1)} %param.5) | copy-start | bytes 3145732
  4.3 1.5 %copy-start.1 = (s32[1,1,18,2]{2,3,1,0:T(2,128)S(1)}, s32[1,1,18,2]{2,3,1,0:T(2,128)}, u32[]{:S(2)}) copy-start(s32[1,1,18,2]{2,3,1,0:T(2,128)} %param.6) | copy-start | bytes 436
  5.9 8.3 %copy-start.2 = (s32[1,1,18,1]{2,3,1,0:T(1,128)S(1)}, s32[1,1,18,1]{2,3,1,0:T(1,128)}, u32[]{:S(2)}) copy-start(s32[1,1,18,1]{2,3,1,0:T(1,128)} %param.7) | copy-start | bytes 220
  7.3 23.3 %all-to-all-start = ((bf16[8,65,1024]{2,1,0:T(8,128)(2,1)}), bf16[8,65,1024]{2,1,0:T(8,128)(2,1)S(1)}, u32[]{:S(2)}, u32[]{:S(2)}) async-start(bf16[8,65,1024]{2,1,0:T(8,128)(2,1)} %pad_maximum_fusion), calls=%async_computation | async-start | bytes 2359296 | tf_op jit(solution)/shard_map/all_to_all | solution.py:183

commit v6 on v5

--- a/solution.py
+++ b/solution.py
@@ -14,7 +14,6 @@
 MOST = 3
 WINDOWS = 2
 FINE = 128
-ROW_CHUNK = 144
 
 
 def phase_angle(bins, lag_index):
@@ -45,50 +44,111 @@
     return (values * scale[:, :, None, :]).astype(jnp.bfloat16)
 
 
-def pair_kernel(left_hot, right_hot, panel, cos_ref, sin_ref, out_ref):
+def pair_rows(left_hot, right_hot, panel, cos_ref, sin_ref, target):
     part = cos_ref.shape[0]
-    chunk = ROW_CHUNK
+    left = left_hot[target]
+    right = right_hot[target]
 
     def rows_of(hot, window, kind):
         col = (window * 2 + kind) * part
         return jnp.dot(hot, panel[:, col:col + part], preferred_element_type=jnp.float32)
 
-    def one_chunk(step, carry):
-        at = pl.multiple_of(step * chunk, chunk)
-        left = left_hot[pl.ds(at, chunk), :]
-        right = right_hot[pl.ds(at, chunk), :]
-        real_sum = None
-        imag_sum = None
-        for window in range(WINDOWS):
-            ra = rows_of(left, window, 0)
-            ia = rows_of(left, window, 1)
-            rb = rows_of(right, window, 0)
-            ib = rows_of(right, window, 1)
-            real = (ra * rb + ia * ib).astype(jnp.bfloat16).astype(jnp.float32)
-            imag = (ia * rb - ra * ib).astype(jnp.bfloat16).astype(jnp.float32)
-            real_sum = real if real_sum is None else real_sum + real
-            imag_sum = imag if imag_sum is None else imag_sum + imag
-        real_stack = (real_sum / WINDOWS).astype(jnp.bfloat16)
-        imag_stack = (imag_sum / WINDOWS).astype(jnp.bfloat16)
-        total = jnp.dot(real_stack, cos_ref[...], preferred_element_type=jnp.float32)
-        total = total + jnp.dot(imag_stack, sin_ref[...], preferred_element_type=jnp.float32)
-        out_ref[pl.ds(at, chunk), :] = total.astype(out_ref.dtype)
+    real_sum = None
+    imag_sum = None
+    for window in range(WINDOWS):
+        ra = rows_of(left, window, 0)
+        ia = rows_of(left, window, 1)
+        rb = rows_of(right, window, 0)
+        ib = rows_of(right, window, 1)
+        real = (ra * rb + ia * ib).astype(jnp.bfloat16).astype(jnp.float32)
+        imag = (ia * rb - ra * ib).astype(jnp.bfloat16).astype(jnp.float32)
+        real_sum = real if real_sum is None else real_sum + real
+        imag_sum = imag if imag_sum is None else imag_sum + imag
+    real_stack = (real_sum / WINDOWS).astype(jnp.bfloat16)
+    imag_stack = (imag_sum / WINDOWS).astype(jnp.bfloat16)
+    total = jnp.dot(real_stack, cos_ref[...], preferred_element_type=jnp.float32)
+    return total + jnp.dot(imag_stack, sin_ref[...], preferred_element_type=jnp.float32)
+
+
+def pair_exchange_kernel(left_hot, right_hot, panel, cos_ref, sin_ref, out_ref, slots, local_sem, send_sem, recv_sem):
+    n = out_ref.shape[0]
+    me = lax.axis_index("chan")
+    group = lax.axis_index("grp")
+
+    barrier = pltpu.get_barrier_semaphore()
+    for step in range(1, n):
+        pl.semaphore_signal(barrier, inc=1, device_id=(group, lax.rem(me + step, n)),
+                            device_id_type=pl.DeviceIdType.MESH)
+    pl.semaphore_wait(barrier, n - 1)
+
+    def fill(target):
+        slots[target] = pair_rows(left_hot, right_hot, panel, cos_ref, sin_ref, target)
+
+    def send(step):
+        target = lax.rem(me + step, n)
+        return pltpu.make_async_remote_copy(
+            src_ref=slots.at[target],
+            dst_ref=out_ref.at[me],
+            send_sem=send_sem.at[step],
+            recv_sem=recv_sem.at[step],
+            device_id=(group, target),
+            device_id_type=pl.DeviceIdType.MESH,
+        )
+
+    def one_step(step, carry):
+        fill(lax.rem(me + step, n))
+
+        @pl.when(step > 1)
+        def _():
+            send(step - 1).start()
+
         return carry
 
-    lax.fori_loop(0, out_ref.shape[0] // chunk, one_chunk, 0)
-
-
-def pair_correlations(left_hot, right_hot, panel, cos_part, sin_part):
+    lax.fori_loop(1, n, one_step, 0)
+    fill(me)
+    send(n - 1).start()
+    own = pltpu.make_async_copy(slots.at[me], out_ref.at[me], local_sem)
+    own.start()
+    own.wait()
+
+    def finish(step, carry):
+        send(step).wait_send()
+        source = lax.rem(me + n - step, n)
+        pltpu.make_async_remote_copy(
+            src_ref=slots.at[source],
+            dst_ref=out_ref.at[source],
+            send_sem=send_sem.at[step],
+            recv_sem=recv_sem.at[step],
+            device_id=(group, source),
+            device_id_type=pl.DeviceIdType.MESH,
+        ).wait_recv()
+        return carry
+
+    lax.fori_loop(1, n, finish, 0)
+
+
+def pair_exchange(left_hot, right_hot, panel, cos_part, sin_part, chan_count, collective):
     rows = left_hot.shape[0]
+    count = rows // chan_count
+    left_hot = left_hot.reshape(chan_count, count, -1)
+    right_hot = right_hot.reshape(chan_count, count, -1)
     part = cos_part.shape[0]
     vmem = pl.BlockSpec(memory_space=pltpu.VMEM)
     flops = 2 * 2 * rows * panel.shape[0] * panel.shape[1] + 2 * 2 * rows * part * LAGS
     return pl.pallas_call(
-        pair_kernel,
-        out_shape=jax.ShapeDtypeStruct((rows, LAGS), jnp.float32),
+        pair_exchange_kernel,
+        out_shape=jax.ShapeDtypeStruct((chan_count, count, LAGS), jnp.float32),
         in_specs=[vmem] * 5,
-        out_specs=vmem,
-        compiler_params=pltpu.CompilerParams(vmem_limit_bytes=56 * 1024 * 1024),
+        out_specs=pl.BlockSpec(memory_space=pl.ANY),
+        scratch_shapes=[
+            pltpu.VMEM((chan_count, count, LAGS), jnp.float32),
+            pltpu.SemaphoreType.DMA(()),
+            pltpu.SemaphoreType.DMA((chan_count,)),
+            pltpu.SemaphoreType.DMA((chan_count,)),
+        ],
+        compiler_params=pltpu.CompilerParams(
+            collective_id=collective, has_side_effects=True, vmem_limit_bytes=56 * 1024 * 1024
+        ),
         cost_estimate=pl.CostEstimate(
             flops=flops,
             transcendentals=0,
@@ -194,9 +254,7 @@
     right_hot = (right_ch.reshape(-1, 1) == channel_ids).astype(jnp.bfloat16)
 
     cos_part, sin_part = table_slice(me * part, part)
-    partial = pair_correlations(left_hot, right_hot, panel, cos_part, sin_part)
-    partial = partial.reshape(chan_count, 1, NB_SRC * pairs, LAGS)
-    gathered = exchange(partial, "chan", "grp", False, 1, 0)
+    gathered = pair_exchange(left_hot, right_hot, panel, cos_part, sin_part, chan_count, 0)
     corr = jnp.sum(gathered, axis=0).reshape(NB_SRC, pairs * LAGS)
 
     owner_list = owners[0, 0, :, 0]

time: 97.9 us -> 91.8 us (0.938)
  Pallas kernels: 56.4 us -> 50.5 us
    pallas_call x2 -> x1, Pallas kernels: 45.2 us -> 13.4 us  [exchange(): pl.pallas_call(functools.partial(exchange_kernel, axis, other_axis, axis_...]
    pallas_call x1, Pallas kernels: 11.2 us -> 37 us  [pair_exchange(): pl.pallas_call(pair_exchange_kernel, out_shape=jax.ShapeDtypeStruct((chan...]
  transfers between devices with their start and end apart: 1 -> 1, of which waited for: 1 -> 1; matrix products, arithmetic and copies ran while one was open for 7% -> 8% of each run, Pallas kernels for 0% -> 0%
where the time goes in v6:
time: 91.8 us; the launch traced here: 91.5 us
  Pallas kernels  50.5 us (55%)
  other arithmetic  18 us (20%)
  waiting for transfers between devices  9.35 us (10%)
  starting transfers between devices  6.81 us (7%)
  local copies, waits for them, and re-layouts  6.65 us (7%)
    pallas_call x1, Pallas kernels, pair_exchange(): pl.pallas_call(pair_exchange_kernel, out_shape=jax.ShapeDtypeStruct((chan...  37 us
    pallas_call x1, Pallas kernels, exchange(): pl.pallas_call(functools.partial(exchange_kernel, axis, other_axis, axis_...  13.4 us
    all_to_all x1, waiting for transfers between devices, local(): got = lax.all_to_all(sent, 'chan', split_axis=0, concat_axis=0, tiled=True)  9.35 us
    all_to_all x1, starting transfers between devices, local(): got = lax.all_to_all(sent, 'chan', split_axis=0, concat_axis=0, tiled=True)  6.81 us
    convert_element_type x1, other arithmetic, table_slice(): sin_part = (-sin_ab * weight).astype(jnp.bfloat16)  2.55 us
    cos x1, other arithmetic, table_slice(): cos_b, sin_b = (jnp.cos(fine)[None, :, :], jnp.sin(fine)[None, :, :])  2.04 us
    reshape x1, other arithmetic, local(): return received.reshape(1, 1, slot_count, pairs, LAGS)  1.98 us
    reduce_sum x1, other arithmetic, local(): corr = jnp.sum(gathered, axis=0).reshape(NB_SRC, pairs * LAGS)  1.89 us
  transfers between devices with their start and end apart: 1, of which 1 were waited for; matrix products, arithmetic and copies ran while one was open for 8% of the time, Pallas kernels for 0%

profile of v6, /device:TPU:1, one launch (start us, length us, event | category | flops | bytes accessed | tf_op | source)
XLA Modules:
  0.0 91.5 jit_solution(12586660827245242223)
XLA Ops:
  0.0 1.8 %copy_convert_fusion = f32[16,2,2,8192]{3,0,2,1:T(8,128)S(1)} fusion(bf16[16,2,2,8192]{3,2,1,0:T(2,128)(2,1)} %param.5), kind=kLoop, calls=%fused_computation.12 | loop fusion | flops 524288 | bytes 3145728 | tf_op jit(solution)/shard_map/convert_element_type | solution.py:40
  1.8 0.0 copy-start
  1.9 0.2 fusion.13
  2.1 0.3 rsqrt_bitcast_fusion
  2.4 0.7 copy-done
  3.1 0.7 multiply_convert_fusion
  3.7 0.6 copy.16
  4.3 0.0 copy-start.1
  4.3 1.1 %copy.14 = bf16[8,16,2,2,1024]{4,3,2,1,0:T(2,128)(2,1)S(1)} copy(bf16[8,16,2,2,1024]{4,0,1,3,2:T(8,128)(2,1)S(1)} %bitcast.24) | data formatting | bytes 2097152 | tf_op jit(solution)/shard_map/transpose | solution.py:237
  5.4 0.4 reshape.349
  5.9 0.0 copy-done.1
  5.9 0.0 copy-start.2
  5.9 0.1 copy.15
  6.0 0.1 convert_element_type.88
  6.2 1.1 %pad_maximum_fusion = bf16[8,65,1024]{2,1,0:T(8,128)(2,1)} fusion(bf16[8,1,1024]{2,1,0:T(2,128)(2,1)S(1)} %broadcast_in_dim.38, bf16[8,64,1024]{2,1,0:T(8,128)(2,1)S(1)} %reshape.349), kind=kLoop, calls=%fused_computation.8 | loop fusion | flops 2129920 | bytes 2129920 | tf_op jit(solution)/shard_map/concatenate | solution.py:242
  7.3 6.8 %all-to-all-start = ((bf16[8,65,1024]{2,1,0:T(8,128)(2,1)}), bf16[8,65,1024]{2,1,0:T(8,128)(2,1)S(1)}, u32[]{:S(2)}, u32[]{:S(2)}) async-start(bf16[8,65,1024]{2,1,0:T(8,128)(2,1)} %pad_maximum_fusion), calls=%async_computation | async-start | bytes 2359296 | tf_op jit(solution)/shard_map/all_to_all | solution.py:243
  14.1 0.0 copy-done.2
  14.2 0.2 convert_reduce_fusion
  14.3 0.6 iota_reduce_fusion
  15.0 0.1 fusion.21
  15.1 2.0 %fusion.12 = (f32[128,1024]{1,0:T(8,128)S(1)}, f32[128,1024]{1,0:T(8,128)S(1)}) fusion(s32[1024]{0:T(1024)S(1)} %iota_add_fusion.2), kind=kLoop, calls=%fused_computation.29 | loop fusion | flops 1835008 | bytes 1052672 | tf_op jit(solution)/shard_map/cos | solution.py:29
  17.1 0.2 fusion.20
  17.3 0.1 broadcast_in_dim.36
  17.4 0.1 broadcast_in_dim.31
  17.5 1.2 %add_negate_fusion = (f32[8,128,1024]{2,1,0:T(8,128)S(1)}, f32[8,128,1024]{2,1,0:T(8,128)S(1)}) fusion(f32[128,1024]{1,0:T(8,128)S(1)} %get-tuple-element.28, f32[8,1024]{1,0:T(8,128)S(1)} %get-tuple-element.24, f32[128,1024]{1,0:T(8,128)S(1)} %get-tuple-element.27, f32[8,1024]{1,0:T(8,128)S(1)} %get-tuple-element.23), kind=kLoop, calls=%fused_computation.5 | loop fusion | flops 7340032 | bytes 9502720 | tf_op jit(solution)/shard_map/neg | solution.py:35
  18.7 2.6 %fusion = (bf16[1024,1024]{1,0:T(8,128)(2,1)}, bf16[1024,1024]{1,0:T(8,128)(2,1)}) fusion(f32[8,128,1024]{2,1,0:T(8,128)S(1)} %get-tuple-element.21, f32[1024]{0:T(1024)S(1)} %select_multiply_fusion, f32[8,128,1024]{2,1,0:T(8,128)S(1)} %get-tuple-element.22), kind=kLoop, calls=%fused_computation.2 | loop fusion | flops 4194304 | bytes 12587008 | tf_op jit(solution)/shard_map/convert_element_type | solution.py:35
  21.3 9.3 %all-to-all-done = bf16[8,65,1024]{2,1,0:T(8,128)(2,1)S(1)} async-done(((bf16[8,65,1024]{2,1,0:T(8,128)(2,1)}), bf16[8,65,1024]{2,1,0:T(8,128)(2,1)S(1)}, u32[]{:S(2)}, u32[]{:S(2)}) %all-to-all-start) | async-done | bytes 1064992 | tf_op jit(solution)/shard_map/all_to_all | solution.py:243
  30.6 0.1 convert_element_type.91
  30.7 0.2 fusion.14
  31.0 0.1 iota_add_fusion
  31.1 0.1 add.165
  31.1 0.2 eq.84
  31.3 0.8 fusion.10.right_hot
  32.1 0.2 add.161
  32.3 0.2 eq.80
  32.5 0.8 fusion.9.left_hot
  33.3 0.1 slice.42
  33.4 1.5 %reshape.350.panel = bf16[128,4096]{1,0:T(8,128)(2,1)} reshape(bf16[8,64,1024]{2,1,0:T(8,128)(2,1)S(1)} %slice.42) | data formatting | bytes 2097152 | tf_op jit(solution)/shard_map/reshape | solution.py:246
  34.9 37.0 %shard_map.37 = f32[8,72,1024]{2,1,0:T(8,128)} custom-call(bf16[8,72,128]{2,1,0:T(8,128)(2,1)} %fusion.9.left_hot, bf16[8,72,128]{2,1,0:T(8,128)(2,1)} %fusion.10.right_hot, bf16[128,4096]{1,0:T(8,128)(2,1)} %reshape.350.panel, bf16[1024,1024]{1,0:T(8,128)(2,1)} %get-tuple-element.26.cos_ref, bf16[1024,1024]{1,0:T(8,128)(2,1)} %get-tuple-element.25.sin_ref), custom_call_target="tpu_custom_call" | custom-call | flops 3623878656 | bytes 7602176 | tf_op jit(solution)/shard_map/pallas_call | solution.py:138
  71.9 1.9 %reduce_sum.29 = bf16[72,1024]{1,0:T(8,128)(2,1)S(1)} reduce(f32[8,72,1024]{2,1,0:T(8,128)} %shard_map.37, f32[]{:T(128)} %constant.91.clone.1), dimensions={0}, to_apply=%region_4.5 | reduce | flops 516096 | bytes 2506756 | tf_op jit(solution)/shard_map/reduce_sum | solution.py:258
  73.8 0.1 reshape.351
  73.9 0.8 gather_fusion
  74.7 0.3 gather.7
  75.0 1.1 %select_convert_fusion.x_ref = bf16[16,1,3,4,1024]{4,3,2,1,0:T(4,128)(2,1)} fusion(bf16[16,1,3,4,1024]{4,3,2,1,0:T(4,128)(2,1)S(1)} %gather.7, pred[16,3]{1,0:T(8,128)(4,1)S(1)} %broadcast_in_dim.36, pred[16,3]{1,0:T(8,128)(4,1)S(1)} %broadcast_in_dim.31), kind=kLoop, calls=%fused_computation.14 | loop fusion | flops 393216 | bytes 786528 | tf_op jit(solution)/shard_map/convert_element_type | solution.py:269
  76.1 13.4 %shard_map.38 = bf16[16,1,3,4,1024]{4,3,2,1,0:T(4,128)(2,1)} custom-call(bf16[16,1,3,4,1024]{4,3,2,1,0:T(4,128)(2,1)} %select_convert_fusion.x_ref), custom_call_target="tpu_custom_call" | custom-call | tf_op jit(solution)/shard_map/pallas_call | solution.py:213
  89.5 2.0 %convert.1 = f32[1,1,48,4,1024]{4,3,2,1,0:T(4,128)} convert(bf16[1,1,48,4,1024]{4,3,2,1,0:T(4,128)(2,1)} %bitcast.25) | non-fusion elementwise | flops 196608 | bytes 1179648 | tf_op jit(solution)/shard_map/reshape | solution.py:271
  (12 shorter events, 0.1 us)
Async XLA Ops:
  1.8 1.2 %copy-start = (bf16[16,2,2,8192]{3,2,1,0:T(2,128)(2,1)S(1)}, bf16[16,2,2,8192]{3,2,1,0:T(2,128)(2,1)}, u32[]{:S(2)}) copy-start(bf16[16,2,2,8192]{3,2,1,0:T(2,128)(2,1)} %param.5) | copy-start | bytes 3145732
  4.3 1.5 %copy-start.1 = (s32[1,1,18,2]{2,3,1,0:T(2,128)S(1)}, s32[1,1,18,2]{2,3,1,0:T(2,128)}, u32[]{:S(2)}) copy-start(s32[1,1,18,2]{2,3,1,0:T(2,128)} %param.6) | copy-start | bytes 436
  5.9 8.3 %copy-start.2 = (s32[1,1,18,1]{2,3,1,0:T(1,128)S(1)}, s32[1,1,18,1]{2,3,1,0:T(1,128)}, u32[]{:S(2)}) copy-start(s32[1,1,18,1]{2,3,1,0:T(1,128)} %param.7) | copy-start | bytes 220
  7.3 23.3 %all-to-all-start = ((bf16[8,65,1024]{2,1,0:T(8,128)(2,1)}), bf16[8,65,1024]{2,1,0:T(8,128)(2,1)S(1)}, u32[]{:S(2)}, u32[]{:S(2)}) async-start(bf16[8,65,1024]{2,1,0:T(8,128)(2,1)} %pad_maximum_fusion), calls=%async_computation | async-start | bytes 2359296 | tf_op jit(solution)/shard_map/all_to_all | solution.py:243

commit v7 on v6

--- a/solution.py
+++ b/solution.py
@@ -82,7 +82,7 @@
     pl.semaphore_wait(barrier, n - 1)
 
     def fill(target):
-        slots[target] = pair_rows(left_hot, right_hot, panel, cos_ref, sin_ref, target)
+        slots[target] = pair_rows(left_hot, right_hot, panel, cos_ref, sin_ref, target).astype(slots.dtype)
 
     def send(step):
         target = lax.rem(me + step, n)
@@ -137,11 +137,11 @@
     flops = 2 * 2 * rows * panel.shape[0] * panel.shape[1] + 2 * 2 * rows * part * LAGS
     return pl.pallas_call(
         pair_exchange_kernel,
-        out_shape=jax.ShapeDtypeStruct((chan_count, count, LAGS), jnp.float32),
+        out_shape=jax.ShapeDtypeStruct((chan_count, count, LAGS), jnp.bfloat16),
         in_specs=[vmem] * 5,
         out_specs=pl.BlockSpec(memory_space=pl.ANY),
         scratch_shapes=[
-            pltpu.VMEM((chan_count, count, LAGS), jnp.float32),
+            pltpu.VMEM((chan_count, count, LAGS), jnp.bfloat16),
             pltpu.SemaphoreType.DMA(()),
             pltpu.SemaphoreType.DMA((chan_count,)),
             pltpu.SemaphoreType.DMA((chan_count,)),
@@ -152,7 +152,7 @@
         cost_estimate=pl.CostEstimate(
             flops=flops,
             transcendentals=0,
-            bytes_accessed=panel.size * 2 + 4 * part * LAGS + rows * LAGS * 4,
+            bytes_accessed=panel.size * 2 + 4 * part * LAGS + rows * LAGS * 2,
         ),
     )(left_hot, right_hot, panel, cos_part, sin_part)
 
@@ -255,7 +255,7 @@
 
     cos_part, sin_part = table_slice(me * part, part)
     gathered = pair_exchange(left_hot, right_hot, panel, cos_part, sin_part, chan_count, 0)
-    corr = jnp.sum(gathered, axis=0).reshape(NB_SRC, pairs * LAGS)
+    corr = jnp.sum(gathered.astype(jnp.float32), axis=0).reshape(NB_SRC, pairs * LAGS)
 
     owner_list = owners[0, 0, :, 0]
     same = owner_list[:, None] == owner_list[None, :]

time: 91.8 us -> 78.8 us (0.86)
  Pallas kernels: 50.5 us -> 37.8 us
    pallas_call x1, Pallas kernels: 37 us -> 24.4 us  [pair_exchange(): pl.pallas_call(pair_exchange_kernel, out_shape=jax.ShapeDtypeStruct((chan...]
  transfers between devices with their start and end apart: 1 -> 1, of which waited for: 1 -> 1; matrix products, arithmetic and copies ran while one was open for 8% -> 9% of each run, Pallas kernels for 0% -> 0%
where the time goes in v7:
time: 78.8 us; the launch traced here: 78.4 us
  Pallas kernels  37.8 us (48%)
  other arithmetic  17.5 us (22%)
  waiting for transfers between devices  9.45 us (12%)
  starting transfers between devices  6.81 us (9%)
  local copies, waits for them, and re-layouts  6.64 us (8%)
    pallas_call x1, Pallas kernels, pair_exchange(): pl.pallas_call(pair_exchange_kernel, out_shape=jax.ShapeDtypeStruct((chan...  24.4 us
    pallas_call x1, Pallas kernels, exchange(): pl.pallas_call(functools.partial(exchange_kernel, axis, other_axis, axis_...  13.4 us
    all_to_all x1, waiting for transfers between devices, local(): got = lax.all_to_all(sent, 'chan', split_axis=0, concat_axis=0, tiled=True)  9.45 us
    all_to_all x1, starting transfers between devices, local(): got = lax.all_to_all(sent, 'chan', split_axis=0, concat_axis=0, tiled=True)  6.81 us
    convert_element_type x1, other arithmetic, table_slice(): sin_part = (-sin_ab * weight).astype(jnp.bfloat16)  2.45 us
    cos x1, other arithmetic, table_slice(): cos_b, sin_b = (jnp.cos(fine)[None, :, :], jnp.sin(fine)[None, :, :])  2.04 us
    reshape x1, other arithmetic, local(): return received.reshape(1, 1, slot_count, pairs, LAGS)  1.98 us
    convert_element_type x1, other arithmetic, whiten(): values = spectra.astype(jnp.float32)  1.84 us
  transfers between devices with their start and end apart: 1, of which 1 were waited for; matrix products, arithmetic and copies ran while one was open for 9% of the time, Pallas kernels for 0%

profile of v7, /device:TPU:1, one launch (start us, length us, event | category | flops | bytes accessed | tf_op | source)
XLA Modules:
  0.0 78.4 jit_solution(7755997029487199858)
XLA Ops:
  0.0 1.8 %copy_convert_fusion = f32[16,2,2,8192]{3,0,2,1:T(8,128)S(1)} fusion(bf16[16,2,2,8192]{3,2,1,0:T(2,128)(2,1)} %param.5), kind=kLoop, calls=%fused_computation.13 | loop fusion | flops 524288 | bytes 3145728 | tf_op jit(solution)/shard_map/convert_element_type | solution.py:40
  1.8 0.0 copy-start
  1.9 0.2 fusion.13
  2.1 0.3 rsqrt_bitcast_fusion
  2.4 0.7 copy-done
  3.1 0.7 multiply_convert_fusion
  3.7 0.6 copy.16
  4.3 0.0 copy-start.1
  4.3 1.1 %copy.14 = bf16[8,16,2,2,1024]{4,3,2,1,0:T(2,128)(2,1)S(1)} copy(bf16[8,16,2,2,1024]{4,0,1,3,2:T(8,128)(2,1)S(1)} %bitcast.24) | data formatting | bytes 2097152 | tf_op jit(solution)/shard_map/transpose | solution.py:237
  5.4 0.4 reshape.349
  5.9 0.0 copy-done.1
  5.9 0.0 copy-start.2
  5.9 0.1 copy.15
  6.0 0.1 convert_element_type.91
  6.2 1.1 %pad_maximum_fusion = bf16[8,65,1024]{2,1,0:T(8,128)(2,1)} fusion(bf16[8,1,1024]{2,1,0:T(2,128)(2,1)S(1)} %broadcast_in_dim.38, bf16[8,64,1024]{2,1,0:T(8,128)(2,1)S(1)} %reshape.349), kind=kLoop, calls=%fused_computation.9 | loop fusion | flops 2129920 | bytes 2129920 | tf_op jit(solution)/shard_map/concatenate | solution.py:242
  7.3 6.8 %all-to-all-start = ((bf16[8,65,1024]{2,1,0:T(8,128)(2,1)}), bf16[8,65,1024]{2,1,0:T(8,128)(2,1)S(1)}, u32[]{:S(2)}, u32[]{:S(2)}) async-start(bf16[8,65,1024]{2,1,0:T(8,128)(2,1)} %pad_maximum_fusion), calls=%async_computation | async-start | bytes 2359296 | tf_op jit(solution)/shard_map/all_to_all | solution.py:243
  14.1 0.0 copy-done.2
  14.2 0.2 convert_reduce_fusion.1
  14.3 0.6 iota_reduce_fusion
  15.0 0.1 fusion.21
  15.1 2.0 %fusion.12 = (f32[128,1024]{1,0:T(8,128)S(1)}, f32[128,1024]{1,0:T(8,128)S(1)}) fusion(s32[1024]{0:T(1024)S(1)} %iota_add_fusion.2), kind=kLoop, calls=%fused_computation.30 | loop fusion | flops 1835008 | bytes 1052672 | tf_op jit(solution)/shard_map/cos | solution.py:29
  17.1 0.2 fusion.20
  17.3 0.1 broadcast_in_dim.36
  17.4 0.1 broadcast_in_dim.31
  17.5 1.2 %add_negate_fusion = (f32[8,128,1024]{2,1,0:T(8,128)S(1)}, f32[8,128,1024]{2,1,0:T(8,128)S(1)}) fusion(f32[128,1024]{1,0:T(8,128)S(1)} %get-tuple-element.28, f32[8,1024]{1,0:T(8,128)S(1)} %get-tuple-element.24, f32[128,1024]{1,0:T(8,128)S(1)} %get-tuple-element.27, f32[8,1024]{1,0:T(8,128)S(1)} %get-tuple-element.23), kind=kLoop, calls=%fused_computation.5 | loop fusion | flops 7340032 | bytes 9502720 | tf_op jit(solution)/shard_map/neg | solution.py:35
  18.7 2.4 %fusion = (bf16[1024,1024]{1,0:T(8,128)(2,1)}, bf16[1024,1024]{1,0:T(8,128)(2,1)}) fusion(f32[8,128,1024]{2,1,0:T(8,128)S(1)} %get-tuple-element.21, f32[1024]{0:T(1024)S(1)} %select_multiply_fusion, f32[8,128,1024]{2,1,0:T(8,128)S(1)} %get-tuple-element.22), kind=kLoop, calls=%fused_computation.2 | loop fusion | flops 4194304 | bytes 12587008 | tf_op jit(solution)/shard_map/convert_element_type | solution.py:35
  21.2 9.5 %all-to-all-done = bf16[8,65,1024]{2,1,0:T(8,128)(2,1)S(1)} async-done(((bf16[8,65,1024]{2,1,0:T(8,128)(2,1)}), bf16[8,65,1024]{2,1,0:T(8,128)(2,1)S(1)}, u32[]{:S(2)}, u32[]{:S(2)}) %all-to-all-start) | async-done | bytes 1064992 | tf_op jit(solution)/shard_map/all_to_all | solution.py:243
  30.6 0.1 convert_element_type.94
  30.7 0.2 fusion.14
  31.0 0.1 iota_add_fusion
  31.1 0.1 add.165
  31.1 0.2 eq.84
  31.3 0.8 %fusion.10.right_hot = bf16[8,72,128]{2,1,0:T(8,128)(2,1)} fusion(s32[8,72]{1,0:T(8,128)S(1)} %eq.84), kind=kLoop, calls=%fused_computation.28 | loop fusion | flops 147456 | bytes 149760 | tf_op jit(solution)/shard_map/convert_element_type | solution.py:254
  32.1 0.2 add.161
  32.3 0.2 eq.80
  32.5 0.8 %fusion.9.left_hot = bf16[8,72,128]{2,1,0:T(8,128)(2,1)} fusion(s32[8,72]{1,0:T(8,128)S(1)} %eq.80), kind=kLoop, calls=%fused_computation.27 | loop fusion | flops 147456 | bytes 149760 | tf_op jit(solution)/shard_map/convert_element_type | solution.py:253
  33.3 0.1 slice.42
  33.4 1.4 %reshape.350.panel = bf16[128,4096]{1,0:T(8,128)(2,1)} reshape(bf16[8,64,1024]{2,1,0:T(8,128)(2,1)S(1)} %slice.42) | data formatting | bytes 2097152 | tf_op jit(solution)/shard_map/reshape | solution.py:246
  34.9 24.4 %shard_map.37 = bf16[8,72,1024]{2,1,0:T(8,128)(2,1)} custom-call(bf16[8,72,128]{2,1,0:T(8,128)(2,1)} %fusion.9.left_hot, bf16[8,72,128]{2,1,0:T(8,128)(2,1)} %fusion.10.right_hot, bf16[128,4096]{1,0:T(8,128)(2,1)} %reshape.350.panel, bf16[1024,1024]{1,0:T(8,128)(2,1)} %get-tuple-element.26.cos_ref, bf16[1024,1024]{1,0:T(8,128)(2,1)} %get-tuple-element.25.sin_ref), custom_call_target="tpu_custom_call" | custom-call | flops 3623878656 | bytes 6422528 | tf_op jit(solution)/shard_map/pallas_call | solution.py:138
  59.3 1.5 %convert_reduce_fusion = bf16[72,1024]{1,0:T(8,128)(2,1)S(1)} fusion(bf16[8,72,1024]{2,1,0:T(8,128)(2,1)} %shard_map.37), kind=kLoop, calls=%fused_computation.7 | loop fusion | flops 1105920 | bytes 1327104 | tf_op jit(solution)/shard_map/reduce_sum | solution.py:258
  60.7 0.1 reshape.351
  60.8 0.8 %gather_fusion = bf16[48,4096]{1,0:T(8,128)(2,1)S(1)} fusion(bf16[18,4096]{1,0:T(8,128)(2,1)S(1)} %reshape.351, s32[1024]{0:T(1024)S(1)} %pad_clamp_fusion), kind=kCustom, calls=%fused_computation | custom fusion | bytes 786624 | tf_op jit(solution)/shard_map/jit(_take)/gather | solution.py:268
  61.6 0.3 gather.7
  61.9 1.1 %select_convert_fusion.x_ref = bf16[16,1,3,4,1024]{4,3,2,1,0:T(4,128)(2,1)} fusion(bf16[16,1,3,4,1024]{4,3,2,1,0:T(4,128)(2,1)S(1)} %gather.7, pred[16,3]{1,0:T(8,128)(4,1)S(1)} %broadcast_in_dim.36, pred[16,3]{1,0:T(8,128)(4,1)S(1)} %broadcast_in_dim.31), kind=kLoop, calls=%fused_computation.15 | loop fusion | flops 393216 | bytes 786528 | tf_op jit(solution)/shard_map/convert_element_type | solution.py:269
  63.0 13.4 %shard_map.38 = bf16[16,1,3,4,1024]{4,3,2,1,0:T(4,128)(2,1)} custom-call(bf16[16,1,3,4,1024]{4,3,2,1,0:T(4,128)(2,1)} %select_convert_fusion.x_ref), custom_call_target="tpu_custom_call" | custom-call | tf_op jit(solution)/shard_map/pallas_call | solution.py:213
  76.5 2.0 %convert.1 = f32[1,1,48,4,1024]{4,3,2,1,0:T(4,128)} convert(bf16[1,1,48,4,1024]{4,3,2,1,0:T(4,128)(2,1)} %bitcast.25) | non-fusion elementwise | flops 196608 | bytes 1179648 | tf_op jit(solution)/shard_map/reshape | solution.py:271
  (12 shorter events, 0.1 us)
Async XLA Ops:
  1.8 1.2 %copy-start = (bf16[16,2,2,8192]{3,2,1,0:T(2,128)(2,1)S(1)}, bf16[16,2,2,8192]{3,2,1,0:T(2,128)(2,1)}, u32[]{:S(2)}) copy-start(bf16[16,2,2,8192]{3,2,1,0:T(2,128)(2,1)} %param.5) | copy-start | bytes 3145732
  4.3 1.5 %copy-start.1 = (s32[1,1,18,2]{2,3,1,0:T(2,128)S(1)}, s32[1,1,18,2]{2,3,1,0:T(2,128)}, u32[]{:S(2)}) copy-start(s32[1,1,18,2]{2,3,1,0:T(2,128)} %param.6) | copy-start | bytes 436
  5.9 8.3 %copy-start.2 = (s32[1,1,18,1]{2,3,1,0:T(1,128)S(1)}, s32[1,1,18,1]{2,3,1,0:T(1,128)}, u32[]{:S(2)}) copy-start(s32[1,1,18,1]{2,3,1,0:T(1,128)} %param.7) | copy-start | bytes 220
  7.3 23.3 %all-to-all-start = ((bf16[8,65,1024]{2,1,0:T(8,128)(2,1)}), bf16[8,65,1024]{2,1,0:T(8,128)(2,1)S(1)}, u32[]{:S(2)}, u32[]{:S(2)}) async-start(bf16[8,65,1024]{2,1,0:T(8,128)(2,1)} %pad_maximum_fusion), calls=%async_computation | async-start | bytes 2359296 | tf_op jit(solution)/shard_map/all_to_all | solution.py:243

commit v8 on v7

--- a/solution.py
+++ b/solution.py
@@ -21,19 +21,25 @@
     return phase.astype(jnp.float32) * (jnp.pi / F)
 
 
-def table_slice(start, count):
+def table_factors(start, count):
     lag_index = jnp.arange(LAGS, dtype=jnp.int32) - LAGS // 2
     coarse = phase_angle(start + FINE * jnp.arange(count // FINE, dtype=jnp.int32), lag_index)
     fine = phase_angle(jnp.arange(FINE, dtype=jnp.int32), lag_index)
-    cos_a, sin_a = jnp.cos(coarse)[:, None, :], jnp.sin(coarse)[:, None, :]
-    cos_b, sin_b = jnp.cos(fine)[None, :, :], jnp.sin(fine)[None, :, :]
-    cos_ab = (cos_a * cos_b - sin_a * sin_b).reshape(count, LAGS)
-    sin_ab = (sin_a * cos_b + cos_a * sin_b).reshape(count, LAGS)
     bins = start + jnp.arange(count, dtype=jnp.int32)
     weight = (jnp.where(bins == 0, 1.0, 2.0).astype(jnp.float32) / jnp.sqrt(jnp.float32(F)))[:, None]
-    cos_part = (cos_ab * weight).astype(jnp.bfloat16)
-    sin_part = (-sin_ab * weight).astype(jnp.bfloat16)
-    return cos_part, sin_part
+    return jnp.cos(coarse), jnp.sin(coarse), jnp.cos(fine), jnp.sin(fine), weight
+
+
+def fill_tables(cos_a, sin_a, cos_b, sin_b, weight, cos_out, sin_out):
+    fine = cos_b.shape[0]
+    for q in range(cos_a.shape[0]):
+        ca = cos_a[q:q + 1, :]
+        sa = sin_a[q:q + 1, :]
+        cb = cos_b[...]
+        sb = sin_b[...]
+        w = weight[q * fine:(q + 1) * fine, :]
+        cos_out[q * fine:(q + 1) * fine, :] = ((ca * cb - sa * sb) * w).astype(cos_out.dtype)
+        sin_out[q * fine:(q + 1) * fine, :] = (-(sa * cb + ca * sb) * w).astype(sin_out.dtype)
 
 
 def whiten(spectra):
@@ -224,6 +230,65 @@
     )(x)
 
 
+def spectra_kernel(x_ref, cos_a, sin_a, cos_b, sin_b, weight, out_ref, cos_out, sin_out,
+                   local_sem, send_sem, recv_sem):
+    n = x_ref.shape[0]
+    me = lax.axis_index("chan")
+    group = lax.axis_index("grp")
+
+    barrier = pltpu.get_barrier_semaphore()
+    for step in range(1, n):
+        pl.semaphore_signal(barrier, inc=1, device_id=(group, lax.rem(me + step, n)),
+                            device_id_type=pl.DeviceIdType.MESH)
+    pl.semaphore_wait(barrier, n - 1)
+
+    def copy(step, target, slot):
+        return pltpu.make_async_remote_copy(
+            src_ref=x_ref.at[target],
+            dst_ref=out_ref.at[slot],
+            send_sem=send_sem.at[step],
+            recv_sem=recv_sem.at[step],
+            device_id=(group, target),
+            device_id_type=pl.DeviceIdType.MESH,
+        )
+
+    own = pltpu.make_async_copy(x_ref.at[me], out_ref.at[me], local_sem)
+    own.start()
+    for step in range(1, n):
+        copy(step, lax.rem(me + step, n), me).start()
+
+    fill_tables(cos_a, sin_a, cos_b, sin_b, weight, cos_out, sin_out)
+
+    own.wait()
+    for step in range(1, n):
+        copy(step, lax.rem(me + step, n), me).wait_send()
+        source = lax.rem(me + n - step, n)
+        copy(step, source, source).wait_recv()
+
+
+def spectra_exchange(x, factors, collective):
+    n = x.shape[0]
+    part = factors[4].shape[0]
+    anywhere = pl.BlockSpec(memory_space=pl.ANY)
+    vmem = pl.BlockSpec(memory_space=pltpu.VMEM)
+    return pl.pallas_call(
+        spectra_kernel,
+        out_shape=(
+            jax.ShapeDtypeStruct(x.shape, x.dtype),
+            jax.ShapeDtypeStruct((part, LAGS), jnp.bfloat16),
+            jax.ShapeDtypeStruct((part, LAGS), jnp.bfloat16),
+        ),
+        in_specs=[anywhere] + [vmem] * 5,
+        out_specs=(anywhere, vmem, vmem),
+        scratch_shapes=[
+            pltpu.SemaphoreType.DMA(()),
+            pltpu.SemaphoreType.DMA((n,)),
+            pltpu.SemaphoreType.DMA((n,)),
+        ],
+        compiler_params=pltpu.CompilerParams(collective_id=collective, has_side_effects=True),
+    )(x, *factors)
+
+
 def local(spectra, pair_blocks, owners):
     groups_count = lax.axis_size("grp")
     chan_count = lax.axis_size("chan")
@@ -240,7 +305,7 @@
     extra = jnp.zeros((part,), jnp.bfloat16).at[: listed.shape[0]].set(listed)
     extra = jnp.broadcast_to(extra[None, None, :], (chan_count, 1, part))
     sent = jnp.concatenate([chunks, extra], axis=1)
-    got = lax.all_to_all(sent, "chan", split_axis=0, concat_axis=0, tiled=True)
+    got, cos_part, sin_part = spectra_exchange(sent, table_factors(me * part, part), 2)
     rows_per = channels * WINDOWS * 2
     group_channels = chan_count * channels
     panel = got[:, :rows_per].reshape(group_channels, WINDOWS * 2 * part)
@@ -253,7 +318,6 @@
     left_hot = (left_ch.reshape(-1, 1) == channel_ids).astype(jnp.bfloat16)
     right_hot = (right_ch.reshape(-1, 1) == channel_ids).astype(jnp.bfloat16)
 
-    cos_part, sin_part = table_slice(me * part, part)
     gathered = pair_exchange(left_hot, right_hot, panel, cos_part, sin_part, chan_count, 0)
     corr = jnp.sum(gathered.astype(jnp.float32), axis=0).reshape(NB_SRC, pairs * LAGS)
 

time: 78.8 us -> 86 us (1.091)
  Pallas kernels: 37.8 us -> 61.4 us
  waiting for transfers between devices: 9.45 us -> 0 us
  starting transfers between devices: 6.81 us -> 0 us
    pallas_call x0 -> x1, Pallas kernels: none -> 23.7 us  [spectra_exchange(): pl.pallas_call(spectra_kernel, out_shape=(jax.ShapeDtypeStruct(x.shape, x...]
    all_to_all x1 -> x0, waiting for transfers between devices: 9.45 us -> none  [local(): got = lax.all_to_all(sent, 'chan', split_axis=0, concat_axis=0, tiled=True)]
    all_to_all x1 -> x0, starting transfers between devices: 6.81 us -> none  [local(): got = lax.all_to_all(sent, 'chan', split_axis=0, concat_axis=0, tiled=True)]
    sin x0 -> x2, other arithmetic: none -> 3.71 us  [the longest x1 2.88 us: table_factors(): jnp.sin(fine)]
    convert_element_type x1 -> x0, other arithmetic: 2.45 us -> none  [table_slice(): sin_part = (-sin_ab * weight).astype(jnp.bfloat16)]
    cos x2 -> x0, other arithmetic: 2.26 us -> none  [the longest x1 2.04 us: table_slice(): cos_b, sin_b = (jnp.cos(fine)[None, :, :], jnp.sin(fine)[None, :, :])]
    neg x1 -> x0, other arithmetic: 1.19 us -> none  [table_slice(): sin_part = (-sin_ab * weight).astype(jnp.bfloat16)]
    reshape x0 -> x1, local copies, waits for them, and re-layouts: none -> 1.08 us  [local(): white.reshape(channels, WINDOWS, 2, chan_count, part)]
  transfers between devices with their start and end apart: 1 -> 0, of which waited for: 1 -> 0; matrix products, arithmetic and copies ran while one was open for 9% -> 0% of each run, Pallas kernels for 0% -> 0%
where the time goes in v8:
time: 86 us; the launch traced here: 85.7 us
  Pallas kernels  61.4 us (71%)
  other arithmetic  17 us (20%)
  local copies, waits for them, and re-layouts  7.08 us (8%)
    pallas_call x1, Pallas kernels, pair_exchange(): pl.pallas_call(pair_exchange_kernel, out_shape=jax.ShapeDtypeStruct((chan...  24.2 us
    pallas_call x1, Pallas kernels, spectra_exchange(): pl.pallas_call(spectra_kernel, out_shape=(jax.ShapeDtypeStruct(x.shape, x...  23.7 us
    pallas_call x1, Pallas kernels, exchange(): pl.pallas_call(functools.partial(exchange_kernel, axis, other_axis, axis_...  13.4 us
    sin x1, other arithmetic, table_factors(): jnp.sin(fine)  2.88 us
    reshape x1, other arithmetic, local(): return received.reshape(1, 1, slot_count, pairs, LAGS)  1.98 us
    convert_element_type x1, other arithmetic, whiten(): values = spectra.astype(jnp.float32)  1.84 us

profile of v8, /device:TPU:1, one launch (start us, length us, event | category | flops | bytes accessed | tf_op | source)
XLA Modules:
  0.0 85.7 jit_solution(10165237385427038794)
XLA Ops:
  0.0 0.8 fusion.17
  0.8 1.8 %copy_convert_fusion = f32[16,2,2,8192]{3,0,2,1:T(8,128)S(1)} fusion(bf16[16,2,2,8192]{3,2,1,0:T(2,128)(2,1)} %param.5), kind=kLoop, calls=%fused_computation.8 | loop fusion | flops 524288 | bytes 3145728 | tf_op jit(solution)/shard_map/convert_element_type | solution.py:46
  2.7 0.2 fusion.11
  2.9 0.0 copy-start
  2.9 0.3 rsqrt_bitcast_fusion
  3.2 1.0 %copy-done = bf16[16,2,2,8192]{3,2,1,0:T(2,128)(2,1)S(1)} copy-done((bf16[16,2,2,8192]{3,2,1,0:T(2,128)(2,1)S(1)}, bf16[16,2,2,8192]{3,2,1,0:T(2,128)(2,1)}, u32[]{:S(2)}) %copy-start) | copy-done | bytes 1048600
  4.2 0.6 multiply_convert_fusion
  4.8 0.6 copy.12
  5.4 0.0 copy-start.2
  5.4 1.1 %copy.17 = bf16[16,2,2,8,1024]{4,2,1,0,3:T(2,128)(2,1)S(1)} copy(bf16[16,2,2,8,1024]{4,3,0,2,1:T(8,128)(2,1)S(1)} %bitcast.17) | data formatting | bytes 2097152 | tf_op jit(solution)/shard_map/reshape | solution.py:302
  6.5 0.6 reshape.228
  7.1 0.0 copy-done.2
  7.1 0.1 copy.11
  7.3 0.1 convert_element_type.67
  7.4 1.2 %pad_maximum_fusion.x_ref = bf16[8,65,1024]{2,1,0:T(8,128)(2,1)} fusion(bf16[8,1,1024]{2,1,0:T(2,128)(2,1)S(1)} %broadcast_in_dim.64, bf16[8,64,1024]{2,1,0:T(8,128)(2,1)S(1)} %reshape.228), kind=kLoop, calls=%fused_computation.3 | loop fusion | flops 2129920 | bytes 2129920 | tf_op jit(solution)/shard_map/concatenate | solution.py:307
  8.6 2.9 %fusion.9 = (f32[128,1024]{1,0:T(8,128)}, f32[128,1024]{1,0:T(8,128)}) fusion(s32[1024]{0:T(1024)S(1)} %iota_add_fusion.2), kind=kLoop, calls=%fused_computation.26 | loop fusion | flops 1835008 | bytes 1052672 | tf_op jit(solution)/shard_map/sin | solution.py:30
  11.5 0.9 %select_multiply_fusion.weight = f32[1024,1]{1,0:T(8,128)} fusion(s32[]{:T(128)S(6)} %mul.112), kind=kLoop, calls=%fused_computation.17 | loop fusion | flops 4096 | bytes 4100 | tf_op jit(solution)/shard_map/div | solution.py:29
  12.4 23.7 %shard_map.37 = (bf16[8,65,1024]{2,1,0:T(8,128)(2,1)}, bf16[1024,1024]{1,0:T(8,128)(2,1)}, bf16[1024,1024]{1,0:T(8,128)(2,1)}) custom-call(bf16[8,65,1024]{2,1,0:T(8,128)(2,1)} %pad_maximum_fusion.x_ref, f32[8,1024]{1,0:T(8,128)} %get-tuple-element.28.cos_a, f32[8,1024]{1,0:T(8,128)} %get-tuple-element.27.sin_a, f32[128,1024]{1,0:T(8,128)} %get-tuple-element.30.cos_b, ...), custom_call_target="tpu_custom_call" | custom-call | tf_op jit(solution)/shard_map/pallas_call | solution.py:274
  36.1 0.0 copy-start.1
  36.1 0.8 convert_reduce_fusion.2
  36.9 0.1 convert_element_type.72
  37.0 0.2 fusion.12
  37.3 0.1 iota_add_fusion
  37.4 0.2 add.147
  37.6 0.2 eq.85
  37.8 0.8 fusion.7.left_hot
  38.6 0.1 add.151
  38.6 0.2 eq.89
  38.8 0.8 fusion.8.right_hot
  39.6 0.0 copy-done.1
  39.6 0.1 slice.34
  39.7 1.4 %reshape.229.panel = bf16[128,4096]{1,0:T(8,128)(2,1)} reshape(bf16[8,64,1024]{2,1,0:T(8,128)(2,1)S(1)} %slice.34) | data formatting | bytes 2097152 | tf_op jit(solution)/shard_map/reshape | solution.py:311
  41.2 0.0 copy-start.3
  41.2 24.2 %shard_map.38 = bf16[8,72,1024]{2,1,0:T(8,128)(2,1)} custom-call(bf16[8,72,128]{2,1,0:T(8,128)(2,1)} %fusion.7.left_hot, bf16[8,72,128]{2,1,0:T(8,128)(2,1)} %fusion.8.right_hot, bf16[128,4096]{1,0:T(8,128)(2,1)} %reshape.229.panel, bf16[1024,1024]{1,0:T(8,128)(2,1)} %get-tuple-element.23.cos_ref, bf16[1024,1024]{1,0:T(8,128)(2,1)} %get-tuple-element.24.sin_ref), custom_call_target="tpu_custom_call" | custom-call | flops 3623878656 | bytes 6422528 | tf_op jit(solution)/shard_map/pallas_call | solution.py:144
  65.4 1.5 %convert_reduce_fusion = bf16[72,1024]{1,0:T(8,128)(2,1)S(1)} fusion(bf16[8,72,1024]{2,1,0:T(8,128)(2,1)} %shard_map.38), kind=kLoop, calls=%fused_computation.1 | loop fusion | flops 1105920 | bytes 1327104 | tf_op jit(solution)/shard_map/reduce_sum | solution.py:322
  66.9 0.1 reshape.230
  67.0 0.0 copy-done.3
  67.0 0.2 convert_reduce_fusion.1
  67.2 0.6 iota_reduce_fusion
  67.8 0.8 gather_fusion
  68.6 0.3 gather.7
  68.9 0.1 broadcast_in_dim.62
  69.0 0.1 fusion.19
  69.1 0.1 broadcast_in_dim.34
  69.2 1.1 %select_convert_fusion.x_ref = bf16[16,1,3,4,1024]{4,3,2,1,0:T(4,128)(2,1)} fusion(bf16[16,1,3,4,1024]{4,3,2,1,0:T(4,128)(2,1)S(1)} %gather.7, pred[16,3]{1,0:T(8,128)(4,1)S(1)} %broadcast_in_dim.62, pred[16,3]{1,0:T(8,128)(4,1)S(1)} %broadcast_in_dim.34), kind=kLoop, calls=%fused_computation.10 | loop fusion | flops 393216 | bytes 786528 | tf_op jit(solution)/shard_map/convert_element_type | solution.py:333
  70.3 13.4 %shard_map.39 = bf16[16,1,3,4,1024]{4,3,2,1,0:T(4,128)(2,1)} custom-call(bf16[16,1,3,4,1024]{4,3,2,1,0:T(4,128)(2,1)} %select_convert_fusion.x_ref), custom_call_target="tpu_custom_call" | custom-call | tf_op jit(solution)/shard_map/pallas_call | solution.py:219
  83.7 2.0 %convert.1 = f32[1,1,48,4,1024]{4,3,2,1,0:T(4,128)} convert(bf16[1,1,48,4,1024]{4,3,2,1,0:T(4,128)(2,1)} %bitcast.19) | non-fusion elementwise | flops 196608 | bytes 1179648 | tf_op jit(solution)/shard_map/reshape | solution.py:335
  (10 shorter events, 0.1 us)
Async XLA Ops:
  2.9 1.2 %copy-start = (bf16[16,2,2,8192]{3,2,1,0:T(2,128)(2,1)S(1)}, bf16[16,2,2,8192]{3,2,1,0:T(2,128)(2,1)}, u32[]{:S(2)}) copy-start(bf16[16,2,2,8192]{3,2,1,0:T(2,128)(2,1)} %param.5) | copy-start | bytes 3145732
  5.4 1.7 %copy-start.2 = (s32[1,1,18,2]{2,3,1,0:T(2,128)S(1)}, s32[1,1,18,2]{2,3,1,0:T(2,128)}, u32[]{:S(2)}) copy-start(s32[1,1,18,2]{2,3,1,0:T(2,128)} %param.6) | copy-start | bytes 436
  36.1 3.5 %copy-start.1 = (bf16[8,65,1024]{2,1,0:T(8,128)(2,1)S(1)}, bf16[8,65,1024]{2,1,0:T(8,128)(2,1)}, u32[]{:S(2)}) copy-start(bf16[8,65,1024]{2,1,0:T(8,128)(2,1)} %get-tuple-element.22) | copy-start | bytes 3194884
  41.2 25.8 %copy-start.3 = (s32[1,1,18,1]{2,3,1,0:T(1,128)S(1)}, s32[1,1,18,1]{2,3,1,0:T(1,128)}, u32[]{:S(2)}) copy-start(s32[1,1,18,1]{2,3,1,0:T(1,128)} %param.7) | copy-start | bytes 220

commit v9 on v7

--- a/solution.py
+++ b/solution.py
@@ -267,7 +267,7 @@
     filled = jnp.any(chooser, axis=1)
     placed = jnp.where(filled[:, None], jnp.take(corr, source, axis=0), 0.0)
     placed = placed.reshape(groups_count, 1, MOST, pairs, LAGS).astype(jnp.bfloat16)
-    received = exchange(placed, "grp", "chan", True, 1, 1).astype(jnp.float32)
+    received = lax.all_to_all(placed, "grp", split_axis=0, concat_axis=0, tiled=True).astype(jnp.float32)
     return received.reshape(1, 1, slot_count, pairs, LAGS)
 
 

time: 78.8 us -> 79.7 us (1.011)
  blocking collectives: 0 us -> 16.1 us
  Pallas kernels: 37.8 us -> 24.4 us
  other arithmetic: 17.5 us -> 15.7 us
    all_to_all x0 -> x1, blocking collectives: none -> 16.1 us  [local(): lax.all_to_all(placed, 'grp', split_axis=0, concat_axis=0, tiled=True)]
    pallas_call x1 -> x0, Pallas kernels: 13.4 us -> none  [exchange(): pl.pallas_call(functools.partial(exchange_kernel, axis, other_axis, axis_...]
    reshape x1, other arithmetic: 1.98 us -> 0.98 us  [local(): return received.reshape(1, 1, slot_count, pairs, LAGS)]
where the time goes in v9:
time: 79.7 us; the launch traced here: 79.3 us
  Pallas kernels  24.4 us (31%)
  blocking collectives  16.1 us (20%)
  other arithmetic  15.7 us (20%)
  waiting for transfers between devices  9.45 us (12%)
  starting transfers between devices  6.81 us (9%)
  local copies, waits for them, and re-layouts  6.64 us (8%)
    pallas_call x1, Pallas kernels, pair_exchange(): pl.pallas_call(pair_exchange_kernel, out_shape=jax.ShapeDtypeStruct((chan...  24.4 us
    all_to_all x1, blocking collectives, local(): lax.all_to_all(placed, 'grp', split_axis=0, concat_axis=0, tiled=True)  16.1 us
    all_to_all x1, waiting for transfers between devices, local(): got = lax.all_to_all(sent, 'chan', split_axis=0, concat_axis=0, tiled=True)  9.45 us
    all_to_all x1, starting transfers between devices, local(): got = lax.all_to_all(sent, 'chan', split_axis=0, concat_axis=0, tiled=True)  6.81 us
    convert_element_type x1, other arithmetic, table_slice(): sin_part = (-sin_ab * weight).astype(jnp.bfloat16)  2.45 us
    cos x1, other arithmetic, table_slice(): cos_b, sin_b = (jnp.cos(fine)[None, :, :], jnp.sin(fine)[None, :, :])  2.04 us
    convert_element_type x1, other arithmetic, whiten(): values = spectra.astype(jnp.float32)  1.84 us
  transfers between devices with their start and end apart: 1, of which 1 were waited for; matrix products, arithmetic and copies ran while one was open for 9% of the time, Pallas kernels for 0%

profile of v9, /device:TPU:1, one launch (start us, length us, event | category | flops | bytes accessed | tf_op | source)
XLA Modules:
  0.0 79.3 jit_solution(50848107300243512)
XLA Ops:
  0.0 1.8 %copy_convert_fusion = f32[16,2,2,8192]{3,0,2,1:T(8,128)S(1)} fusion(bf16[16,2,2,8192]{3,2,1,0:T(2,128)(2,1)} %param.5), kind=kLoop, calls=%fused_computation.13 | loop fusion | flops 524288 | bytes 3145728 | tf_op jit(solution)/shard_map/convert_element_type | solution.py:40
  1.8 0.0 copy-start
  1.9 0.2 fusion.15
  2.1 0.3 rsqrt_bitcast_fusion
  2.4 0.7 copy-done
  3.1 0.7 multiply_convert_fusion
  3.7 0.6 copy.18
  4.3 0.0 copy-start.1
  4.3 1.1 %copy.15 = bf16[8,16,2,2,1024]{4,3,2,1,0:T(2,128)(2,1)S(1)} copy(bf16[8,16,2,2,1024]{4,0,1,3,2:T(8,128)(2,1)S(1)} %bitcast.30) | data formatting | bytes 2097152 | tf_op jit(solution)/shard_map/transpose | solution.py:237
  5.4 0.4 reshape.349
  5.9 0.0 copy-done.1
  5.9 0.0 copy-start.2
  5.9 0.1 copy.16
  6.0 0.1 convert_element_type.99
  6.2 1.1 %pad_maximum_fusion = bf16[8,65,1024]{2,1,0:T(8,128)(2,1)} fusion(bf16[8,1,1024]{2,1,0:T(2,128)(2,1)S(1)} %broadcast_in_dim.38, bf16[8,64,1024]{2,1,0:T(8,128)(2,1)S(1)} %reshape.349), kind=kLoop, calls=%fused_computation.9 | loop fusion | flops 2129920 | bytes 2129920 | tf_op jit(solution)/shard_map/concatenate | solution.py:242
  7.3 6.8 %all-to-all-start = ((bf16[8,65,1024]{2,1,0:T(8,128)(2,1)}), bf16[8,65,1024]{2,1,0:T(8,128)(2,1)S(1)}, u32[]{:S(2)}, u32[]{:S(2)}) async-start(bf16[8,65,1024]{2,1,0:T(8,128)(2,1)} %pad_maximum_fusion), calls=%async_computation | async-start | bytes 2359296 | tf_op jit(solution)/shard_map/all_to_all | solution.py:243
  14.1 0.0 copy-done.2
  14.2 0.2 convert_reduce_fusion.1
  14.3 0.6 iota_reduce_fusion
  15.0 0.1 fusion.23
  15.1 2.0 %fusion.14 = (f32[128,1024]{1,0:T(8,128)S(1)}, f32[128,1024]{1,0:T(8,128)S(1)}) fusion(s32[1024]{0:T(1024)S(1)} %iota_add_fusion.2), kind=kLoop, calls=%fused_computation.32 | loop fusion | flops 1835008 | bytes 1052672 | tf_op jit(solution)/shard_map/cos | solution.py:29
  17.1 0.2 fusion.22
  17.3 0.1 broadcast_in_dim.36
  17.4 0.1 broadcast_in_dim.31
  17.5 1.2 %add_negate_fusion = (f32[8,128,1024]{2,1,0:T(8,128)S(1)}, f32[8,128,1024]{2,1,0:T(8,128)S(1)}) fusion(f32[128,1024]{1,0:T(8,128)S(1)} %get-tuple-element.28, f32[8,1024]{1,0:T(8,128)S(1)} %get-tuple-element.24, f32[128,1024]{1,0:T(8,128)S(1)} %get-tuple-element.27, f32[8,1024]{1,0:T(8,128)S(1)} %get-tuple-element.23), kind=kLoop, calls=%fused_computation.5 | loop fusion | flops 7340032 | bytes 9502720 | tf_op jit(solution)/shard_map/neg | solution.py:35
  18.7 2.4 %fusion = (bf16[1024,1024]{1,0:T(8,128)(2,1)}, bf16[1024,1024]{1,0:T(8,128)(2,1)}) fusion(f32[8,128,1024]{2,1,0:T(8,128)S(1)} %get-tuple-element.21, f32[1024]{0:T(1024)S(1)} %select_multiply_fusion, f32[8,128,1024]{2,1,0:T(8,128)S(1)} %get-tuple-element.22), kind=kLoop, calls=%fused_computation.2 | loop fusion | flops 4194304 | bytes 12587008 | tf_op jit(solution)/shard_map/convert_element_type | solution.py:35
  21.2 9.5 %all-to-all-done = bf16[8,65,1024]{2,1,0:T(8,128)(2,1)S(1)} async-done(((bf16[8,65,1024]{2,1,0:T(8,128)(2,1)}), bf16[8,65,1024]{2,1,0:T(8,128)(2,1)S(1)}, u32[]{:S(2)}, u32[]{:S(2)}) %all-to-all-start) | async-done | bytes 1064992 | tf_op jit(solution)/shard_map/all_to_all | solution.py:243
  30.6 0.1 convert_element_type.102
  30.7 0.2 fusion.16
  31.0 0.1 iota_add_fusion
  31.1 0.2 add.161
  31.3 0.2 eq.80
  31.5 0.8 %fusion.11.left_hot = bf16[8,72,128]{2,1,0:T(8,128)(2,1)} fusion(s32[8,72]{1,0:T(8,128)S(1)} %eq.80), kind=kLoop, calls=%fused_computation.29 | loop fusion | flops 147456 | bytes 149760 | tf_op jit(solution)/shard_map/convert_element_type | solution.py:253
  32.3 0.1 add.165
  32.3 0.2 eq.84
  32.5 0.8 %fusion.12.right_hot = bf16[8,72,128]{2,1,0:T(8,128)(2,1)} fusion(s32[8,72]{1,0:T(8,128)S(1)} %eq.84), kind=kLoop, calls=%fused_computation.30 | loop fusion | flops 147456 | bytes 149760 | tf_op jit(solution)/shard_map/convert_element_type | solution.py:254
  33.3 0.1 slice.42
  33.4 1.4 %reshape.350.panel = bf16[128,4096]{1,0:T(8,128)(2,1)} reshape(bf16[8,64,1024]{2,1,0:T(8,128)(2,1)S(1)} %slice.42) | data formatting | bytes 2097152 | tf_op jit(solution)/shard_map/reshape | solution.py:246
  34.9 24.4 %shard_map.37 = bf16[8,72,1024]{2,1,0:T(8,128)(2,1)} custom-call(bf16[8,72,128]{2,1,0:T(8,128)(2,1)} %fusion.11.left_hot, bf16[8,72,128]{2,1,0:T(8,128)(2,1)} %fusion.12.right_hot, bf16[128,4096]{1,0:T(8,128)(2,1)} %reshape.350.panel, bf16[1024,1024]{1,0:T(8,128)(2,1)} %get-tuple-element.26.cos_ref, bf16[1024,1024]{1,0:T(8,128)(2,1)} %get-tuple-element.25.sin_ref), custom_call_target="tpu_custom_call" | custom-call | flops 3623878656 | bytes 6422528 | tf_op jit(solution)/shard_map/pallas_call | solution.py:138
  59.3 1.5 %convert_reduce_fusion = bf16[72,1024]{1,0:T(8,128)(2,1)S(1)} fusion(bf16[8,72,1024]{2,1,0:T(8,128)(2,1)} %shard_map.37), kind=kLoop, calls=%fused_computation.7 | loop fusion | flops 1105920 | bytes 1327104 | tf_op jit(solution)/shard_map/reduce_sum | solution.py:258
  60.7 0.1 reshape.351
  60.8 0.8 gather_fusion
  61.6 0.3 gather.7
  61.9 0.3 fusion.4
  62.3 16.1 %all_to_all.10 = bf16[16,1,3,4,1024]{4,3,2,1,0:T(4,128)(2,1)S(1)} all-to-all(bf16[16,1,3,4,1024]{4,3,2,1,0:T(4,128)(2,1)S(1)} %fusion.4), channel_id=1, replica_groups=mesh['grp'=16,'chan'=8] {'grp'}, dimensions={0} | all-to-all | bytes 786432 | tf_op jit(solution)/shard_map/all_to_all | solution.py:270
  78.4 1.0 %convert.1 = f32[1,1,48,4,1024]{4,3,2,1,0:T(4,128)} convert(bf16[1,1,48,4,1024]{4,3,2,1,0:T(4,128)(2,1)S(1)} %bitcast.31) | non-fusion elementwise | flops 196608 | bytes 1179648 | tf_op jit(solution)/shard_map/reshape | solution.py:271
  (12 shorter events, 0.1 us)
Async XLA Ops:
  1.8 1.2 %copy-start = (bf16[16,2,2,8192]{3,2,1,0:T(2,128)(2,1)S(1)}, bf16[16,2,2,8192]{3,2,1,0:T(2,128)(2,1)}, u32[]{:S(2)}) copy-start(bf16[16,2,2,8192]{3,2,1,0:T(2,128)(2,1)} %param.5) | copy-start | bytes 3145732
  4.3 1.5 %copy-start.1 = (s32[1,1,18,2]{2,3,1,0:T(2,128)S(1)}, s32[1,1,18,2]{2,3,1,0:T(2,128)}, u32[]{:S(2)}) copy-start(s32[1,1,18,2]{2,3,1,0:T(2,128)} %param.6) | copy-start | bytes 436
  5.9 8.3 %copy-start.2 = (s32[1,1,18,1]{2,3,1,0:T(1,128)S(1)}, s32[1,1,18,1]{2,3,1,0:T(1,128)}, u32[]{:S(2)}) copy-start(s32[1,1,18,1]{2,3,1,0:T(1,128)} %param.7) | copy-start | bytes 220
  7.3 23.3 %all-to-all-start = ((bf16[8,65,1024]{2,1,0:T(8,128)(2,1)}), bf16[8,65,1024]{2,1,0:T(8,128)(2,1)S(1)}, u32[]{:S(2)}, u32[]{:S(2)}) async-start(bf16[8,65,1024]{2,1,0:T(8,128)(2,1)} %pad_maximum_fusion), calls=%async_computation | async-start | bytes 2359296 | tf_op jit(solution)/shard_map/all_to_all | solution.py:243

commit v10 on v7

--- a/solution.py
+++ b/solution.py
@@ -255,17 +255,15 @@
 
     cos_part, sin_part = table_slice(me * part, part)
     gathered = pair_exchange(left_hot, right_hot, panel, cos_part, sin_part, chan_count, 0)
-    corr = jnp.sum(gathered.astype(jnp.float32), axis=0).reshape(NB_SRC, pairs * LAGS)
-
     owner_list = owners[0, 0, :, 0]
     same = owner_list[:, None] == owner_list[None, :]
     earlier = jnp.arange(NB_SRC)[None, :] < jnp.arange(NB_SRC)[:, None]
     order_rank = jnp.sum(jnp.logical_and(same, earlier), axis=1)
     slot_ids = owner_list * MOST + order_rank
-    chooser = slot_ids[None, :] == jnp.arange(slot_count, dtype=jnp.int32)[:, None]
-    source = jnp.argmax(chooser, axis=1)
-    filled = jnp.any(chooser, axis=1)
-    placed = jnp.where(filled[:, None], jnp.take(corr, source, axis=0), 0.0)
+    chooser = (slot_ids[None, :] == jnp.arange(slot_count, dtype=jnp.int32)[:, None]).astype(jnp.bfloat16)
+    chooser = jnp.tile(chooser, (1, chan_count))
+    gathered = gathered.reshape(chan_count * NB_SRC, pairs * LAGS)
+    placed = jnp.dot(chooser, gathered, preferred_element_type=jnp.float32)
     placed = placed.reshape(groups_count, 1, MOST, pairs, LAGS).astype(jnp.bfloat16)
     received = exchange(placed, "grp", "chan", True, 1, 1).astype(jnp.float32)
     return received.reshape(1, 1, slot_count, pairs, LAGS)

time: 78.8 us -> 79.2 us (level)
  other arithmetic: 17.5 us -> 14.2 us
  local copies, waits for them, and re-layouts: 6.64 us -> 9.15 us
    reshape x1, local copies, waits for them, and re-layouts: 0.1 us -> 2.38 us  [local(): gathered = gathered.reshape(chan_count * NB_SRC, pairs * LAGS)]
    reduce_sum x1 -> x0, other arithmetic: 1.47 us -> none  [local(): jnp.sum(gathered.astype(jnp.float32), axis=0).reshape(NB_SRC, pairs * LAGS)]
    unnamed x7 -> x8, local copies, waits for them, and re-layouts: 1.32 us -> 2.62 us
    convert_element_type x1, other arithmetic: 1.1 us -> 0.01 us  [local(): (slot_ids[None, :] == jnp.arange(slot_count, dtype=jnp.int32)[:, None]).a...]
    gather x2 -> x0, local copies, waits for them, and re-layouts: 1.07 us -> none  [local(): placed = jnp.where(filled[:, None], jnp.take(corr, source, axis=0), 0.0)]
  transfers between devices with their start and end apart: 1 -> 1, of which waited for: 1 -> 1; matrix products, arithmetic and copies ran while one was open for 9% -> 8% of each run, Pallas kernels for 0% -> 0%
where the time goes in v10:
time: 79.2 us; the launch traced here: 78.8 us
  Pallas kernels  37.8 us (48%)
  other arithmetic  14.2 us (18%)
  waiting for transfers between devices  10.2 us (13%)
  local copies, waits for them, and re-layouts  9.15 us (12%)
  starting transfers between devices  6.95 us (9%)
    pallas_call x1, Pallas kernels, pair_exchange(): pl.pallas_call(pair_exchange_kernel, out_shape=jax.ShapeDtypeStruct((chan...  24.4 us
    pallas_call x1, Pallas kernels, exchange(): pl.pallas_call(functools.partial(exchange_kernel, axis, other_axis, axis_...  13.4 us
    all_to_all x1, waiting for transfers between devices, local(): got = lax.all_to_all(sent, 'chan', split_axis=0, concat_axis=0, tiled=True)  10.2 us
    all_to_all x1, starting transfers between devices, local(): got = lax.all_to_all(sent, 'chan', split_axis=0, concat_axis=0, tiled=True)  6.95 us
    unnamed x8, local copies, waits for them, and re-layouts  2.62 us
    convert_element_type x1, other arithmetic, table_slice(): sin_part = (-sin_ab * weight).astype(jnp.bfloat16)  2.45 us
    reshape x1, local copies, waits for them, and re-layouts, local(): gathered = gathered.reshape(chan_count * NB_SRC, pairs * LAGS)  2.38 us
    cos x1, other arithmetic, table_slice(): cos_b, sin_b = (jnp.cos(fine)[None, :, :], jnp.sin(fine)[None, :, :])  2.04 us
  transfers between devices with their start and end apart: 1, of which 1 were waited for; matrix products, arithmetic and copies ran while one was open for 8% of the time, Pallas kernels for 0%

profile of v10, /device:TPU:1, one launch (start us, length us, event | category | flops | bytes accessed | tf_op | source)
XLA Modules:
  0.0 78.8 jit_solution(16692489178978025170)
XLA Ops:
  0.0 1.8 %copy_convert_fusion = f32[16,2,2,8192]{3,0,2,1:T(8,128)S(1)} fusion(bf16[16,2,2,8192]{3,2,1,0:T(2,128)(2,1)} %param.5), kind=kLoop, calls=%fused_computation.14 | loop fusion | flops 524288 | bytes 3145728 | tf_op jit(solution)/shard_map/convert_element_type | solution.py:40
  1.8 0.2 fusion.14
  2.1 0.0 copy-start
  2.1 0.3 rsqrt_bitcast_fusion
  2.4 1.0 %copy-done = bf16[16,2,2,8192]{3,2,1,0:T(2,128)(2,1)S(1)} copy-done((bf16[16,2,2,8192]{3,2,1,0:T(2,128)(2,1)S(1)}, bf16[16,2,2,8192]{3,2,1,0:T(2,128)(2,1)}, u32[]{:S(2)}) %copy-start) | copy-done | bytes 1048600
  3.3 0.7 multiply_convert_fusion
  4.0 0.6 copy.30
  4.6 0.0 copy-start.1
  4.6 1.1 %copy.21 = bf16[8,16,2,2,1024]{4,3,2,1,0:T(2,128)(2,1)S(1)} copy(bf16[8,16,2,2,1024]{4,0,1,3,2:T(8,128)(2,1)S(1)} %bitcast.37) | data formatting | bytes 2097152 | tf_op jit(solution)/shard_map/transpose | solution.py:237
  5.7 0.4 reshape.343
  6.1 0.0 copy-done.1
  6.1 0.1 copy.22
  6.3 0.1 convert_element_type.98
  6.4 1.1 %pad_maximum_fusion = bf16[8,65,1024]{2,1,0:T(8,128)(2,1)} fusion(bf16[8,1,1024]{2,1,0:T(2,128)(2,1)S(1)} %broadcast_in_dim.8, bf16[8,64,1024]{2,1,0:T(8,128)(2,1)S(1)} %reshape.343), kind=kLoop, calls=%fused_computation.10 | loop fusion | flops 2129920 | bytes 2129920 | tf_op jit(solution)/shard_map/concatenate | solution.py:242
  7.5 0.0 copy-start.2
  7.5 6.9 %all-to-all-start = ((bf16[8,65,1024]{2,1,0:T(8,128)(2,1)}), bf16[8,65,1024]{2,1,0:T(8,128)(2,1)S(1)}, u32[]{:S(2)}, u32[]{:S(2)}) async-start(bf16[8,65,1024]{2,1,0:T(8,128)(2,1)} %pad_maximum_fusion), calls=%async_computation | async-start | bytes 2359296 | tf_op jit(solution)/shard_map/all_to_all | solution.py:243
  14.5 2.0 %fusion.13 = (f32[128,1024]{1,0:T(8,128)S(1)}, f32[128,1024]{1,0:T(8,128)S(1)}) fusion(s32[1024]{0:T(1024)S(1)} %iota_add_fusion.2), kind=kLoop, calls=%fused_computation.31 | loop fusion | flops 1835008 | bytes 1052672 | tf_op jit(solution)/shard_map/cos | solution.py:29
  16.6 0.2 fusion.23
  16.8 0.0 copy-done.2
  16.8 0.2 convert_reduce_fusion
  17.0 0.1 dot_general.9
  17.2 1.2 %add_negate_fusion = (f32[8,128,1024]{2,1,0:T(8,128)S(1)}, f32[8,128,1024]{2,1,0:T(8,128)S(1)}) fusion(f32[128,1024]{1,0:T(8,128)S(1)} %get-tuple-element.26, f32[8,1024]{1,0:T(8,128)S(1)} %get-tuple-element.22, f32[128,1024]{1,0:T(8,128)S(1)} %get-tuple-element.25, f32[8,1024]{1,0:T(8,128)S(1)} %get-tuple-element.21), kind=kLoop, calls=%fused_computation.4 | loop fusion | flops 7340032 | bytes 9502720 | tf_op jit(solution)/shard_map/neg | solution.py:35
  18.3 2.4 %fusion = (bf16[1024,1024]{1,0:T(8,128)(2,1)}, bf16[1024,1024]{1,0:T(8,128)(2,1)}) fusion(f32[8,128,1024]{2,1,0:T(8,128)S(1)} %get-tuple-element.19, f32[1024]{0:T(1024)S(1)} %select_multiply_fusion, f32[8,128,1024]{2,1,0:T(8,128)S(1)} %get-tuple-element.20), kind=kLoop, calls=%fused_computation.1 | loop fusion | flops 4194304 | bytes 12587008 | tf_op jit(solution)/shard_map/convert_element_type | solution.py:35
  20.8 10.2 %all-to-all-done = bf16[8,65,1024]{2,1,0:T(8,128)(2,1)S(1)} async-done(((bf16[8,65,1024]{2,1,0:T(8,128)(2,1)}), bf16[8,65,1024]{2,1,0:T(8,128)(2,1)S(1)}, u32[]{:S(2)}, u32[]{:S(2)}) %all-to-all-start) | async-done | bytes 1064992 | tf_op jit(solution)/shard_map/all_to_all | solution.py:243
  31.0 0.1 convert_element_type.101
  31.1 0.2 fusion.15
  31.3 0.1 iota_add_fusion
  31.4 0.2 add.151
  31.7 0.2 eq.82
  31.8 0.8 %fusion.10.left_hot = bf16[8,72,128]{2,1,0:T(8,128)(2,1)} fusion(s32[8,72]{1,0:T(8,128)S(1)} %eq.82), kind=kLoop, calls=%fused_computation.28 | loop fusion | flops 147456 | bytes 149760 | tf_op jit(solution)/shard_map/convert_element_type | solution.py:253
  32.7 0.1 add.155
  32.7 0.2 eq.86
  32.9 0.8 %fusion.11.right_hot = bf16[8,72,128]{2,1,0:T(8,128)(2,1)} fusion(s32[8,72]{1,0:T(8,128)S(1)} %eq.86), kind=kLoop, calls=%fused_computation.29 | loop fusion | flops 147456 | bytes 149760 | tf_op jit(solution)/shard_map/convert_element_type | solution.py:254
  33.7 0.1 slice.40
  33.8 1.4 %reshape.344.panel = bf16[128,4096]{1,0:T(8,128)(2,1)} reshape(bf16[8,64,1024]{2,1,0:T(8,128)(2,1)S(1)} %slice.40) | data formatting | bytes 2097152 | tf_op jit(solution)/shard_map/reshape | solution.py:246
  35.2 24.4 %shard_map.37 = bf16[8,72,1024]{2,1,0:T(8,128)(2,1)} custom-call(bf16[8,72,128]{2,1,0:T(8,128)(2,1)} %fusion.10.left_hot, bf16[8,72,128]{2,1,0:T(8,128)(2,1)} %fusion.11.right_hot, bf16[128,4096]{1,0:T(8,128)(2,1)} %reshape.344.panel, bf16[1024,1024]{1,0:T(8,128)(2,1)} %get-tuple-element.24.cos_ref, bf16[1024,1024]{1,0:T(8,128)(2,1)} %get-tuple-element.23.sin_ref), custom_call_target="tpu_custom_call" | custom-call | flops 3623878656 | bytes 6422528 | tf_op jit(solution)/shard_map/pallas_call | solution.py:138
  59.6 2.4 %reshape.345 = bf16[144,4096]{1,0:T(8,128)(2,1)S(1)} reshape(bf16[8,72,1024]{2,1,0:T(8,128)(2,1)} %shard_map.37) | data formatting | bytes 2359296 | tf_op jit(solution)/shard_map/reshape | solution.py:265
  62.0 0.3 convolution_convert_fusion
  62.3 1.1 %copy.42 = bf16[16,3,4,1024]{3,2,1,0:T(4,128)(2,1)} copy(bf16[16,3,4,1024]{3,0,2,1:T(8,128)(2,1)S(1)} %convolution_convert_fusion) | data formatting | bytes 786432
  63.4 13.4 %shard_map.38 = bf16[16,1,3,4,1024]{4,3,2,1,0:T(4,128)(2,1)} custom-call(bf16[16,1,3,4,1024]{4,3,2,1,0:T(4,128)(2,1)} %bitcast.38), custom_call_target="tpu_custom_call" | custom-call | tf_op jit(solution)/shard_map/pallas_call | solution.py:213
  76.8 2.0 %convert.1 = f32[1,1,48,4,1024]{4,3,2,1,0:T(4,128)} convert(bf16[1,1,48,4,1024]{4,3,2,1,0:T(4,128)(2,1)} %bitcast.39) | non-fusion elementwise | flops 196608 | bytes 1179648 | tf_op jit(solution)/shard_map/reshape | solution.py:269
  (11 shorter events, 0.1 us)
Async XLA Ops:
  2.1 1.2 %copy-start = (bf16[16,2,2,8192]{3,2,1,0:T(2,128)(2,1)S(1)}, bf16[16,2,2,8192]{3,2,1,0:T(2,128)(2,1)}, u32[]{:S(2)}) copy-start(bf16[16,2,2,8192]{3,2,1,0:T(2,128)(2,1)} %param.5) | copy-start | bytes 3145732
  4.6 1.5 %copy-start.1 = (s32[1,1,18,2]{2,3,1,0:T(2,128)S(1)}, s32[1,1,18,2]{2,3,1,0:T(2,128)}, u32[]{:S(2)}) copy-start(s32[1,1,18,2]{2,3,1,0:T(2,128)} %param.6) | copy-start | bytes 436
  7.5 9.2 %copy-start.2 = (s32[1,1,18,1]{2,3,1,0:T(1,128)S(1)}, s32[1,1,18,1]{2,3,1,0:T(1,128)}, u32[]{:S(2)}) copy-start(s32[1,1,18,1]{2,3,1,0:T(1,128)} %param.7) | copy-start | bytes 220
  7.5 23.4 %all-to-all-start = ((bf16[8,65,1024]{2,1,0:T(8,128)(2,1)}), bf16[8,65,1024]{2,1,0:T(8,128)(2,1)S(1)}, u32[]{:S(2)}, u32[]{:S(2)}) async-start(bf16[8,65,1024]{2,1,0:T(8,128)(2,1)} %pad_maximum_fusion), calls=%async_computation | async-start | bytes 2359296 | tf_op jit(solution)/shard_map/all_to_all | solution.py:243

commit v11 on v7

--- a/solution.py
+++ b/solution.py
@@ -14,6 +14,7 @@
 MOST = 3
 WINDOWS = 2
 FINE = 128
+EXTRA_ROWS = 16
 
 
 def phase_angle(bins, lag_index):
@@ -36,12 +37,35 @@
     return cos_part, sin_part
 
 
-def whiten(spectra):
-    values = spectra.astype(jnp.float32)
-    power = values[:, :, 0] ** 2 + values[:, :, 1] ** 2
+def whiten_kernel(x_ref, extra_ref, out_ref):
+    x = x_ref[...].astype(jnp.float32)
+    rows = x.shape[0]
+    square = x * x
+    after = pltpu.roll(square, rows - 1, 0)
+    before = pltpu.roll(square, 1, 0)
+    odd = lax.broadcasted_iota(jnp.int32, x.shape, 0) % 2 == 1
+    power = jnp.where(odd, before + square, square + after)
     level = jnp.mean(power, axis=-1, keepdims=True) + 1e-05
-    scale = lax.rsqrt(power + 0.1 * level)
-    return (values * scale[:, :, None, :]).astype(jnp.bfloat16)
+    white = (x * lax.rsqrt(power + 0.1 * level)).astype(out_ref.dtype)
+    part = out_ref.shape[2]
+    for chunk in range(out_ref.shape[0]):
+        out_ref[chunk, :rows, :] = white[:, chunk * part:(chunk + 1) * part]
+        out_ref[chunk, rows:, :] = extra_ref[...]
+
+
+def whiten_chunks(spectra, extra, chan_count):
+    channels = spectra.shape[0]
+    rows = channels * WINDOWS * 2
+    x = spectra.reshape(rows, F)
+    vmem = pl.BlockSpec(memory_space=pltpu.VMEM)
+    return pl.pallas_call(
+        whiten_kernel,
+        out_shape=jax.ShapeDtypeStruct((chan_count, rows + extra.shape[0], F // chan_count), jnp.bfloat16),
+        in_specs=[vmem, vmem],
+        out_specs=vmem,
+        compiler_params=pltpu.CompilerParams(vmem_limit_bytes=48 * 1024 * 1024),
+        cost_estimate=pl.CostEstimate(flops=8 * rows * F, transcendentals=rows * F, bytes_accessed=4 * rows * F),
+    )(x, extra)
 
 
 def pair_rows(left_hot, right_hot, panel, cos_ref, sin_ref, target):
@@ -232,14 +256,10 @@
     part = F // chan_count
     me = lax.axis_index("chan")
 
-    white = whiten(spectra)
-    channels = white.shape[0]
-    chunks = white.reshape(channels, WINDOWS, 2, chan_count, part).transpose(3, 0, 1, 2, 4)
-    chunks = chunks.reshape(chan_count, channels * WINDOWS * 2, part)
+    channels = spectra.shape[0]
     listed = pair_blocks[0, 0].reshape(-1).astype(jnp.bfloat16)
-    extra = jnp.zeros((part,), jnp.bfloat16).at[: listed.shape[0]].set(listed)
-    extra = jnp.broadcast_to(extra[None, None, :], (chan_count, 1, part))
-    sent = jnp.concatenate([chunks, extra], axis=1)
+    extra = jnp.zeros((EXTRA_ROWS, part), jnp.bfloat16).at[0, : listed.shape[0]].set(listed)
+    sent = whiten_chunks(spectra, extra, chan_count)
     got = lax.all_to_all(sent, "chan", split_axis=0, concat_axis=0, tiled=True)
     rows_per = channels * WINDOWS * 2
     group_channels = chan_count * channels

time: 78.8 us -> 77.9 us (0.989)
  other arithmetic: 17.5 us -> 14 us
  Pallas kernels: 37.8 us -> 40.5 us
  waiting for transfers between devices: 9.45 us -> 10.9 us
  local copies, waits for them, and re-layouts: 6.64 us -> 5.29 us
    pallas_call x0 -> x1, Pallas kernels: none -> 2.63 us  [whiten_chunks(): pl.pallas_call(whiten_kernel, out_shape=jax.ShapeDtypeStruct((chan_count,...]
    convert_element_type x2 -> x0, other arithmetic: 2.49 us -> none  [the longest x1 1.84 us: whiten(): values = spectra.astype(jnp.float32)]
    all_to_all x1, waiting for transfers between devices: 9.45 us -> 10.9 us  [local(): got = lax.all_to_all(sent, 'chan', split_axis=0, concat_axis=0, tiled=True)]
    unnamed x7 -> x2, local copies, waits for them, and re-layouts: 1.32 us -> 0.01 us
    concatenate x1 -> x0, other arithmetic: 1.14 us -> none  [local(): sent = jnp.concatenate([chunks, extra], axis=1)]
    transpose x1 -> x0, local copies, waits for them, and re-layouts: 1.08 us -> none  [local(): white.reshape(channels, WINDOWS, 2, chan_count, part)]
    reshape x1, local copies, waits for them, and re-layouts: 0.44 us -> 1.48 us  [whiten_chunks(): x = spectra.reshape(rows, F)]
where the time goes in v11:
time: 77.9 us; the launch traced here: 77.6 us
  Pallas kernels  40.5 us (52%)
  other arithmetic  14 us (18%)
  waiting for transfers between devices  10.9 us (14%)
  starting transfers between devices  6.81 us (9%)
  local copies, waits for them, and re-layouts  5.29 us (7%)
    pallas_call x1, Pallas kernels, pair_exchange(): pl.pallas_call(pair_exchange_kernel, out_shape=jax.ShapeDtypeStruct((chan...  24.4 us
    pallas_call x1, Pallas kernels, exchange(): pl.pallas_call(functools.partial(exchange_kernel, axis, other_axis, axis_...  13.4 us
    all_to_all x1, waiting for transfers between devices, local(): got = lax.all_to_all(sent, 'chan', split_axis=0, concat_axis=0, tiled=True)  10.9 us
    all_to_all x1, starting transfers between devices, local(): got = lax.all_to_all(sent, 'chan', split_axis=0, concat_axis=0, tiled=True)  6.81 us
    pallas_call x1, Pallas kernels, whiten_chunks(): pl.pallas_call(whiten_kernel, out_shape=jax.ShapeDtypeStruct((chan_count,...  2.63 us
    convert_element_type x1, other arithmetic, table_slice(): sin_part = (-sin_ab * weight).astype(jnp.bfloat16)  2.45 us
    cos x1, other arithmetic, table_slice(): cos_b, sin_b = (jnp.cos(fine)[None, :, :], jnp.sin(fine)[None, :, :])  2.04 us
    reshape x1, other arithmetic, local(): return received.reshape(1, 1, slot_count, pairs, LAGS)  1.98 us
  transfers between devices with their start and end apart: 1, of which 1 were waited for; matrix products, arithmetic and copies ran while one was open for 9% of the time, Pallas kernels for 0%

profile of v11, /device:TPU:1, one launch (start us, length us, event | category | flops | bytes accessed | tf_op | source)
XLA Modules:
  0.0 77.6 jit_solution(1434941103637625837)
XLA Ops:
  0.0 0.0 copy-start
  0.0 1.5 %reshape.336.x_ref = bf16[64,8192]{1,0:T(8,128)(2,1)S(1)} reshape(bf16[16,2,2,8192]{3,2,1,0:T(2,128)(2,1)} %param.5) | data formatting | bytes 2097152 | tf_op jit(solution)/shard_map/reshape | solution.py:59
  1.5 0.7 convert_element_type.86
  2.2 0.1 copy.6
  2.3 0.1 convert_element_type.87
  2.4 2.6 %shard_map.37 = bf16[8,80,1024]{2,1,0:T(8,128)(2,1)} custom-call(bf16[64,8192]{1,0:T(8,128)(2,1)S(1)} %reshape.336.x_ref, bf16[16,1024]{1,0:T(8,128)(2,1)S(1)} %scatter.4.extra_ref), custom_call_target="tpu_custom_call" | custom-call | flops 4194304 | bytes 2097152 | tf_op jit(solution)/shard_map/pallas_call | solution.py:61
  5.0 6.8 %all-to-all-start = ((bf16[8,80,1024]{2,1,0:T(8,128)(2,1)}), bf16[8,80,1024]{2,1,0:T(8,128)(2,1)S(1)}, u32[]{:S(2)}, u32[]{:S(2)}) async-start(bf16[8,80,1024]{2,1,0:T(8,128)(2,1)} %shard_map.37), calls=%async_computation | async-start | bytes 2621440 | tf_op jit(solution)/shard_map/all_to_all | solution.py:263
  11.8 0.0 copy-done
  11.8 0.2 convert_reduce_fusion.1
  12.0 0.6 iota_reduce_fusion
  12.7 0.1 fusion.19
  12.8 2.0 %fusion.11 = (f32[128,1024]{1,0:T(8,128)S(1)}, f32[128,1024]{1,0:T(8,128)S(1)}) fusion(s32[1024]{0:T(1024)S(1)} %iota_add_fusion.2), kind=kLoop, calls=%fused_computation.23 | loop fusion | flops 1835008 | bytes 1052672 | tf_op jit(solution)/shard_map/cos | solution.py:30
  14.8 0.2 fusion.18
  15.0 0.1 broadcast_in_dim.58
  15.1 0.1 broadcast_in_dim.32
  15.2 1.2 %add_negate_fusion = (f32[8,128,1024]{2,1,0:T(8,128)S(1)}, f32[8,128,1024]{2,1,0:T(8,128)S(1)}) fusion(f32[128,1024]{1,0:T(8,128)S(1)} %get-tuple-element.28, f32[8,1024]{1,0:T(8,128)S(1)} %get-tuple-element.24, f32[128,1024]{1,0:T(8,128)S(1)} %get-tuple-element.27, f32[8,1024]{1,0:T(8,128)S(1)} %get-tuple-element.23), kind=kLoop, calls=%fused_computation.5 | loop fusion | flops 7340032 | bytes 9502720 | tf_op jit(solution)/shard_map/neg | solution.py:36
  16.4 2.4 %fusion = (bf16[1024,1024]{1,0:T(8,128)(2,1)}, bf16[1024,1024]{1,0:T(8,128)(2,1)}) fusion(f32[8,128,1024]{2,1,0:T(8,128)S(1)} %get-tuple-element.21, f32[1024]{0:T(1024)S(1)} %select_multiply_fusion, f32[8,128,1024]{2,1,0:T(8,128)S(1)} %get-tuple-element.22), kind=kLoop, calls=%fused_computation.2 | loop fusion | flops 4194304 | bytes 12587008 | tf_op jit(solution)/shard_map/convert_element_type | solution.py:36
  18.9 10.9 %all-to-all-done = bf16[8,80,1024]{2,1,0:T(8,128)(2,1)S(1)} async-done(((bf16[8,80,1024]{2,1,0:T(8,128)(2,1)}), bf16[8,80,1024]{2,1,0:T(8,128)(2,1)S(1)}, u32[]{:S(2)}, u32[]{:S(2)}) %all-to-all-start) | async-done | bytes 1310752 | tf_op jit(solution)/shard_map/all_to_all | solution.py:263
  29.8 0.1 convert_element_type.90
  29.9 0.2 fusion.12
  30.1 0.1 iota_add_fusion
  30.2 0.2 add.131
  30.4 0.2 eq.80
  30.6 0.8 %fusion.8.left_hot = bf16[8,72,128]{2,1,0:T(8,128)(2,1)} fusion(s32[8,72]{1,0:T(8,128)S(1)} %eq.80), kind=kLoop, calls=%fused_computation.20 | loop fusion | flops 147456 | bytes 149760 | tf_op jit(solution)/shard_map/convert_element_type | solution.py:273
  31.4 0.1 add.135
  31.5 0.2 eq.84
  31.6 0.8 %fusion.9.right_hot = bf16[8,72,128]{2,1,0:T(8,128)(2,1)} fusion(s32[8,72]{1,0:T(8,128)S(1)} %eq.84), kind=kLoop, calls=%fused_computation.21 | loop fusion | flops 147456 | bytes 149760 | tf_op jit(solution)/shard_map/convert_element_type | solution.py:274
  32.5 0.1 slice.37
  32.6 1.4 %reshape.337.panel = bf16[128,4096]{1,0:T(8,128)(2,1)} reshape(bf16[8,64,1024]{2,1,0:T(8,128)(2,1)S(1)} %slice.37) | data formatting | bytes 2097152 | tf_op jit(solution)/shard_map/reshape | solution.py:266
  34.0 24.4 %shard_map.38 = bf16[8,72,1024]{2,1,0:T(8,128)(2,1)} custom-call(bf16[8,72,128]{2,1,0:T(8,128)(2,1)} %fusion.8.left_hot, bf16[8,72,128]{2,1,0:T(8,128)(2,1)} %fusion.9.right_hot, bf16[128,4096]{1,0:T(8,128)(2,1)} %reshape.337.panel, bf16[1024,1024]{1,0:T(8,128)(2,1)} %get-tuple-element.26.cos_ref, bf16[1024,1024]{1,0:T(8,128)(2,1)} %get-tuple-element.25.sin_ref), custom_call_target="tpu_custom_call" | custom-call | flops 3623878656 | bytes 6422528 | tf_op jit(solution)/shard_map/pallas_call | solution.py:162
  58.4 1.5 %convert_reduce_fusion = bf16[72,1024]{1,0:T(8,128)(2,1)S(1)} fusion(bf16[8,72,1024]{2,1,0:T(8,128)(2,1)} %shard_map.38), kind=kLoop, calls=%fused_computation.7 | loop fusion | flops 1105920 | bytes 1327104 | tf_op jit(solution)/shard_map/reduce_sum | solution.py:278
  59.9 0.1 reshape.338
  60.0 0.8 %gather_fusion = bf16[48,4096]{1,0:T(8,128)(2,1)S(1)} fusion(bf16[18,4096]{1,0:T(8,128)(2,1)S(1)} %reshape.338, s32[1024]{0:T(1024)S(1)} %pad_clamp_fusion), kind=kCustom, calls=%fused_computation | custom fusion | bytes 786624 | tf_op jit(solution)/shard_map/jit(_take)/gather | solution.py:288
  60.8 0.3 gather.7
  61.1 1.1 %select_convert_fusion.x_ref = bf16[16,1,3,4,1024]{4,3,2,1,0:T(4,128)(2,1)} fusion(bf16[16,1,3,4,1024]{4,3,2,1,0:T(4,128)(2,1)S(1)} %gather.7, pred[16,3]{1,0:T(8,128)(4,1)S(1)} %broadcast_in_dim.58, pred[16,3]{1,0:T(8,128)(4,1)S(1)} %broadcast_in_dim.32), kind=kLoop, calls=%fused_computation.8 | loop fusion | flops 393216 | bytes 786528 | tf_op jit(solution)/shard_map/convert_element_type | solution.py:289
  62.2 13.4 %shard_map.39 = bf16[16,1,3,4,1024]{4,3,2,1,0:T(4,128)(2,1)} custom-call(bf16[16,1,3,4,1024]{4,3,2,1,0:T(4,128)(2,1)} %select_convert_fusion.x_ref), custom_call_target="tpu_custom_call" | custom-call | tf_op jit(solution)/shard_map/pallas_call | solution.py:237
  75.6 2.0 %convert.1 = f32[1,1,48,4,1024]{4,3,2,1,0:T(4,128)} convert(bf16[1,1,48,4,1024]{4,3,2,1,0:T(4,128)(2,1)} %bitcast.12) | non-fusion elementwise | flops 196608 | bytes 1179648 | tf_op jit(solution)/shard_map/reshape | solution.py:291
  (9 shorter events, 0.1 us)
Async XLA Ops:
  0.0 11.8 %copy-start = (s32[1,1,18,1]{2,3,1,0:T(1,128)S(1)}, s32[1,1,18,1]{2,3,1,0:T(1,128)}, u32[]{:S(2)}) copy-start(s32[1,1,18,1]{2,3,1,0:T(1,128)} %param.7) | copy-start | bytes 220
  5.0 24.7 %all-to-all-start = ((bf16[8,80,1024]{2,1,0:T(8,128)(2,1)}), bf16[8,80,1024]{2,1,0:T(8,128)(2,1)S(1)}, u32[]{:S(2)}, u32[]{:S(2)}) async-start(bf16[8,80,1024]{2,1,0:T(8,128)(2,1)} %shard_map.37), calls=%async_computation | async-start | bytes 2621440 | tf_op jit(solution)/shard_map/all_to_all | solution.py:263

commit v12 on v11

--- a/solution.py
+++ b/solution.py
@@ -14,7 +14,7 @@
 MOST = 3
 WINDOWS = 2
 FINE = 128
-EXTRA_ROWS = 16
+EXTRA_ROWS = 1
 
 
 def phase_angle(bins, lag_index):

time: 77.9 us -> 77.7 us (level)
  waiting for transfers between devices: 10.9 us -> 9.45 us
  other arithmetic: 14 us -> 15.3 us
    another operation x0 -> x2, other arithmetic: none -> 1.97 us
    all_to_all x1, waiting for transfers between devices: 10.9 us -> 9.45 us  [local(): got = lax.all_to_all(sent, 'chan', split_axis=0, concat_axis=0, tiled=True)]
where the time goes in v12:
time: 77.7 us; the launch traced here: 77.4 us
  Pallas kernels  40.4 us (52%)
  other arithmetic  15.3 us (20%)
  waiting for transfers between devices  9.45 us (12%)
  starting transfers between devices  6.81 us (9%)
  local copies, waits for them, and re-layouts  5.26 us (7%)
    pallas_call x1, Pallas kernels, pair_exchange(): pl.pallas_call(pair_exchange_kernel, out_shape=jax.ShapeDtypeStruct((chan...  24.4 us
    pallas_call x1, Pallas kernels, exchange(): pl.pallas_call(functools.partial(exchange_kernel, axis, other_axis, axis_...  13.4 us
    all_to_all x1, waiting for transfers between devices, local(): got = lax.all_to_all(sent, 'chan', split_axis=0, concat_axis=0, tiled=True)  9.45 us
    all_to_all x1, starting transfers between devices, local(): got = lax.all_to_all(sent, 'chan', split_axis=0, concat_axis=0, tiled=True)  6.81 us
    pallas_call x1, Pallas kernels, whiten_chunks(): pl.pallas_call(whiten_kernel, out_shape=jax.ShapeDtypeStruct((chan_count,...  2.57 us
    convert_element_type x1, other arithmetic, table_slice(): sin_part = (-sin_ab * weight).astype(jnp.bfloat16)  2.45 us
    cos x1, other arithmetic, table_slice(): cos_b, sin_b = (jnp.cos(fine)[None, :, :], jnp.sin(fine)[None, :, :])  2.04 us
    reshape x1, other arithmetic, local(): return received.reshape(1, 1, slot_count, pairs, LAGS)  1.98 us
  transfers between devices with their start and end apart: 1, of which 1 were waited for; matrix products, arithmetic and copies ran while one was open for 9% of the time, Pallas kernels for 0%

profile of v12, /device:TPU:1, one launch (start us, length us, event | category | flops | bytes accessed | tf_op | source)
XLA Modules:
  0.0 77.4 jit_solution(6505704984996518033)
XLA Ops:
  0.0 0.0 copy-start
  0.0 0.6 compare_reduce_fusion
  0.6 1.5 %reshape.343.x_ref = bf16[64,8192]{1,0:T(8,128)(2,1)S(1)} reshape(bf16[16,2,2,8192]{3,2,1,0:T(2,128)(2,1)} %param.5) | data formatting | bytes 2097152 | tf_op jit(solution)/shard_map/reshape | solution.py:59
  2.1 1.3 %broadcast_select_fusion = bf16[1,1,18,2]{2,3,1,0:T(2,128)(2,1)S(1)} fusion(pred[]{:T(512)} %compare_reduce_fusion, s32[1,1,18,2]{2,3,1,0:T(2,128)} %param.6), kind=kLoop, calls=%fused_computation.56 | loop fusion | flops 72 | bytes 217 | tf_op jit(solution)/shard_map/select.32
  3.4 0.1 copy.6
  3.6 0.1 reshape.344
  3.7 2.6 %shard_map.37 = bf16[8,65,1024]{2,1,0:T(8,128)(2,1)} custom-call(bf16[64,8192]{1,0:T(8,128)(2,1)S(1)} %reshape.343.x_ref, bf16[1,1024]{1,0:T(2,128)(2,1)S(1)} %scatter.4.extra_ref), custom_call_target="tpu_custom_call" | custom-call | flops 4194304 | bytes 2097152 | tf_op jit(solution)/shard_map/pallas_call | solution.py:61
  6.2 6.8 %all-to-all-start = ((bf16[8,65,1024]{2,1,0:T(8,128)(2,1)}), bf16[8,65,1024]{2,1,0:T(8,128)(2,1)S(1)}, u32[]{:S(2)}, u32[]{:S(2)}) async-start(bf16[8,65,1024]{2,1,0:T(8,128)(2,1)} %shard_map.37), calls=%async_computation | async-start | bytes 2359296 | tf_op jit(solution)/shard_map/all_to_all | solution.py:263
  13.1 0.0 copy-done
  13.1 0.2 convert_reduce_fusion.1
  13.3 0.6 iota_reduce_fusion
  13.9 0.1 fusion.19
  14.0 2.0 %fusion.11 = (f32[128,1024]{1,0:T(8,128)S(1)}, f32[128,1024]{1,0:T(8,128)S(1)}) fusion(s32[1024]{0:T(1024)S(1)} %iota_add_fusion.2), kind=kLoop, calls=%fused_computation.23 | loop fusion | flops 1835008 | bytes 1052672 | tf_op jit(solution)/shard_map/cos | solution.py:30
  16.0 0.2 fusion.18
  16.3 0.1 broadcast_in_dim.58
  16.4 0.1 broadcast_in_dim.32
  16.5 1.2 %add_negate_fusion = (f32[8,128,1024]{2,1,0:T(8,128)S(1)}, f32[8,128,1024]{2,1,0:T(8,128)S(1)}) fusion(f32[128,1024]{1,0:T(8,128)S(1)} %get-tuple-element.28, f32[8,1024]{1,0:T(8,128)S(1)} %get-tuple-element.24, f32[128,1024]{1,0:T(8,128)S(1)} %get-tuple-element.27, f32[8,1024]{1,0:T(8,128)S(1)} %get-tuple-element.23), kind=kLoop, calls=%fused_computation.5 | loop fusion | flops 7340032 | bytes 9502720 | tf_op jit(solution)/shard_map/neg | solution.py:36
  17.7 2.4 %fusion = (bf16[1024,1024]{1,0:T(8,128)(2,1)}, bf16[1024,1024]{1,0:T(8,128)(2,1)}) fusion(f32[8,128,1024]{2,1,0:T(8,128)S(1)} %get-tuple-element.21, f32[1024]{0:T(1024)S(1)} %select_multiply_fusion, f32[8,128,1024]{2,1,0:T(8,128)S(1)} %get-tuple-element.22), kind=kLoop, calls=%fused_computation.2 | loop fusion | flops 4194304 | bytes 12587008 | tf_op jit(solution)/shard_map/convert_element_type | solution.py:36
  20.1 9.5 %all-to-all-done = bf16[8,65,1024]{2,1,0:T(8,128)(2,1)S(1)} async-done(((bf16[8,65,1024]{2,1,0:T(8,128)(2,1)}), bf16[8,65,1024]{2,1,0:T(8,128)(2,1)S(1)}, u32[]{:S(2)}, u32[]{:S(2)}) %all-to-all-start) | async-done | bytes 1064992 | tf_op jit(solution)/shard_map/all_to_all | solution.py:263
  29.6 0.1 convert_element_type.87
  29.7 0.2 fusion.12
  29.9 0.1 iota_add_fusion
  30.0 0.2 add.131
  30.2 0.2 eq.80
  30.4 0.8 %fusion.8.left_hot = bf16[8,72,128]{2,1,0:T(8,128)(2,1)} fusion(s32[8,72]{1,0:T(8,128)S(1)} %eq.80), kind=kLoop, calls=%fused_computation.20 | loop fusion | flops 147456 | bytes 149760 | tf_op jit(solution)/shard_map/convert_element_type | solution.py:273
  31.2 0.1 add.135
  31.3 0.2 eq.84
  31.4 0.8 %fusion.9.right_hot = bf16[8,72,128]{2,1,0:T(8,128)(2,1)} fusion(s32[8,72]{1,0:T(8,128)S(1)} %eq.84), kind=kLoop, calls=%fused_computation.21 | loop fusion | flops 147456 | bytes 149760 | tf_op jit(solution)/shard_map/convert_element_type | solution.py:274
  32.3 0.1 slice.37
  32.4 1.4 %reshape.345.panel = bf16[128,4096]{1,0:T(8,128)(2,1)} reshape(bf16[8,64,1024]{2,1,0:T(8,128)(2,1)S(1)} %slice.37) | data formatting | bytes 2097152 | tf_op jit(solution)/shard_map/reshape | solution.py:266
  33.8 24.4 %shard_map.38 = bf16[8,72,1024]{2,1,0:T(8,128)(2,1)} custom-call(bf16[8,72,128]{2,1,0:T(8,128)(2,1)} %fusion.8.left_hot, bf16[8,72,128]{2,1,0:T(8,128)(2,1)} %fusion.9.right_hot, bf16[128,4096]{1,0:T(8,128)(2,1)} %reshape.345.panel, bf16[1024,1024]{1,0:T(8,128)(2,1)} %get-tuple-element.26.cos_ref, bf16[1024,1024]{1,0:T(8,128)(2,1)} %get-tuple-element.25.sin_ref), custom_call_target="tpu_custom_call" | custom-call | flops 3623878656 | bytes 6422528 | tf_op jit(solution)/shard_map/pallas_call | solution.py:162
  58.2 1.5 %convert_reduce_fusion = bf16[72,1024]{1,0:T(8,128)(2,1)S(1)} fusion(bf16[8,72,1024]{2,1,0:T(8,128)(2,1)} %shard_map.38), kind=kLoop, calls=%fused_computation.7 | loop fusion | flops 1105920 | bytes 1327104 | tf_op jit(solution)/shard_map/reduce_sum | solution.py:278
  59.7 0.1 reshape.346
  59.8 0.8 %gather_fusion = bf16[48,4096]{1,0:T(8,128)(2,1)S(1)} fusion(bf16[18,4096]{1,0:T(8,128)(2,1)S(1)} %reshape.346, s32[1024]{0:T(1024)S(1)} %pad_clamp_fusion), kind=kCustom, calls=%fused_computation | custom fusion | bytes 786624 | tf_op jit(solution)/shard_map/jit(_take)/gather | solution.py:288
  60.6 0.3 gather.7
  60.9 1.1 %select_convert_fusion.x_ref = bf16[16,1,3,4,1024]{4,3,2,1,0:T(4,128)(2,1)} fusion(bf16[16,1,3,4,1024]{4,3,2,1,0:T(4,128)(2,1)S(1)} %gather.7, pred[16,3]{1,0:T(8,128)(4,1)S(1)} %broadcast_in_dim.58, pred[16,3]{1,0:T(8,128)(4,1)S(1)} %broadcast_in_dim.32), kind=kLoop, calls=%fused_computation.8 | loop fusion | flops 393216 | bytes 786528 | tf_op jit(solution)/shard_map/convert_element_type | solution.py:289
  62.0 13.4 %shard_map.39 = bf16[16,1,3,4,1024]{4,3,2,1,0:T(4,128)(2,1)} custom-call(bf16[16,1,3,4,1024]{4,3,2,1,0:T(4,128)(2,1)} %select_convert_fusion.x_ref), custom_call_target="tpu_custom_call" | custom-call | tf_op jit(solution)/shard_map/pallas_call | solution.py:237
  75.4 2.0 %convert.1 = f32[1,1,48,4,1024]{4,3,2,1,0:T(4,128)} convert(bf16[1,1,48,4,1024]{4,3,2,1,0:T(4,128)(2,1)} %bitcast.12) | non-fusion elementwise | flops 196608 | bytes 1179648 | tf_op jit(solution)/shard_map/reshape | solution.py:291
  (9 shorter events, 0.1 us)
Async XLA Ops:
  0.0 13.1 %copy-start = (s32[1,1,18,1]{2,3,1,0:T(1,128)S(1)}, s32[1,1,18,1]{2,3,1,0:T(1,128)}, u32[]{:S(2)}) copy-start(s32[1,1,18,1]{2,3,1,0:T(1,128)} %param.7) | copy-start | bytes 220
  6.2 23.3 %all-to-all-start = ((bf16[8,65,1024]{2,1,0:T(8,128)(2,1)}), bf16[8,65,1024]{2,1,0:T(8,128)(2,1)S(1)}, u32[]{:S(2)}, u32[]{:S(2)}) async-start(bf16[8,65,1024]{2,1,0:T(8,128)(2,1)} %shard_map.37), calls=%async_computation | async-start | bytes 2359296 | tf_op jit(solution)/shard_map/all_to_all | solution.py:263

commit v13 on v12

--- a/solution.py
+++ b/solution.py
@@ -14,7 +14,6 @@
 MOST = 3
 WINDOWS = 2
 FINE = 128
-EXTRA_ROWS = 1
 
 
 def phase_angle(bins, lag_index):
@@ -37,7 +36,7 @@
     return cos_part, sin_part
 
 
-def whiten_kernel(x_ref, extra_ref, out_ref):
+def whiten_kernel(x_ref, blocks_ref, out_ref):
     x = x_ref[...].astype(jnp.float32)
     rows = x.shape[0]
     square = x * x
@@ -48,24 +47,31 @@
     level = jnp.mean(power, axis=-1, keepdims=True) + 1e-05
     white = (x * lax.rsqrt(power + 0.1 * level)).astype(out_ref.dtype)
     part = out_ref.shape[2]
+    lane = lax.broadcasted_iota(jnp.int32, (1, part), 1)
+    extra = jnp.zeros((1, part), jnp.float32)
+    for pair in range(blocks_ref.shape[2]):
+        for side in range(2):
+            value = blocks_ref[0, 0, pair, side].astype(jnp.float32)
+            extra = jnp.where(lane == pair * 2 + side, value, extra)
+    extra = extra.astype(out_ref.dtype)
     for chunk in range(out_ref.shape[0]):
         out_ref[chunk, :rows, :] = white[:, chunk * part:(chunk + 1) * part]
-        out_ref[chunk, rows:, :] = extra_ref[...]
-
-
-def whiten_chunks(spectra, extra, chan_count):
+        out_ref[chunk, rows:, :] = extra
+
+
+def whiten_chunks(spectra, pair_blocks, chan_count):
     channels = spectra.shape[0]
     rows = channels * WINDOWS * 2
     x = spectra.reshape(rows, F)
     vmem = pl.BlockSpec(memory_space=pltpu.VMEM)
     return pl.pallas_call(
         whiten_kernel,
-        out_shape=jax.ShapeDtypeStruct((chan_count, rows + extra.shape[0], F // chan_count), jnp.bfloat16),
-        in_specs=[vmem, vmem],
+        out_shape=jax.ShapeDtypeStruct((chan_count, rows + 1, F // chan_count), jnp.bfloat16),
+        in_specs=[vmem, pl.BlockSpec(memory_space=pltpu.SMEM)],
         out_specs=vmem,
         compiler_params=pltpu.CompilerParams(vmem_limit_bytes=48 * 1024 * 1024),
         cost_estimate=pl.CostEstimate(flops=8 * rows * F, transcendentals=rows * F, bytes_accessed=4 * rows * F),
-    )(x, extra)
+    )(x, pair_blocks)
 
 
 def pair_rows(left_hot, right_hot, panel, cos_ref, sin_ref, target):
@@ -257,9 +263,7 @@
     me = lax.axis_index("chan")
 
     channels = spectra.shape[0]
-    listed = pair_blocks[0, 0].reshape(-1).astype(jnp.bfloat16)
-    extra = jnp.zeros((EXTRA_ROWS, part), jnp.bfloat16).at[0, : listed.shape[0]].set(listed)
-    sent = whiten_chunks(spectra, extra, chan_count)
+    sent = whiten_chunks(spectra, pair_blocks, chan_count)
     got = lax.all_to_all(sent, "chan", split_axis=0, concat_axis=0, tiled=True)
     rows_per = channels * WINDOWS * 2
     group_channels = chan_count * channels

time: 77.7 us -> 77 us (level)
  other arithmetic: 15.3 us -> 13.3 us
    another operation x2 -> x0, other arithmetic: 1.97 us -> none
where the time goes in v13:
time: 77 us; the launch traced here: 76.7 us
  Pallas kernels  41.1 us (53%)
  other arithmetic  13.3 us (17%)
  waiting for transfers between devices  9.45 us (12%)
  starting transfers between devices  6.81 us (9%)
  local copies, waits for them, and re-layouts  5.83 us (8%)
    pallas_call x1, Pallas kernels, pair_exchange(): pl.pallas_call(pair_exchange_kernel, out_shape=jax.ShapeDtypeStruct((chan...  24.4 us
    pallas_call x1, Pallas kernels, exchange(): pl.pallas_call(functools.partial(exchange_kernel, axis, other_axis, axis_...  13.4 us
    all_to_all x1, waiting for transfers between devices, local(): got = lax.all_to_all(sent, 'chan', split_axis=0, concat_axis=0, tiled=True)  9.45 us
    all_to_all x1, starting transfers between devices, local(): got = lax.all_to_all(sent, 'chan', split_axis=0, concat_axis=0, tiled=True)  6.81 us
    pallas_call x1, Pallas kernels, whiten_chunks(): pl.pallas_call(whiten_kernel, out_shape=jax.ShapeDtypeStruct((chan_count,...  3.31 us
    convert_element_type x1, other arithmetic, table_slice(): sin_part = (-sin_ab * weight).astype(jnp.bfloat16)  2.45 us
    cos x1, other arithmetic, table_slice(): cos_b, sin_b = (jnp.cos(fine)[None, :, :], jnp.sin(fine)[None, :, :])  2.04 us
    reshape x1, other arithmetic, local(): return received.reshape(1, 1, slot_count, pairs, LAGS)  1.98 us
  transfers between devices with their start and end apart: 1, of which 1 were waited for; matrix products, arithmetic and copies ran while one was open for 9% of the time, Pallas kernels for 0%

profile of v13, /device:TPU:1, one launch (start us, length us, event | category | flops | bytes accessed | tf_op | source)
XLA Modules:
  0.0 76.7 jit_solution(9237753216298743734)
XLA Ops:
  0.0 0.0 copy-start
  0.0 1.5 %reshape.300.x_ref = bf16[64,8192]{1,0:T(8,128)(2,1)S(1)} reshape(bf16[16,2,2,8192]{3,2,1,0:T(2,128)(2,1)} %param.3) | data formatting | bytes 2097152 | tf_op jit(solution)/shard_map/reshape | solution.py:65
  1.5 0.8 %copy.6.blocks_ref = s32[1,1,18,2]{3,2,1,0:T(8,128)S(1)} copy(s32[1,1,18,2]{2,3,1,0:T(2,128)} %param.4) | data formatting | bytes 288 | tf_op args[1]
  2.3 3.3 %shard_map.37 = bf16[8,65,1024]{2,1,0:T(8,128)(2,1)} custom-call(bf16[64,8192]{1,0:T(8,128)(2,1)S(1)} %reshape.300.x_ref, s32[1,1,18,2]{3,2,1,0:T(8,128)S(1)} %copy.6.blocks_ref), custom_call_target="tpu_custom_call" | custom-call | flops 4194304 | bytes 2097152 | tf_op jit(solution)/shard_map/pallas_call | solution.py:67
  5.6 6.8 %all-to-all-start = ((bf16[8,65,1024]{2,1,0:T(8,128)(2,1)}), bf16[8,65,1024]{2,1,0:T(8,128)(2,1)S(1)}, u32[]{:S(2)}, u32[]{:S(2)}) async-start(bf16[8,65,1024]{2,1,0:T(8,128)(2,1)} %shard_map.37), calls=%async_computation | async-start | bytes 2359296 | tf_op jit(solution)/shard_map/all_to_all | solution.py:267
  12.4 0.0 copy-done
  12.4 0.2 convert_reduce_fusion.1
  12.6 0.6 iota_reduce_fusion
  13.2 0.1 fusion.19
  13.3 2.0 %fusion.11 = (f32[128,1024]{1,0:T(8,128)S(1)}, f32[128,1024]{1,0:T(8,128)S(1)}) fusion(s32[1024]{0:T(1024)S(1)} %iota_add_fusion.2), kind=kLoop, calls=%fused_computation.23 | loop fusion | flops 1835008 | bytes 1052672 | tf_op jit(solution)/shard_map/cos | solution.py:29
  15.4 0.2 fusion.18
  15.6 0.1 broadcast_in_dim.57
  15.7 0.1 broadcast_in_dim.32
  15.8 1.2 %add_negate_fusion = (f32[8,128,1024]{2,1,0:T(8,128)S(1)}, f32[8,128,1024]{2,1,0:T(8,128)S(1)}) fusion(f32[128,1024]{1,0:T(8,128)S(1)} %get-tuple-element.16, f32[8,1024]{1,0:T(8,128)S(1)} %get-tuple-element.12, f32[128,1024]{1,0:T(8,128)S(1)} %get-tuple-element.15, f32[8,1024]{1,0:T(8,128)S(1)} %get-tuple-element.11), kind=kLoop, calls=%fused_computation.5 | loop fusion | flops 7340032 | bytes 9502720 | tf_op jit(solution)/shard_map/neg | solution.py:35
  17.0 2.4 %fusion = (bf16[1024,1024]{1,0:T(8,128)(2,1)}, bf16[1024,1024]{1,0:T(8,128)(2,1)}) fusion(f32[8,128,1024]{2,1,0:T(8,128)S(1)} %get-tuple-element.9, f32[1024]{0:T(1024)S(1)} %select_multiply_fusion, f32[8,128,1024]{2,1,0:T(8,128)S(1)} %get-tuple-element.10), kind=kLoop, calls=%fused_computation.2 | loop fusion | flops 4194304 | bytes 12587008 | tf_op jit(solution)/shard_map/convert_element_type | solution.py:35
  19.4 9.5 %all-to-all-done = bf16[8,65,1024]{2,1,0:T(8,128)(2,1)S(1)} async-done(((bf16[8,65,1024]{2,1,0:T(8,128)(2,1)}), bf16[8,65,1024]{2,1,0:T(8,128)(2,1)S(1)}, u32[]{:S(2)}, u32[]{:S(2)}) %all-to-all-start) | async-done | bytes 1064992 | tf_op jit(solution)/shard_map/all_to_all | solution.py:267
  28.9 0.1 convert_element_type.77
  29.0 0.2 fusion.12
  29.2 0.1 iota_add_fusion
  29.4 0.2 add.127
  29.6 0.2 eq.80
  29.7 0.8 %fusion.8.left_hot = bf16[8,72,128]{2,1,0:T(8,128)(2,1)} fusion(s32[8,72]{1,0:T(8,128)S(1)} %eq.80), kind=kLoop, calls=%fused_computation.20 | loop fusion | flops 147456 | bytes 149760 | tf_op jit(solution)/shard_map/convert_element_type | solution.py:277
  30.6 0.1 add.131
  30.6 0.2 eq.84
  30.8 0.8 %fusion.9.right_hot = bf16[8,72,128]{2,1,0:T(8,128)(2,1)} fusion(s32[8,72]{1,0:T(8,128)S(1)} %eq.84), kind=kLoop, calls=%fused_computation.21 | loop fusion | flops 147456 | bytes 149760 | tf_op jit(solution)/shard_map/convert_element_type | solution.py:278
  31.6 0.1 slice.21
  31.7 1.4 %reshape.301.panel = bf16[128,4096]{1,0:T(8,128)(2,1)} reshape(bf16[8,64,1024]{2,1,0:T(8,128)(2,1)S(1)} %slice.21) | data formatting | bytes 2097152 | tf_op jit(solution)/shard_map/reshape | solution.py:270
  33.1 24.4 %shard_map.38 = bf16[8,72,1024]{2,1,0:T(8,128)(2,1)} custom-call(bf16[8,72,128]{2,1,0:T(8,128)(2,1)} %fusion.8.left_hot, bf16[8,72,128]{2,1,0:T(8,128)(2,1)} %fusion.9.right_hot, bf16[128,4096]{1,0:T(8,128)(2,1)} %reshape.301.panel, bf16[1024,1024]{1,0:T(8,128)(2,1)} %get-tuple-element.14.cos_ref, bf16[1024,1024]{1,0:T(8,128)(2,1)} %get-tuple-element.13.sin_ref), custom_call_target="tpu_custom_call" | custom-call | flops 3623878656 | bytes 6422528 | tf_op jit(solution)/shard_map/pallas_call | solution.py:168
  57.5 1.5 %convert_reduce_fusion = bf16[72,1024]{1,0:T(8,128)(2,1)S(1)} fusion(bf16[8,72,1024]{2,1,0:T(8,128)(2,1)} %shard_map.38), kind=kLoop, calls=%fused_computation.7 | loop fusion | flops 1105920 | bytes 1327104 | tf_op jit(solution)/shard_map/reduce_sum | solution.py:282
  59.0 0.1 reshape.302
  59.1 0.8 %gather_fusion = bf16[48,4096]{1,0:T(8,128)(2,1)S(1)} fusion(bf16[18,4096]{1,0:T(8,128)(2,1)S(1)} %reshape.302, s32[1024]{0:T(1024)S(1)} %pad_clamp_fusion), kind=kCustom, calls=%fused_computation | custom fusion | bytes 786624 | tf_op jit(solution)/shard_map/jit(_take)/gather | solution.py:292
  59.9 0.3 gather.7
  60.2 1.1 %select_convert_fusion.x_ref = bf16[16,1,3,4,1024]{4,3,2,1,0:T(4,128)(2,1)} fusion(bf16[16,1,3,4,1024]{4,3,2,1,0:T(4,128)(2,1)S(1)} %gather.7, pred[16,3]{1,0:T(8,128)(4,1)S(1)} %broadcast_in_dim.57, pred[16,3]{1,0:T(8,128)(4,1)S(1)} %broadcast_in_dim.32), kind=kLoop, calls=%fused_computation.8 | loop fusion | flops 393216 | bytes 786528 | tf_op jit(solution)/shard_map/convert_element_type | solution.py:293
  61.3 13.4 %shard_map.39 = bf16[16,1,3,4,1024]{4,3,2,1,0:T(4,128)(2,1)} custom-call(bf16[16,1,3,4,1024]{4,3,2,1,0:T(4,128)(2,1)} %select_convert_fusion.x_ref), custom_call_target="tpu_custom_call" | custom-call | tf_op jit(solution)/shard_map/pallas_call | solution.py:243
  74.7 2.0 %convert.1 = f32[1,1,48,4,1024]{4,3,2,1,0:T(4,128)} convert(bf16[1,1,48,4,1024]{4,3,2,1,0:T(4,128)(2,1)} %bitcast.12) | non-fusion elementwise | flops 196608 | bytes 1179648 | tf_op jit(solution)/shard_map/reshape | solution.py:295
  (8 shorter events, 0.1 us)
Async XLA Ops:
  0.0 12.4 %copy-start = (s32[1,1,18,1]{2,3,1,0:T(1,128)S(1)}, s32[1,1,18,1]{2,3,1,0:T(1,128)}, u32[]{:S(2)}) copy-start(s32[1,1,18,1]{2,3,1,0:T(1,128)} %param.5) | copy-start | bytes 220
  5.6 23.3 %all-to-all-start = ((bf16[8,65,1024]{2,1,0:T(8,128)(2,1)}), bf16[8,65,1024]{2,1,0:T(8,128)(2,1)S(1)}, u32[]{:S(2)}, u32[]{:S(2)}) async-start(bf16[8,65,1024]{2,1,0:T(8,128)(2,1)} %shard_map.37), calls=%async_computation | async-start | bytes 2359296 | tf_op jit(solution)/shard_map/all_to_all | solution.py:267

commit v14 on v13

--- a/solution.py
+++ b/solution.py
@@ -46,6 +46,11 @@
     power = jnp.where(odd, before + square, square + after)
     level = jnp.mean(power, axis=-1, keepdims=True) + 1e-05
     white = (x * lax.rsqrt(power + 0.1 * level)).astype(out_ref.dtype)
+    channels = rows // (WINDOWS * 2)
+    dest = lax.broadcasted_iota(jnp.int32, (rows, rows), 0)
+    source = lax.broadcasted_iota(jnp.int32, (rows, rows), 1)
+    order = (source == (dest % channels) * (WINDOWS * 2) + dest // channels).astype(white.dtype)
+    white = jnp.dot(order, white, preferred_element_type=jnp.float32).astype(out_ref.dtype)
     part = out_ref.shape[2]
     lane = lax.broadcasted_iota(jnp.int32, (1, part), 1)
     extra = jnp.zeros((1, part), jnp.float32)
@@ -79,9 +84,13 @@
     left = left_hot[target]
     right = right_hot[target]
 
+    sources = panel.shape[0]
+    channels = (panel.shape[1] - 1) // (WINDOWS * 2)
+
     def rows_of(hot, window, kind):
-        col = (window * 2 + kind) * part
-        return jnp.dot(hot, panel[:, col:col + part], preferred_element_type=jnp.float32)
+        at = (window * 2 + kind) * channels
+        cols = panel[:, at:at + channels, :].reshape(sources * channels, part)
+        return jnp.dot(hot, cols, preferred_element_type=jnp.float32)
 
     real_sum = None
     imag_sum = None
@@ -164,7 +173,7 @@
     right_hot = right_hot.reshape(chan_count, count, -1)
     part = cos_part.shape[0]
     vmem = pl.BlockSpec(memory_space=pltpu.VMEM)
-    flops = 2 * 2 * rows * panel.shape[0] * panel.shape[1] + 2 * 2 * rows * part * LAGS
+    flops = 2 * 2 * rows * panel.size + 2 * 2 * rows * part * LAGS
     return pl.pallas_call(
         pair_exchange_kernel,
         out_shape=jax.ShapeDtypeStruct((chan_count, count, LAGS), jnp.bfloat16),
@@ -267,7 +276,7 @@
     got = lax.all_to_all(sent, "chan", split_axis=0, concat_axis=0, tiled=True)
     rows_per = channels * WINDOWS * 2
     group_channels = chan_count * channels
-    panel = got[:, :rows_per].reshape(group_channels, WINDOWS * 2 * part)
+    panel = got
     all_blocks = got[:, rows_per, : NB_SRC * 2].astype(jnp.float32).astype(jnp.int32)
     all_blocks = all_blocks.reshape(chan_count * NB_SRC, 1, 2)
     offsets = jnp.arange(BLK, dtype=jnp.int32)

time: 77 us -> 75.5 us (0.981)
  local copies, waits for them, and re-layouts: 5.83 us -> 4.3 us
    reshape x1 -> x0, local copies, waits for them, and re-layouts: 1.45 us -> none  [local(): panel = got[:, :rows_per].reshape(group_channels, WINDOWS * 2 * part)]
where the time goes in v14:
time: 75.5 us; the launch traced here: 75.2 us
  Pallas kernels  41.2 us (55%)
  other arithmetic  13.3 us (18%)
  waiting for transfers between devices  9.45 us (13%)
  starting transfers between devices  6.81 us (9%)
  local copies, waits for them, and re-layouts  4.3 us (6%)
    pallas_call x1, Pallas kernels, pair_exchange(): pl.pallas_call(pair_exchange_kernel, out_shape=jax.ShapeDtypeStruct((chan...  24.4 us
    pallas_call x1, Pallas kernels, exchange(): pl.pallas_call(functools.partial(exchange_kernel, axis, other_axis, axis_...  13.4 us
    all_to_all x1, waiting for transfers between devices, local(): got = lax.all_to_all(sent, 'chan', split_axis=0, concat_axis=0, tiled=True)  9.45 us
    all_to_all x1, starting transfers between devices, local(): got = lax.all_to_all(sent, 'chan', split_axis=0, concat_axis=0, tiled=True)  6.81 us
    pallas_call x1, Pallas kernels, whiten_chunks(): pl.pallas_call(whiten_kernel, out_shape=jax.ShapeDtypeStruct((chan_count,...  3.29 us
    convert_element_type x1, other arithmetic, table_slice(): sin_part = (-sin_ab * weight).astype(jnp.bfloat16)  2.45 us
    cos x1, other arithmetic, table_slice(): cos_b, sin_b = (jnp.cos(fine)[None, :, :], jnp.sin(fine)[None, :, :])  2.04 us
    reshape x1, other arithmetic, local(): return received.reshape(1, 1, slot_count, pairs, LAGS)  1.98 us
  transfers between devices with their start and end apart: 1, of which 1 were waited for; matrix products, arithmetic and copies ran while one was open for 9% of the time, Pallas kernels for 0%

profile of v14, /device:TPU:1, one launch (start us, length us, event | category | flops | bytes accessed | tf_op | source)
XLA Modules:
  0.0 75.2 jit_solution(12565306162204618181)
XLA Ops:
  0.0 0.0 copy-start.1
  0.0 1.5 %reshape.297.x_ref = bf16[64,8192]{1,0:T(8,128)(2,1)S(1)} reshape(bf16[16,2,2,8192]{3,2,1,0:T(2,128)(2,1)} %param.3) | data formatting | bytes 2097152 | tf_op jit(solution)/shard_map/reshape | solution.py:70
  1.5 0.8 %copy.6.blocks_ref = s32[1,1,18,2]{3,2,1,0:T(8,128)S(1)} copy(s32[1,1,18,2]{2,3,1,0:T(2,128)} %param.4) | data formatting | bytes 288 | tf_op args[1]
  2.3 3.3 %shard_map.37 = bf16[8,65,1024]{2,1,0:T(8,128)(2,1)} custom-call(bf16[64,8192]{1,0:T(8,128)(2,1)S(1)} %reshape.297.x_ref, s32[1,1,18,2]{3,2,1,0:T(8,128)S(1)} %copy.6.blocks_ref), custom_call_target="tpu_custom_call" | custom-call | flops 4194304 | bytes 2097152 | tf_op jit(solution)/shard_map/pallas_call | solution.py:72
  5.5 6.8 %all-to-all-start = ((bf16[8,65,1024]{2,1,0:T(8,128)(2,1)}), bf16[8,65,1024]{2,1,0:T(8,128)(2,1)S(1)}, u32[]{:S(2)}, u32[]{:S(2)}) async-start(bf16[8,65,1024]{2,1,0:T(8,128)(2,1)} %shard_map.37), calls=%async_computation | async-start | bytes 2359296 | tf_op jit(solution)/shard_map/all_to_all | solution.py:276
  12.4 0.0 copy-done.1
  12.4 0.2 convert_reduce_fusion.1
  12.6 0.6 iota_reduce_fusion
  13.2 0.1 fusion.19
  13.3 2.0 %fusion.11 = (f32[128,1024]{1,0:T(8,128)S(1)}, f32[128,1024]{1,0:T(8,128)S(1)}) fusion(s32[1024]{0:T(1024)S(1)} %iota_add_fusion.2), kind=kLoop, calls=%fused_computation.23 | loop fusion | flops 1835008 | bytes 1052672 | tf_op jit(solution)/shard_map/cos | solution.py:29
  15.3 0.2 fusion.18
  15.6 0.1 broadcast_in_dim.57
  15.7 0.1 broadcast_in_dim.32
  15.8 1.2 %add_negate_fusion = (f32[8,128,1024]{2,1,0:T(8,128)S(1)}, f32[8,128,1024]{2,1,0:T(8,128)S(1)}) fusion(f32[128,1024]{1,0:T(8,128)S(1)} %get-tuple-element.16, f32[8,1024]{1,0:T(8,128)S(1)} %get-tuple-element.12, f32[128,1024]{1,0:T(8,128)S(1)} %get-tuple-element.15, f32[8,1024]{1,0:T(8,128)S(1)} %get-tuple-element.11), kind=kLoop, calls=%fused_computation.5 | loop fusion | flops 7340032 | bytes 9502720 | tf_op jit(solution)/shard_map/neg | solution.py:35
  17.0 2.4 %fusion = (bf16[1024,1024]{1,0:T(8,128)(2,1)}, bf16[1024,1024]{1,0:T(8,128)(2,1)}) fusion(f32[8,128,1024]{2,1,0:T(8,128)S(1)} %get-tuple-element.9, f32[1024]{0:T(1024)S(1)} %select_multiply_fusion, f32[8,128,1024]{2,1,0:T(8,128)S(1)} %get-tuple-element.10), kind=kLoop, calls=%fused_computation.2 | loop fusion | flops 4194304 | bytes 12587008 | tf_op jit(solution)/shard_map/convert_element_type | solution.py:35
  19.4 9.5 %all-to-all-done.panel = bf16[8,65,1024]{2,1,0:T(8,128)(2,1)S(1)} async-done(((bf16[8,65,1024]{2,1,0:T(8,128)(2,1)}), bf16[8,65,1024]{2,1,0:T(8,128)(2,1)S(1)}, u32[]{:S(2)}, u32[]{:S(2)}) %all-to-all-start) | async-done | bytes 1064992 | tf_op jit(solution)/shard_map/all_to_all | solution.py:276
  28.9 0.0 copy-start
  28.9 0.1 convert_element_type.77
  29.0 0.2 fusion.12
  29.2 0.1 iota_add_fusion
  29.3 0.2 add.127
  29.5 0.2 eq.80
  29.7 0.8 %fusion.8.left_hot = bf16[8,72,128]{2,1,0:T(8,128)(2,1)} fusion(s32[8,72]{1,0:T(8,128)S(1)} %eq.80), kind=kLoop, calls=%fused_computation.20 | loop fusion | flops 147456 | bytes 149760 | tf_op jit(solution)/shard_map/convert_element_type | solution.py:286
  30.5 0.1 add.131
  30.6 0.2 eq.84
  30.8 0.8 %fusion.9.right_hot = bf16[8,72,128]{2,1,0:T(8,128)(2,1)} fusion(s32[8,72]{1,0:T(8,128)S(1)} %eq.84), kind=kLoop, calls=%fused_computation.21 | loop fusion | flops 147456 | bytes 149760 | tf_op jit(solution)/shard_map/convert_element_type | solution.py:287
  31.6 0.0 copy-done
  31.6 24.4 %shard_map.38 = bf16[8,72,1024]{2,1,0:T(8,128)(2,1)} custom-call(bf16[8,72,128]{2,1,0:T(8,128)(2,1)} %fusion.8.left_hot, bf16[8,72,128]{2,1,0:T(8,128)(2,1)} %fusion.9.right_hot, bf16[8,65,1024]{2,1,0:T(8,128)(2,1)} %copy-done, bf16[1024,1024]{1,0:T(8,128)(2,1)} %get-tuple-element.14.cos_ref, bf16[1024,1024]{1,0:T(8,128)(2,1)} %get-tuple-element.13.sin_ref), custom_call_target="tpu_custom_call" | custom-call | flops 3642753024 | bytes 6438912 | tf_op jit(solution)/shard_map/pallas_call | solution.py:177
  56.0 1.5 %convert_reduce_fusion = bf16[72,1024]{1,0:T(8,128)(2,1)S(1)} fusion(bf16[8,72,1024]{2,1,0:T(8,128)(2,1)} %shard_map.38), kind=kLoop, calls=%fused_computation.7 | loop fusion | flops 1105920 | bytes 1327104 | tf_op jit(solution)/shard_map/reduce_sum | solution.py:291
  57.5 0.1 reshape.298
  57.6 0.8 %gather_fusion = bf16[48,4096]{1,0:T(8,128)(2,1)S(1)} fusion(bf16[18,4096]{1,0:T(8,128)(2,1)S(1)} %reshape.298, s32[1024]{0:T(1024)S(1)} %pad_clamp_fusion), kind=kCustom, calls=%fused_computation | custom fusion | bytes 786624 | tf_op jit(solution)/shard_map/jit(_take)/gather | solution.py:301
  58.4 0.3 gather.7
  58.7 1.1 %select_convert_fusion.x_ref = bf16[16,1,3,4,1024]{4,3,2,1,0:T(4,128)(2,1)} fusion(bf16[16,1,3,4,1024]{4,3,2,1,0:T(4,128)(2,1)S(1)} %gather.7, pred[16,3]{1,0:T(8,128)(4,1)S(1)} %broadcast_in_dim.57, pred[16,3]{1,0:T(8,128)(4,1)S(1)} %broadcast_in_dim.32), kind=kLoop, calls=%fused_computation.8 | loop fusion | flops 393216 | bytes 786528 | tf_op jit(solution)/shard_map/convert_element_type | solution.py:302
  59.7 13.4 %shard_map.39 = bf16[16,1,3,4,1024]{4,3,2,1,0:T(4,128)(2,1)} custom-call(bf16[16,1,3,4,1024]{4,3,2,1,0:T(4,128)(2,1)} %select_convert_fusion.x_ref), custom_call_target="tpu_custom_call" | custom-call | tf_op jit(solution)/shard_map/pallas_call | solution.py:252
  73.2 2.0 %convert.1 = f32[1,1,48,4,1024]{4,3,2,1,0:T(4,128)} convert(bf16[1,1,48,4,1024]{4,3,2,1,0:T(4,128)(2,1)} %bitcast.12) | non-fusion elementwise | flops 196608 | bytes 1179648 | tf_op jit(solution)/shard_map/reshape | solution.py:304
  (8 shorter events, 0.1 us)
Async XLA Ops:
  0.0 12.4 %copy-start.1 = (s32[1,1,18,1]{2,3,1,0:T(1,128)S(1)}, s32[1,1,18,1]{2,3,1,0:T(1,128)}, u32[]{:S(2)}) copy-start(s32[1,1,18,1]{2,3,1,0:T(1,128)} %param.5) | copy-start | bytes 220
  5.5 23.3 %all-to-all-start = ((bf16[8,65,1024]{2,1,0:T(8,128)(2,1)}), bf16[8,65,1024]{2,1,0:T(8,128)(2,1)S(1)}, u32[]{:S(2)}, u32[]{:S(2)}) async-start(bf16[8,65,1024]{2,1,0:T(8,128)(2,1)} %shard_map.37), calls=%async_computation | async-start | bytes 2359296 | tf_op jit(solution)/shard_map/all_to_all | solution.py:276
  28.9 2.7 %copy-start = (bf16[8,65,1024]{2,1,0:T(8,128)(2,1)}, bf16[8,65,1024]{2,1,0:T(8,128)(2,1)S(1)}, u32[]{:S(2)}) copy-start(bf16[8,65,1024]{2,1,0:T(8,128)(2,1)S(1)} %all-to-all-done.panel) | copy-start | bytes 3194884

commit v15 on v14

--- a/solution.py
+++ b/solution.py
@@ -109,8 +109,9 @@
     return total + jnp.dot(imag_stack, sin_ref[...], preferred_element_type=jnp.float32)
 
 
-def pair_exchange_kernel(left_hot, right_hot, panel, cos_ref, sin_ref, out_ref, slots, local_sem, send_sem, recv_sem):
-    n = out_ref.shape[0]
+def pair_exchange_kernel(left_hot, right_hot, panel, cos_ref, sin_ref, out_ref, slots, received, local_sem,
+                         send_sem, recv_sem):
+    n = slots.shape[0]
     me = lax.axis_index("chan")
     group = lax.axis_index("grp")
 
@@ -127,7 +128,7 @@
         target = lax.rem(me + step, n)
         return pltpu.make_async_remote_copy(
             src_ref=slots.at[target],
-            dst_ref=out_ref.at[me],
+            dst_ref=received.at[me],
             send_sem=send_sem.at[step],
             recv_sem=recv_sem.at[step],
             device_id=(group, target),
@@ -146,7 +147,7 @@
     lax.fori_loop(1, n, one_step, 0)
     fill(me)
     send(n - 1).start()
-    own = pltpu.make_async_copy(slots.at[me], out_ref.at[me], local_sem)
+    own = pltpu.make_async_copy(slots.at[me], received.at[me], local_sem)
     own.start()
     own.wait()
 
@@ -155,7 +156,7 @@
         source = lax.rem(me + n - step, n)
         pltpu.make_async_remote_copy(
             src_ref=slots.at[source],
-            dst_ref=out_ref.at[source],
+            dst_ref=received.at[source],
             send_sem=send_sem.at[step],
             recv_sem=recv_sem.at[step],
             device_id=(group, source),
@@ -164,6 +165,13 @@
         return carry
 
     lax.fori_loop(1, n, finish, 0)
+    total = received[0].astype(jnp.float32)
+    for source in range(1, n):
+        total = total + received[source].astype(jnp.float32)
+    listed = out_ref.shape[0]
+    lags = cos_ref.shape[1]
+    for pq in range(total.shape[0] // listed):
+        out_ref[:, pq * lags:(pq + 1) * lags] = total[pq * listed:(pq + 1) * listed]
 
 
 def pair_exchange(left_hot, right_hot, panel, cos_part, sin_part, chan_count, collective):
@@ -172,14 +180,16 @@
     left_hot = left_hot.reshape(chan_count, count, -1)
     right_hot = right_hot.reshape(chan_count, count, -1)
     part = cos_part.shape[0]
+    pairs = BLK * BLK
     vmem = pl.BlockSpec(memory_space=pltpu.VMEM)
     flops = 2 * 2 * rows * panel.size + 2 * 2 * rows * part * LAGS
     return pl.pallas_call(
         pair_exchange_kernel,
-        out_shape=jax.ShapeDtypeStruct((chan_count, count, LAGS), jnp.bfloat16),
+        out_shape=jax.ShapeDtypeStruct((count // pairs, pairs * LAGS), jnp.float32),
         in_specs=[vmem] * 5,
-        out_specs=pl.BlockSpec(memory_space=pl.ANY),
+        out_specs=vmem,
         scratch_shapes=[
+            pltpu.VMEM((chan_count, count, LAGS), jnp.bfloat16),
             pltpu.VMEM((chan_count, count, LAGS), jnp.bfloat16),
             pltpu.SemaphoreType.DMA(()),
             pltpu.SemaphoreType.DMA((chan_count,)),
@@ -283,12 +293,13 @@
     left_ch = (all_blocks[:, :, 0] * BLK + offsets[None, :])[:, :, None] + jnp.zeros((1, 1, BLK), jnp.int32)
     right_ch = (all_blocks[:, :, 1] * BLK + offsets[None, :])[:, None, :] + jnp.zeros((1, BLK, 1), jnp.int32)
     channel_ids = jnp.arange(group_channels, dtype=jnp.int32)[None, :]
+    left_ch = left_ch.reshape(chan_count, NB_SRC, BLK, BLK).transpose(0, 2, 3, 1)
+    right_ch = right_ch.reshape(chan_count, NB_SRC, BLK, BLK).transpose(0, 2, 3, 1)
     left_hot = (left_ch.reshape(-1, 1) == channel_ids).astype(jnp.bfloat16)
     right_hot = (right_ch.reshape(-1, 1) == channel_ids).astype(jnp.bfloat16)
 
     cos_part, sin_part = table_slice(me * part, part)
-    gathered = pair_exchange(left_hot, right_hot, panel, cos_part, sin_part, chan_count, 0)
-    corr = jnp.sum(gathered.astype(jnp.float32), axis=0).reshape(NB_SRC, pairs * LAGS)
+    corr = pair_exchange(left_hot, right_hot, panel, cos_part, sin_part, chan_count, 0)
 
     owner_list = owners[0, 0, :, 0]
     same = owner_list[:, None] == owner_list[None, :]

time: 75.5 us -> 75 us (level)
  other arithmetic: 13.3 us -> 11.1 us
  local copies, waits for them, and re-layouts: 4.3 us -> 5.3 us
    reduce_sum x1 -> x0, other arithmetic: 1.47 us -> none  [local(): jnp.sum(gathered.astype(jnp.float32), axis=0).reshape(NB_SRC, pairs * LAGS)]
    gather x2, local copies, waits for them, and re-layouts: 1.07 us -> 2.44 us  [local(): placed = jnp.where(filled[:, None], jnp.take(corr, source, axis=0), 0.0)]
    pallas_call x1, Pallas kernels: 24.4 us -> 25.2 us  [pair_exchange(): pl.pallas_call(pair_exchange_kernel, out_shape=jax.ShapeDtypeStruct((coun...]
    convert_element_type x1 -> x0, other arithmetic: 0.8 us -> none  [local(): right_hot = (right_ch.reshape(-1, 1) == channel_ids).astype(jnp.bfloat16)]
where the time goes in v15:
time: 75 us; the launch traced here: 74.7 us
  Pallas kernels  41.9 us (56%)
  other arithmetic  11.1 us (15%)
  waiting for transfers between devices  9.45 us (13%)
  starting transfers between devices  6.81 us (9%)
  local copies, waits for them, and re-layouts  5.3 us (7%)
    pallas_call x1, Pallas kernels, pair_exchange(): pl.pallas_call(pair_exchange_kernel, out_shape=jax.ShapeDtypeStruct((coun...  25.2 us
    pallas_call x1, Pallas kernels, exchange(): pl.pallas_call(functools.partial(exchange_kernel, axis, other_axis, axis_...  13.4 us
    all_to_all x1, waiting for transfers between devices, local(): got = lax.all_to_all(sent, 'chan', split_axis=0, concat_axis=0, tiled=True)  9.45 us
    all_to_all x1, starting transfers between devices, local(): got = lax.all_to_all(sent, 'chan', split_axis=0, concat_axis=0, tiled=True)  6.81 us
    pallas_call x1, Pallas kernels, whiten_chunks(): pl.pallas_call(whiten_kernel, out_shape=jax.ShapeDtypeStruct((chan_count,...  3.29 us
    convert_element_type x1, other arithmetic, table_slice(): sin_part = (-sin_ab * weight).astype(jnp.bfloat16)  2.45 us
    gather x2, local copies, waits for them, and re-layouts, local(): placed = jnp.where(filled[:, None], jnp.take(corr, source, axis=0), 0.0)  2.44 us
    cos x1, other arithmetic, table_slice(): cos_b, sin_b = (jnp.cos(fine)[None, :, :], jnp.sin(fine)[None, :, :])  2.04 us
  transfers between devices with their start and end apart: 1, of which 1 were waited for; matrix products, arithmetic and copies ran while one was open for 9% of the time, Pallas kernels for 0%

profile of v15, /device:TPU:1, one launch (start us, length us, event | category | flops | bytes accessed | tf_op | source)
XLA Modules:
  0.0 74.7 jit_solution(8359128541673649738)
XLA Ops:
  0.0 0.0 copy-start.1
  0.0 1.5 %reshape.304.x_ref = bf16[64,8192]{1,0:T(8,128)(2,1)S(1)} reshape(bf16[16,2,2,8192]{3,2,1,0:T(2,128)(2,1)} %param.3) | data formatting | bytes 2097152 | tf_op jit(solution)/shard_map/reshape | solution.py:70
  1.5 0.8 %copy.6.blocks_ref = s32[1,1,18,2]{3,2,1,0:T(8,128)S(1)} copy(s32[1,1,18,2]{2,3,1,0:T(2,128)} %param.4) | data formatting | bytes 288 | tf_op args[1]
  2.3 3.3 %shard_map.37 = bf16[8,65,1024]{2,1,0:T(8,128)(2,1)} custom-call(bf16[64,8192]{1,0:T(8,128)(2,1)S(1)} %reshape.304.x_ref, s32[1,1,18,2]{3,2,1,0:T(8,128)S(1)} %copy.6.blocks_ref), custom_call_target="tpu_custom_call" | custom-call | flops 4194304 | bytes 2097152 | tf_op jit(solution)/shard_map/pallas_call | solution.py:72
  5.5 6.8 %all-to-all-start = ((bf16[8,65,1024]{2,1,0:T(8,128)(2,1)}), bf16[8,65,1024]{2,1,0:T(8,128)(2,1)S(1)}, u32[]{:S(2)}, u32[]{:S(2)}) async-start(bf16[8,65,1024]{2,1,0:T(8,128)(2,1)} %shard_map.37), calls=%async_computation | async-start | bytes 2359296 | tf_op jit(solution)/shard_map/all_to_all | solution.py:286
  12.4 0.0 copy-done.1
  12.4 0.2 convert_reduce_fusion
  12.6 0.6 iota_reduce_fusion
  13.2 0.1 fusion.19
  13.3 2.0 %fusion.11 = (f32[128,1024]{1,0:T(8,128)S(1)}, f32[128,1024]{1,0:T(8,128)S(1)}) fusion(s32[1024]{0:T(1024)S(1)} %iota_add_fusion.2), kind=kLoop, calls=%fused_computation.22 | loop fusion | flops 1835008 | bytes 1052672 | tf_op jit(solution)/shard_map/cos | solution.py:29
  15.3 0.2 fusion.18
  15.6 0.1 broadcast_in_dim.57
  15.7 0.1 broadcast_in_dim.32
  15.8 1.2 %add_negate_fusion = (f32[8,128,1024]{2,1,0:T(8,128)S(1)}, f32[8,128,1024]{2,1,0:T(8,128)S(1)}) fusion(f32[128,1024]{1,0:T(8,128)S(1)} %get-tuple-element.16, f32[8,1024]{1,0:T(8,128)S(1)} %get-tuple-element.12, f32[128,1024]{1,0:T(8,128)S(1)} %get-tuple-element.15, f32[8,1024]{1,0:T(8,128)S(1)} %get-tuple-element.11), kind=kLoop, calls=%fused_computation.5 | loop fusion | flops 7340032 | bytes 9502720 | tf_op jit(solution)/shard_map/neg | solution.py:35
  17.0 2.4 %fusion = (bf16[1024,1024]{1,0:T(8,128)(2,1)}, bf16[1024,1024]{1,0:T(8,128)(2,1)}) fusion(f32[8,128,1024]{2,1,0:T(8,128)S(1)} %get-tuple-element.9, f32[1024]{0:T(1024)S(1)} %select_multiply_fusion, f32[8,128,1024]{2,1,0:T(8,128)S(1)} %get-tuple-element.10), kind=kLoop, calls=%fused_computation.2 | loop fusion | flops 4194304 | bytes 12587008 | tf_op jit(solution)/shard_map/convert_element_type | solution.py:35
  19.4 9.5 %all-to-all-done.panel = bf16[8,65,1024]{2,1,0:T(8,128)(2,1)S(1)} async-done(((bf16[8,65,1024]{2,1,0:T(8,128)(2,1)}), bf16[8,65,1024]{2,1,0:T(8,128)(2,1)S(1)}, u32[]{:S(2)}, u32[]{:S(2)}) %all-to-all-start) | async-done | bytes 1064992 | tf_op jit(solution)/shard_map/all_to_all | solution.py:286
  28.9 0.0 copy-start
  28.9 0.1 convert_element_type.74
  29.0 0.2 fusion.12
  29.2 0.1 mul.203
  29.3 0.1 eq.80
  29.4 0.1 mul.205
  29.5 0.1 eq.84
  29.6 0.9 %fusion.8 = (bf16[8,72,128]{2,1,0:T(8,128)(2,1)}, bf16[8,72,128]{2,1,0:T(8,128)(2,1)}) fusion(s32[8,72]{1,0:T(8,128)S(1)} %eq.80, s32[8,72]{1,0:T(8,128)S(1)} %eq.84), kind=kLoop, calls=%fused_computation.19 | loop fusion | flops 294912 | bytes 299520 | tf_op jit(solution)/shard_map/convert_element_type | solution.py:298
  30.5 0.0 copy-done
  30.6 25.2 %shard_map.38 = f32[18,4096]{1,0:T(8,128)} custom-call(bf16[8,72,128]{2,1,0:T(8,128)(2,1)} %get-tuple-element.17.left_hot, bf16[8,72,128]{2,1,0:T(8,128)(2,1)} %get-tuple-element.18.right_hot, bf16[8,65,1024]{2,1,0:T(8,128)(2,1)} %copy-done, bf16[1024,1024]{1,0:T(8,128)(2,1)} %get-tuple-element.14.cos_ref, bf16[1024,1024]{1,0:T(8,128)(2,1)} %get-tuple-element.13.sin_ref), custom_call_target="tpu_custom_call" | custom-call | flops 3642753024 | bytes 6438912 | tf_op jit(solution)/shard_map/pallas_call | solution.py:186
  55.8 2.2 %gather_fusion = bf16[48,4096]{1,0:T(8,128)(2,1)S(1)} fusion(f32[18,4096]{1,0:T(8,128)} %shard_map.38, s32[1024]{0:T(1024)S(1)} %pad_clamp_fusion), kind=kCustom, calls=%fused_computation | custom fusion | bytes 786624 | tf_op jit(solution)/shard_map/jit(_take)/gather | solution.py:312
  58.0 0.3 gather.7
  58.2 1.1 %select_convert_fusion.x_ref = bf16[16,1,3,4,1024]{4,3,2,1,0:T(4,128)(2,1)} fusion(bf16[16,1,3,4,1024]{4,3,2,1,0:T(4,128)(2,1)S(1)} %gather.7, pred[16,3]{1,0:T(8,128)(4,1)S(1)} %broadcast_in_dim.57, pred[16,3]{1,0:T(8,128)(4,1)S(1)} %broadcast_in_dim.32), kind=kLoop, calls=%fused_computation.7 | loop fusion | flops 393216 | bytes 786528 | tf_op jit(solution)/shard_map/convert_element_type | solution.py:313
  59.3 13.4 %shard_map.39 = bf16[16,1,3,4,1024]{4,3,2,1,0:T(4,128)(2,1)} custom-call(bf16[16,1,3,4,1024]{4,3,2,1,0:T(4,128)(2,1)} %select_convert_fusion.x_ref), custom_call_target="tpu_custom_call" | custom-call | tf_op jit(solution)/shard_map/pallas_call | solution.py:262
  72.7 2.0 %convert.1 = f32[1,1,48,4,1024]{4,3,2,1,0:T(4,128)} convert(bf16[1,1,48,4,1024]{4,3,2,1,0:T(4,128)(2,1)} %bitcast.16) | non-fusion elementwise | flops 196608 | bytes 1179648 | tf_op jit(solution)/shard_map/reshape | solution.py:315
  (12 shorter events, 0.1 us)
Async XLA Ops:
  0.0 12.4 %copy-start.1 = (s32[1,1,18,1]{2,3,1,0:T(1,128)S(1)}, s32[1,1,18,1]{2,3,1,0:T(1,128)}, u32[]{:S(2)}) copy-start(s32[1,1,18,1]{2,3,1,0:T(1,128)} %param.5) | copy-start | bytes 220
  5.5 23.3 %all-to-all-start = ((bf16[8,65,1024]{2,1,0:T(8,128)(2,1)}), bf16[8,65,1024]{2,1,0:T(8,128)(2,1)S(1)}, u32[]{:S(2)}, u32[]{:S(2)}) async-start(bf16[8,65,1024]{2,1,0:T(8,128)(2,1)} %shard_map.37), calls=%async_computation | async-start | bytes 2359296 | tf_op jit(solution)/shard_map/all_to_all | solution.py:286
  28.9 1.7 %copy-start = (bf16[8,65,1024]{2,1,0:T(8,128)(2,1)}, bf16[8,65,1024]{2,1,0:T(8,128)(2,1)S(1)}, u32[]{:S(2)}) copy-start(bf16[8,65,1024]{2,1,0:T(8,128)(2,1)S(1)} %all-to-all-done.panel) | copy-start | bytes 3194884

commit v16 on v15

--- a/solution.py
+++ b/solution.py
@@ -306,10 +306,8 @@
     earlier = jnp.arange(NB_SRC)[None, :] < jnp.arange(NB_SRC)[:, None]
     order_rank = jnp.sum(jnp.logical_and(same, earlier), axis=1)
     slot_ids = owner_list * MOST + order_rank
-    chooser = slot_ids[None, :] == jnp.arange(slot_count, dtype=jnp.int32)[:, None]
-    source = jnp.argmax(chooser, axis=1)
-    filled = jnp.any(chooser, axis=1)
-    placed = jnp.where(filled[:, None], jnp.take(corr, source, axis=0), 0.0)
+    chooser = (slot_ids[None, :] == jnp.arange(slot_count, dtype=jnp.int32)[:, None]).astype(jnp.bfloat16)
+    placed = jnp.dot(chooser, corr.astype(jnp.bfloat16), preferred_element_type=jnp.float32)
     placed = placed.reshape(groups_count, 1, MOST, pairs, LAGS).astype(jnp.bfloat16)
     received = exchange(placed, "grp", "chan", True, 1, 1).astype(jnp.float32)
     return received.reshape(1, 1, slot_count, pairs, LAGS)

time: 75 us -> 73.7 us (0.983)
  other arithmetic: 11.1 us -> 9.28 us
  local copies, waits for them, and re-layouts: 5.3 us -> 3.7 us
  matrix products: 0 us -> 1.24 us
  waiting for transfers between devices: 9.45 us -> 10.4 us
    gather x2 -> x0, local copies, waits for them, and re-layouts: 2.44 us -> none  [local(): placed = jnp.where(filled[:, None], jnp.take(corr, source, axis=0), 0.0)]
    dot_general x0 -> x1, matrix products: none -> 1.24 us  [local(): jnp.dot(chooser, corr.astype(jnp.bfloat16), preferred_element_type=jnp.fl...]
    convert_element_type x1 -> x0, other arithmetic: 1.1 us -> none  [local(): placed.reshape(groups_count, 1, MOST, pairs, LAGS).astype(jnp.bfloat16)]
    convert_element_type x0 -> x1, local copies, waits for them, and re-layouts: none -> 1.02 us  [local(): placed.reshape(groups_count, 1, MOST, pairs, LAGS).astype(jnp.bfloat16)]
    all_to_all x1, waiting for transfers between devices: 9.45 us -> 10.4 us  [local(): got = lax.all_to_all(sent, 'chan', split_axis=0, concat_axis=0, tiled=True)]
  transfers between devices with their start and end apart: 1 -> 1, of which waited for: 1 -> 1; matrix products, arithmetic and copies ran while one was open for 9% -> 8% of each run, Pallas kernels for 0% -> 0%
where the time goes in v16:
time: 73.7 us; the launch traced here: 73.4 us
  Pallas kernels  41.9 us (57%)
  waiting for transfers between devices  10.4 us (14%)
  other arithmetic  9.28 us (13%)
  starting transfers between devices  6.81 us (9%)
  local copies, waits for them, and re-layouts  3.7 us (5%)
  matrix products  1.24 us (2%)
    pallas_call x1, Pallas kernels, pair_exchange(): pl.pallas_call(pair_exchange_kernel, out_shape=jax.ShapeDtypeStruct((coun...  25.2 us
    pallas_call x1, Pallas kernels, exchange(): pl.pallas_call(functools.partial(exchange_kernel, axis, other_axis, axis_...  13.4 us
    all_to_all x1, waiting for transfers between devices, local(): got = lax.all_to_all(sent, 'chan', split_axis=0, concat_axis=0, tiled=True)  10.4 us
    all_to_all x1, starting transfers between devices, local(): got = lax.all_to_all(sent, 'chan', split_axis=0, concat_axis=0, tiled=True)  6.81 us
    pallas_call x1, Pallas kernels, whiten_chunks(): pl.pallas_call(whiten_kernel, out_shape=jax.ShapeDtypeStruct((chan_count,...  3.29 us
    convert_element_type x1, other arithmetic, table_slice(): sin_part = (-sin_ab * weight).astype(jnp.bfloat16)  2.45 us
    cos x1, other arithmetic, table_slice(): cos_b, sin_b = (jnp.cos(fine)[None, :, :], jnp.sin(fine)[None, :, :])  2.04 us
    reshape x1, other arithmetic, local(): return received.reshape(1, 1, slot_count, pairs, LAGS)  1.98 us
  transfers between devices with their start and end apart: 1, of which 1 were waited for; matrix products, arithmetic and copies ran while one was open for 8% of the time, Pallas kernels for 0%

profile of v16, /device:TPU:1, one launch (start us, length us, event | category | flops | bytes accessed | tf_op | source)
XLA Modules:
  0.0 73.4 jit_solution(15343069837987673557)
XLA Ops:
  0.0 0.0 copy-start.1
  0.0 1.5 %reshape.282.x_ref = bf16[64,8192]{1,0:T(8,128)(2,1)S(1)} reshape(bf16[16,2,2,8192]{3,2,1,0:T(2,128)(2,1)} %param.3) | data formatting | bytes 2097152 | tf_op jit(solution)/shard_map/reshape | solution.py:70
  1.5 0.8 %copy.6.blocks_ref = s32[1,1,18,2]{3,2,1,0:T(8,128)S(1)} copy(s32[1,1,18,2]{2,3,1,0:T(2,128)} %param.4) | data formatting | bytes 288 | tf_op args[1]
  2.3 3.3 %shard_map.37 = bf16[8,65,1024]{2,1,0:T(8,128)(2,1)} custom-call(bf16[64,8192]{1,0:T(8,128)(2,1)S(1)} %reshape.282.x_ref, s32[1,1,18,2]{3,2,1,0:T(8,128)S(1)} %copy.6.blocks_ref), custom_call_target="tpu_custom_call" | custom-call | flops 4194304 | bytes 2097152 | tf_op jit(solution)/shard_map/pallas_call | solution.py:72
  5.5 6.8 %all-to-all-start = ((bf16[8,65,1024]{2,1,0:T(8,128)(2,1)}), bf16[8,65,1024]{2,1,0:T(8,128)(2,1)S(1)}, u32[]{:S(2)}, u32[]{:S(2)}) async-start(bf16[8,65,1024]{2,1,0:T(8,128)(2,1)} %shard_map.37), calls=%async_computation | async-start | bytes 2359296 | tf_op jit(solution)/shard_map/all_to_all | solution.py:286
  12.4 2.0 %fusion.11 = (f32[128,1024]{1,0:T(8,128)S(1)}, f32[128,1024]{1,0:T(8,128)S(1)}) fusion(s32[1024]{0:T(1024)S(1)} %iota_add_fusion.2), kind=kLoop, calls=%fused_computation.21 | loop fusion | flops 1835008 | bytes 1052672 | tf_op jit(solution)/shard_map/cos | solution.py:29
  14.4 0.2 fusion.19
  14.7 0.0 copy-done.1
  14.7 0.2 convert_reduce_fusion
  14.8 1.2 %add_negate_fusion = (f32[8,128,1024]{2,1,0:T(8,128)S(1)}, f32[8,128,1024]{2,1,0:T(8,128)S(1)}) fusion(f32[128,1024]{1,0:T(8,128)S(1)} %get-tuple-element.14, f32[8,1024]{1,0:T(8,128)S(1)} %get-tuple-element.10, f32[128,1024]{1,0:T(8,128)S(1)} %get-tuple-element.13, f32[8,1024]{1,0:T(8,128)S(1)} %get-tuple-element.9), kind=kLoop, calls=%fused_computation.5 | loop fusion | flops 7340032 | bytes 9502720 | tf_op jit(solution)/shard_map/neg | solution.py:35
  16.0 2.4 %fusion = (bf16[1024,1024]{1,0:T(8,128)(2,1)}, bf16[1024,1024]{1,0:T(8,128)(2,1)}) fusion(f32[8,128,1024]{2,1,0:T(8,128)S(1)} %get-tuple-element.7, f32[1024]{0:T(1024)S(1)} %select_multiply_fusion, f32[8,128,1024]{2,1,0:T(8,128)S(1)} %get-tuple-element.8), kind=kLoop, calls=%fused_computation.2 | loop fusion | flops 4194304 | bytes 12587008 | tf_op jit(solution)/shard_map/convert_element_type | solution.py:35
  18.5 10.4 %all-to-all-done.panel = bf16[8,65,1024]{2,1,0:T(8,128)(2,1)S(1)} async-done(((bf16[8,65,1024]{2,1,0:T(8,128)(2,1)}), bf16[8,65,1024]{2,1,0:T(8,128)(2,1)S(1)}, u32[]{:S(2)}, u32[]{:S(2)}) %all-to-all-start) | async-done | bytes 1064992 | tf_op jit(solution)/shard_map/all_to_all | solution.py:286
  28.9 0.0 copy-start
  28.9 0.1 convert_element_type.80
  29.0 0.2 fusion.13
  29.2 0.1 mul.203
  29.3 0.1 eq.78
  29.4 0.1 mul.205
  29.5 0.1 eq.82
  29.6 0.9 %fusion.8 = (bf16[8,72,128]{2,1,0:T(8,128)(2,1)}, bf16[8,72,128]{2,1,0:T(8,128)(2,1)}) fusion(s32[8,72]{1,0:T(8,128)S(1)} %eq.78, s32[8,72]{1,0:T(8,128)S(1)} %eq.82), kind=kLoop, calls=%fused_computation.18 | loop fusion | flops 294912 | bytes 299520 | tf_op jit(solution)/shard_map/convert_element_type | solution.py:298
  30.5 0.0 copy-done
  30.5 25.2 %shard_map.38 = f32[18,4096]{1,0:T(8,128)} custom-call(bf16[8,72,128]{2,1,0:T(8,128)(2,1)} %get-tuple-element.15.left_hot, bf16[8,72,128]{2,1,0:T(8,128)(2,1)} %get-tuple-element.16.right_hot, bf16[8,65,1024]{2,1,0:T(8,128)(2,1)} %copy-done, bf16[1024,1024]{1,0:T(8,128)(2,1)} %get-tuple-element.12.cos_ref, bf16[1024,1024]{1,0:T(8,128)(2,1)} %get-tuple-element.11.sin_ref), custom_call_target="tpu_custom_call" | custom-call | flops 3642753024 | bytes 6438912 | tf_op jit(solution)/shard_map/pallas_call | solution.py:186
  55.8 1.2 %convolution_convert_fusion = bf16[48,4096]{1,0:T(8,128)(2,1)S(1)} fusion(f32[18,4096]{1,0:T(8,128)} %shard_map.38, s32[18]{0:T(128)S(1)} %multiply_add_fusion.1), kind=kOutput, calls=%fused_computation | convolution fusion | flops 7349088 | bytes 688200 | tf_op jit(solution)/shard_map/dot_general | solution.py:310
  57.0 1.0 %convert_element_type.89.x_ref = bf16[16,1,3,4,1024]{4,3,2,1,0:T(4,128)(2,1)} reshape(bf16[48,4096]{1,0:T(8,128)(2,1)S(1)} %convolution_convert_fusion) | data formatting | bytes 786432 | tf_op jit(solution)/shard_map/convert_element_type | solution.py:311
  58.1 13.4 %shard_map.39 = bf16[16,1,3,4,1024]{4,3,2,1,0:T(4,128)(2,1)} custom-call(bf16[16,1,3,4,1024]{4,3,2,1,0:T(4,128)(2,1)} %convert_element_type.89.x_ref), custom_call_target="tpu_custom_call" | custom-call | tf_op jit(solution)/shard_map/pallas_call | solution.py:262
  71.4 2.0 %convert.1 = f32[1,1,48,4,1024]{4,3,2,1,0:T(4,128)} convert(bf16[1,1,48,4,1024]{4,3,2,1,0:T(4,128)(2,1)} %bitcast.16) | non-fusion elementwise | flops 196608 | bytes 1179648 | tf_op jit(solution)/shard_map/reshape | solution.py:313
  (9 shorter events, 0.1 us)
Async XLA Ops:
  0.0 14.7 %copy-start.1 = (s32[1,1,18,1]{2,3,1,0:T(1,128)S(1)}, s32[1,1,18,1]{2,3,1,0:T(1,128)}, u32[]{:S(2)}) copy-start(s32[1,1,18,1]{2,3,1,0:T(1,128)} %param.5) | copy-start | bytes 220
  5.5 23.3 %all-to-all-start = ((bf16[8,65,1024]{2,1,0:T(8,128)(2,1)}), bf16[8,65,1024]{2,1,0:T(8,128)(2,1)S(1)}, u32[]{:S(2)}, u32[]{:S(2)}) async-start(bf16[8,65,1024]{2,1,0:T(8,128)(2,1)} %shard_map.37), calls=%async_computation | async-start | bytes 2359296 | tf_op jit(solution)/shard_map/all_to_all | solution.py:286
  28.9 1.7 %copy-start = (bf16[8,65,1024]{2,1,0:T(8,128)(2,1)}, bf16[8,65,1024]{2,1,0:T(8,128)(2,1)S(1)}, u32[]{:S(2)}) copy-start(bf16[8,65,1024]{2,1,0:T(8,128)(2,1)S(1)} %all-to-all-done.panel) | copy-start | bytes 3194884

commit v17 on v16

--- a/solution.py
+++ b/solution.py
@@ -81,11 +81,11 @@
 
 def pair_rows(left_hot, right_hot, panel, cos_ref, sin_ref, target):
     part = cos_ref.shape[0]
-    left = left_hot[target]
-    right = right_hot[target]
-
     sources = panel.shape[0]
     channels = (panel.shape[1] - 1) // (WINDOWS * 2)
+    ids = lax.broadcasted_iota(jnp.int32, (left_hot.shape[1], sources * channels), 1)
+    left = (left_hot[target] == ids).astype(jnp.bfloat16)
+    right = (right_hot[target] == ids).astype(jnp.bfloat16)
 
     def rows_of(hot, window, kind):
         at = (window * 2 + kind) * channels
@@ -295,8 +295,8 @@
     channel_ids = jnp.arange(group_channels, dtype=jnp.int32)[None, :]
     left_ch = left_ch.reshape(chan_count, NB_SRC, BLK, BLK).transpose(0, 2, 3, 1)
     right_ch = right_ch.reshape(chan_count, NB_SRC, BLK, BLK).transpose(0, 2, 3, 1)
-    left_hot = (left_ch.reshape(-1, 1) == channel_ids).astype(jnp.bfloat16)
-    right_hot = (right_ch.reshape(-1, 1) == channel_ids).astype(jnp.bfloat16)
+    left_hot = left_ch.reshape(-1, 1)
+    right_hot = right_ch.reshape(-1, 1)
 
     cos_part, sin_part = table_slice(me * part, part)
     corr = pair_exchange(left_hot, right_hot, panel, cos_part, sin_part, chan_count, 0)

time: 73.7 us -> 74.6 us (1.012)
  local copies, waits for them, and re-layouts: 3.7 us -> 5.28 us
  other arithmetic: 9.28 us -> 8.34 us
    another operation x0 -> x2, local copies, waits for them, and re-layouts: none -> 1.74 us  [the longest x1 0.88 us: pair_exchange(): right_hot = right_hot.reshape(chan_count, count, -1)]
    convert_element_type x1 -> x0, other arithmetic: 0.94 us -> none  [local(): left_hot = (left_ch.reshape(-1, 1) == channel_ids).astype(jnp.bfloat16)]
where the time goes in v17:
time: 74.6 us; the launch traced here: 74.3 us
  Pallas kernels  42.1 us (56%)
  waiting for transfers between devices  10.4 us (14%)
  other arithmetic  8.34 us (11%)
  starting transfers between devices  6.81 us (9%)
  local copies, waits for them, and re-layouts  5.28 us (7%)
  matrix products  1.24 us (2%)
    pallas_call x1, Pallas kernels, pair_exchange(): pl.pallas_call(pair_exchange_kernel, out_shape=jax.ShapeDtypeStruct((coun...  25.5 us
    pallas_call x1, Pallas kernels, exchange(): pl.pallas_call(functools.partial(exchange_kernel, axis, other_axis, axis_...  13.3 us
    all_to_all x1, waiting for transfers between devices, local(): got = lax.all_to_all(sent, 'chan', split_axis=0, concat_axis=0, tiled=True)  10.4 us
    all_to_all x1, starting transfers between devices, local(): got = lax.all_to_all(sent, 'chan', split_axis=0, concat_axis=0, tiled=True)  6.81 us
    pallas_call x1, Pallas kernels, whiten_chunks(): pl.pallas_call(whiten_kernel, out_shape=jax.ShapeDtypeStruct((chan_count,...  3.29 us
    convert_element_type x1, other arithmetic, table_slice(): sin_part = (-sin_ab * weight).astype(jnp.bfloat16)  2.45 us
    cos x1, other arithmetic, table_slice(): cos_b, sin_b = (jnp.cos(fine)[None, :, :], jnp.sin(fine)[None, :, :])  2.04 us
    reshape x1, other arithmetic, local(): return received.reshape(1, 1, slot_count, pairs, LAGS)  1.98 us
  transfers between devices with their start and end apart: 1, of which 1 were waited for; matrix products, arithmetic and copies ran while one was open for 8% of the time, Pallas kernels for 0%

profile of v17, /device:TPU:1, one launch (start us, length us, event | category | flops | bytes accessed | tf_op | source)
XLA Modules:
  0.0 74.3 jit_solution(11602482964678859343)
XLA Ops:
  0.0 0.0 copy-start.1
  0.0 1.5 %reshape.260.x_ref = bf16[64,8192]{1,0:T(8,128)(2,1)S(1)} reshape(bf16[16,2,2,8192]{3,2,1,0:T(2,128)(2,1)} %param.3) | data formatting | bytes 2097152 | tf_op jit(solution)/shard_map/reshape | solution.py:70
  1.5 0.8 %copy.8.blocks_ref = s32[1,1,18,2]{3,2,1,0:T(8,128)S(1)} copy(s32[1,1,18,2]{2,3,1,0:T(2,128)} %param.4) | data formatting | bytes 288 | tf_op args[1]
  2.3 3.3 %shard_map.37 = bf16[8,65,1024]{2,1,0:T(8,128)(2,1)} custom-call(bf16[64,8192]{1,0:T(8,128)(2,1)S(1)} %reshape.260.x_ref, s32[1,1,18,2]{3,2,1,0:T(8,128)S(1)} %copy.8.blocks_ref), custom_call_target="tpu_custom_call" | custom-call | flops 4194304 | bytes 2097152 | tf_op jit(solution)/shard_map/pallas_call | solution.py:72
  5.5 6.8 %all-to-all-start = ((bf16[8,65,1024]{2,1,0:T(8,128)(2,1)}), bf16[8,65,1024]{2,1,0:T(8,128)(2,1)S(1)}, u32[]{:S(2)}, u32[]{:S(2)}) async-start(bf16[8,65,1024]{2,1,0:T(8,128)(2,1)} %shard_map.37), calls=%async_computation | async-start | bytes 2359296 | tf_op jit(solution)/shard_map/all_to_all | solution.py:286
  12.4 2.0 %fusion.9 = (f32[128,1024]{1,0:T(8,128)S(1)}, f32[128,1024]{1,0:T(8,128)S(1)}) fusion(s32[1024]{0:T(1024)S(1)} %iota_add_fusion.2), kind=kLoop, calls=%fused_computation.17 | loop fusion | flops 1835008 | bytes 1052672 | tf_op jit(solution)/shard_map/cos | solution.py:29
  14.4 0.2 fusion.17
  14.7 0.0 copy-done.1
  14.7 0.2 convert_reduce_fusion
  14.8 1.2 %add_negate_fusion = (f32[8,128,1024]{2,1,0:T(8,128)S(1)}, f32[8,128,1024]{2,1,0:T(8,128)S(1)}) fusion(f32[128,1024]{1,0:T(8,128)S(1)} %get-tuple-element.14, f32[8,1024]{1,0:T(8,128)S(1)} %get-tuple-element.10, f32[128,1024]{1,0:T(8,128)S(1)} %get-tuple-element.13, f32[8,1024]{1,0:T(8,128)S(1)} %get-tuple-element.9), kind=kLoop, calls=%fused_computation.5 | loop fusion | flops 7340032 | bytes 9502720 | tf_op jit(solution)/shard_map/neg | solution.py:35
  16.0 2.4 %fusion = (bf16[1024,1024]{1,0:T(8,128)(2,1)}, bf16[1024,1024]{1,0:T(8,128)(2,1)}) fusion(f32[8,128,1024]{2,1,0:T(8,128)S(1)} %get-tuple-element.7, f32[1024]{0:T(1024)S(1)} %select_multiply_fusion, f32[8,128,1024]{2,1,0:T(8,128)S(1)} %get-tuple-element.8), kind=kLoop, calls=%fused_computation.2 | loop fusion | flops 4194304 | bytes 12587008 | tf_op jit(solution)/shard_map/convert_element_type | solution.py:35
  18.5 10.4 %all-to-all-done.panel = bf16[8,65,1024]{2,1,0:T(8,128)(2,1)S(1)} async-done(((bf16[8,65,1024]{2,1,0:T(8,128)(2,1)}), bf16[8,65,1024]{2,1,0:T(8,128)(2,1)S(1)}, u32[]{:S(2)}, u32[]{:S(2)}) %all-to-all-start) | async-done | bytes 1064992 | tf_op jit(solution)/shard_map/all_to_all | solution.py:286
  28.9 0.0 copy-start
  28.9 0.1 convert_element_type.72
  29.0 0.2 fusion.11
  29.2 0.1 mul.203
  29.3 0.9 %reshape_reshape.8.left_hot = s32[8,72,1]{2,1,0:T(8,128)} reshape(s32[8,2,2,18]{3,2,1,0:T(2,128)S(1)} %broadcast_bitcast_fusion.1) | data formatting | bytes 4608 | tf_op jit(solution)/shard_map/reshape;reshape | solution.py:180
  30.2 0.1 mul.205
  30.3 0.9 %reshape_reshape.9.right_hot = s32[8,72,1]{2,1,0:T(8,128)} reshape(s32[8,2,2,18]{3,2,1,0:T(2,128)S(1)} %broadcast_bitcast_fusion) | data formatting | bytes 4608 | tf_op jit(solution)/shard_map/reshape;reshape | solution.py:181
  31.2 0.0 copy-done
  31.2 25.5 %shard_map.38 = f32[18,4096]{1,0:T(8,128)} custom-call(s32[8,72,1]{2,1,0:T(8,128)} %reshape_reshape.8.left_hot, s32[8,72,1]{2,1,0:T(8,128)} %reshape_reshape.9.right_hot, bf16[8,65,1024]{2,1,0:T(8,128)(2,1)} %copy-done, bf16[1024,1024]{1,0:T(8,128)(2,1)} %get-tuple-element.12.cos_ref, bf16[1024,1024]{1,0:T(8,128)(2,1)} %get-tuple-element.11.sin_ref), custom_call_target="tpu_custom_call" | custom-call | flops 3642753024 | bytes 6438912 | tf_op jit(solution)/shard_map/pallas_call | solution.py:186
  56.7 1.2 %convolution_convert_fusion = bf16[48,4096]{1,0:T(8,128)(2,1)S(1)} fusion(f32[18,4096]{1,0:T(8,128)} %shard_map.38, s32[18]{0:T(128)S(1)} %multiply_add_fusion.1), kind=kOutput, calls=%fused_computation | convolution fusion | flops 7349088 | bytes 688200 | tf_op jit(solution)/shard_map/dot_general | solution.py:310
  58.0 1.0 %convert_element_type.79.x_ref = bf16[16,1,3,4,1024]{4,3,2,1,0:T(4,128)(2,1)} reshape(bf16[48,4096]{1,0:T(8,128)(2,1)S(1)} %convolution_convert_fusion) | data formatting | bytes 786432 | tf_op jit(solution)/shard_map/convert_element_type | solution.py:311
  59.0 13.3 %shard_map.39 = bf16[16,1,3,4,1024]{4,3,2,1,0:T(4,128)(2,1)} custom-call(bf16[16,1,3,4,1024]{4,3,2,1,0:T(4,128)(2,1)} %convert_element_type.79.x_ref), custom_call_target="tpu_custom_call" | custom-call | tf_op jit(solution)/shard_map/pallas_call | solution.py:262
  72.3 2.0 %convert.1 = f32[1,1,48,4,1024]{4,3,2,1,0:T(4,128)} convert(bf16[1,1,48,4,1024]{4,3,2,1,0:T(4,128)(2,1)} %bitcast.16) | non-fusion elementwise | flops 196608 | bytes 1179648 | tf_op jit(solution)/shard_map/reshape | solution.py:313
  (9 shorter events, 0.1 us)
Async XLA Ops:
  0.0 14.7 %copy-start.1 = (s32[1,1,18,1]{2,3,1,0:T(1,128)S(1)}, s32[1,1,18,1]{2,3,1,0:T(1,128)}, u32[]{:S(2)}) copy-start(s32[1,1,18,1]{2,3,1,0:T(1,128)} %param.5) | copy-start | bytes 220
  5.5 23.3 %all-to-all-start = ((bf16[8,65,1024]{2,1,0:T(8,128)(2,1)}), bf16[8,65,1024]{2,1,0:T(8,128)(2,1)S(1)}, u32[]{:S(2)}, u32[]{:S(2)}) async-start(bf16[8,65,1024]{2,1,0:T(8,128)(2,1)} %shard_map.37), calls=%async_computation | async-start | bytes 2359296 | tf_op jit(solution)/shard_map/all_to_all | solution.py:286
  28.9 2.3 %copy-start = (bf16[8,65,1024]{2,1,0:T(8,128)(2,1)}, bf16[8,65,1024]{2,1,0:T(8,128)(2,1)S(1)}, u32[]{:S(2)}) copy-start(bf16[8,65,1024]{2,1,0:T(8,128)(2,1)S(1)} %all-to-all-done.panel) | copy-start | bytes 3194884

commit v18 on v16

--- a/solution.py
+++ b/solution.py
@@ -109,6 +109,15 @@
     return total + jnp.dot(imag_stack, sin_ref[...], preferred_element_type=jnp.float32)
 
 
+def flip(x, step, n):
+    out = 0
+    bit = 1
+    while bit < n:
+        out = out + ((x // bit + step // bit) % 2) * bit
+        bit = bit * 2
+    return out
+
+
 def pair_exchange_kernel(left_hot, right_hot, panel, cos_ref, sin_ref, out_ref, slots, received, local_sem,
                          send_sem, recv_sem):
     n = slots.shape[0]
@@ -125,7 +134,7 @@
         slots[target] = pair_rows(left_hot, right_hot, panel, cos_ref, sin_ref, target).astype(slots.dtype)
 
     def send(step):
-        target = lax.rem(me + step, n)
+        target = flip(me, step, n)
         return pltpu.make_async_remote_copy(
             src_ref=slots.at[target],
             dst_ref=received.at[me],
@@ -136,7 +145,7 @@
         )
 
     def one_step(step, carry):
-        fill(lax.rem(me + step, n))
+        fill(flip(me, step, n))
 
         @pl.when(step > 1)
         def _():
@@ -153,7 +162,7 @@
 
     def finish(step, carry):
         send(step).wait_send()
-        source = lax.rem(me + n - step, n)
+        source = flip(me, step, n)
         pltpu.make_async_remote_copy(
             src_ref=slots.at[source],
             dst_ref=received.at[source],

time: 73.7 us -> 78.9 us (1.071)
  Pallas kernels: 41.9 us -> 46.4 us
    pallas_call x1, Pallas kernels: 25.2 us -> 30.8 us  [pair_exchange(): pl.pallas_call(pair_exchange_kernel, out_shape=jax.ShapeDtypeStruct((coun...]
    pallas_call x1, Pallas kernels: 13.4 us -> 12.4 us  [exchange(): pl.pallas_call(functools.partial(exchange_kernel, axis, other_axis, axis_...]
where the time goes in v18:
time: 78.9 us; the launch traced here: 78 us
  Pallas kernels  46.4 us (59%)
  waiting for transfers between devices  10.4 us (13%)
  other arithmetic  9.28 us (12%)
  starting transfers between devices  6.81 us (9%)
  local copies, waits for them, and re-layouts  3.7 us (5%)
  matrix products  1.25 us (2%)
    pallas_call x1, Pallas kernels, pair_exchange(): pl.pallas_call(pair_exchange_kernel, out_shape=jax.ShapeDtypeStruct((coun...  30.8 us
    pallas_call x1, Pallas kernels, exchange(): pl.pallas_call(functools.partial(exchange_kernel, axis, other_axis, axis_...  12.4 us
    all_to_all x1, waiting for transfers between devices, local(): got = lax.all_to_all(sent, 'chan', split_axis=0, concat_axis=0, tiled=True)  10.4 us
    all_to_all x1, starting transfers between devices, local(): got = lax.all_to_all(sent, 'chan', split_axis=0, concat_axis=0, tiled=True)  6.81 us
    pallas_call x1, Pallas kernels, whiten_chunks(): pl.pallas_call(whiten_kernel, out_shape=jax.ShapeDtypeStruct((chan_count,...  3.29 us
    convert_element_type x1, other arithmetic, table_slice(): sin_part = (-sin_ab * weight).astype(jnp.bfloat16)  2.45 us
    cos x1, other arithmetic, table_slice(): cos_b, sin_b = (jnp.cos(fine)[None, :, :], jnp.sin(fine)[None, :, :])  2.04 us
    reshape x1, other arithmetic, local(): return received.reshape(1, 1, slot_count, pairs, LAGS)  1.98 us
  transfers between devices with their start and end apart: 1, of which 1 were waited for; matrix products, arithmetic and copies ran while one was open for 8% of the time, Pallas kernels for 0%

profile of v18, /device:TPU:1, one launch (start us, length us, event | category | flops | bytes accessed | tf_op | source)
XLA Modules:
  0.0 78.0 jit_solution(2645144502157499822)
XLA Ops:
  0.0 0.0 copy-start.1
  0.0 1.5 %reshape.282.x_ref = bf16[64,8192]{1,0:T(8,128)(2,1)S(1)} reshape(bf16[16,2,2,8192]{3,2,1,0:T(2,128)(2,1)} %param.3) | data formatting | bytes 2097152 | tf_op jit(solution)/shard_map/reshape | solution.py:70
  1.5 0.8 copy.6.blocks_ref
  2.3 3.3 %shard_map.37 = bf16[8,65,1024]{2,1,0:T(8,128)(2,1)} custom-call(bf16[64,8192]{1,0:T(8,128)(2,1)S(1)} %reshape.282.x_ref, s32[1,1,18,2]{3,2,1,0:T(8,128)S(1)} %copy.6.blocks_ref), custom_call_target="tpu_custom_call" | custom-call | flops 4194304 | bytes 2097152 | tf_op jit(solution)/shard_map/pallas_call | solution.py:72
  5.5 6.8 %all-to-all-start = ((bf16[8,65,1024]{2,1,0:T(8,128)(2,1)}), bf16[8,65,1024]{2,1,0:T(8,128)(2,1)S(1)}, u32[]{:S(2)}, u32[]{:S(2)}) async-start(bf16[8,65,1024]{2,1,0:T(8,128)(2,1)} %shard_map.37), calls=%async_computation | async-start | bytes 2359296 | tf_op jit(solution)/shard_map/all_to_all | solution.py:295
  12.4 2.0 %fusion.11 = (f32[128,1024]{1,0:T(8,128)S(1)}, f32[128,1024]{1,0:T(8,128)S(1)}) fusion(s32[1024]{0:T(1024)S(1)} %iota_add_fusion.2), kind=kLoop, calls=%fused_computation.21 | loop fusion | flops 1835008 | bytes 1052672 | tf_op jit(solution)/shard_map/cos | solution.py:29
  14.4 0.2 fusion.19
  14.7 0.0 copy-done.1
  14.7 0.2 convert_reduce_fusion
  14.8 1.2 %add_negate_fusion = (f32[8,128,1024]{2,1,0:T(8,128)S(1)}, f32[8,128,1024]{2,1,0:T(8,128)S(1)}) fusion(f32[128,1024]{1,0:T(8,128)S(1)} %get-tuple-element.14, f32[8,1024]{1,0:T(8,128)S(1)} %get-tuple-element.10, f32[128,1024]{1,0:T(8,128)S(1)} %get-tuple-element.13, f32[8,1024]{1,0:T(8,128)S(1)} %get-tuple-element.9), kind=kLoop, calls=%fused_computation.5 | loop fusion | flops 7340032 | bytes 9502720 | tf_op jit(solution)/shard_map/neg | solution.py:35
  16.0 2.4 %fusion = (bf16[1024,1024]{1,0:T(8,128)(2,1)}, bf16[1024,1024]{1,0:T(8,128)(2,1)}) fusion(f32[8,128,1024]{2,1,0:T(8,128)S(1)} %get-tuple-element.7, f32[1024]{0:T(1024)S(1)} %select_multiply_fusion, f32[8,128,1024]{2,1,0:T(8,128)S(1)} %get-tuple-element.8), kind=kLoop, calls=%fused_computation.2 | loop fusion | flops 4194304 | bytes 12587008 | tf_op jit(solution)/shard_map/convert_element_type | solution.py:35
  18.5 10.4 %all-to-all-done.panel = bf16[8,65,1024]{2,1,0:T(8,128)(2,1)S(1)} async-done(((bf16[8,65,1024]{2,1,0:T(8,128)(2,1)}), bf16[8,65,1024]{2,1,0:T(8,128)(2,1)S(1)}, u32[]{:S(2)}, u32[]{:S(2)}) %all-to-all-start) | async-done | bytes 1064992 | tf_op jit(solution)/shard_map/all_to_all | solution.py:295
  28.9 0.0 copy-start
  28.9 0.1 convert_element_type.80
  29.0 0.2 fusion.13
  29.2 0.1 mul.203
  29.3 0.1 eq.78
  29.4 0.1 mul.205
  29.5 0.1 eq.82
  29.6 0.9 %fusion.8 = (bf16[8,72,128]{2,1,0:T(8,128)(2,1)}, bf16[8,72,128]{2,1,0:T(8,128)(2,1)}) fusion(s32[8,72]{1,0:T(8,128)S(1)} %eq.78, s32[8,72]{1,0:T(8,128)S(1)} %eq.82), kind=kLoop, calls=%fused_computation.18 | loop fusion | flops 294912 | bytes 299520 | tf_op jit(solution)/shard_map/convert_element_type | solution.py:307
  30.5 0.0 copy-done
  30.5 30.8 %shard_map.38 = f32[18,4096]{1,0:T(8,128)} custom-call(bf16[8,72,128]{2,1,0:T(8,128)(2,1)} %get-tuple-element.15.left_hot, bf16[8,72,128]{2,1,0:T(8,128)(2,1)} %get-tuple-element.16.right_hot, bf16[8,65,1024]{2,1,0:T(8,128)(2,1)} %copy-done, bf16[1024,1024]{1,0:T(8,128)(2,1)} %get-tuple-element.12.cos_ref, bf16[1024,1024]{1,0:T(8,128)(2,1)} %get-tuple-element.11.sin_ref), custom_call_target="tpu_custom_call" | custom-call | flops 3642753024 | bytes 6438912 | tf_op jit(solution)/shard_map/pallas_call | solution.py:195
  61.3 1.2 %convolution_convert_fusion = bf16[48,4096]{1,0:T(8,128)(2,1)S(1)} fusion(f32[18,4096]{1,0:T(8,128)} %shard_map.38, s32[18]{0:T(128)S(1)} %multiply_add_fusion.1), kind=kOutput, calls=%fused_computation | convolution fusion | flops 7349088 | bytes 688200 | tf_op jit(solution)/shard_map/dot_general | solution.py:319
  62.6 1.0 %convert_element_type.89.x_ref = bf16[16,1,3,4,1024]{4,3,2,1,0:T(4,128)(2,1)} reshape(bf16[48,4096]{1,0:T(8,128)(2,1)S(1)} %convolution_convert_fusion) | data formatting | bytes 786432 | tf_op jit(solution)/shard_map/convert_element_type | solution.py:320
  63.6 12.4 %shard_map.39 = bf16[16,1,3,4,1024]{4,3,2,1,0:T(4,128)(2,1)} custom-call(bf16[16,1,3,4,1024]{4,3,2,1,0:T(4,128)(2,1)} %convert_element_type.89.x_ref), custom_call_target="tpu_custom_call" | custom-call | tf_op jit(solution)/shard_map/pallas_call | solution.py:271
  76.0 2.0 %convert.1 = f32[1,1,48,4,1024]{4,3,2,1,0:T(4,128)} convert(bf16[1,1,48,4,1024]{4,3,2,1,0:T(4,128)(2,1)} %bitcast.16) | non-fusion elementwise | flops 196608 | bytes 1179648 | tf_op jit(solution)/shard_map/reshape | solution.py:322
  (9 shorter events, 0.1 us)
Async XLA Ops:
  0.0 14.7 %copy-start.1 = (s32[1,1,18,1]{2,3,1,0:T(1,128)S(1)}, s32[1,1,18,1]{2,3,1,0:T(1,128)}, u32[]{:S(2)}) copy-start(s32[1,1,18,1]{2,3,1,0:T(1,128)} %param.5) | copy-start | bytes 220
  5.5 23.3 %all-to-all-start = ((bf16[8,65,1024]{2,1,0:T(8,128)(2,1)}), bf16[8,65,1024]{2,1,0:T(8,128)(2,1)S(1)}, u32[]{:S(2)}, u32[]{:S(2)}) async-start(bf16[8,65,1024]{2,1,0:T(8,128)(2,1)} %shard_map.37), calls=%async_computation | async-start | bytes 2359296 | tf_op jit(solution)/shard_map/all_to_all | solution.py:295
  28.9 1.7 %copy-start = (bf16[8,65,1024]{2,1,0:T(8,128)(2,1)}, bf16[8,65,1024]{2,1,0:T(8,128)(2,1)S(1)}, u32[]{:S(2)}) copy-start(bf16[8,65,1024]{2,1,0:T(8,128)(2,1)S(1)} %all-to-all-done.panel) | copy-start | bytes 3194884

commit v19 on v16

--- a/solution.py
+++ b/solution.py
@@ -121,22 +121,27 @@
                             device_id_type=pl.DeviceIdType.MESH)
     pl.semaphore_wait(barrier, n - 1)
 
+    parity = me % 2
+
+    def offset(step):
+        return step + parity * ((step + n - 3) % (n - 1) + 1 - step)
+
     def fill(target):
         slots[target] = pair_rows(left_hot, right_hot, panel, cos_ref, sin_ref, target).astype(slots.dtype)
 
     def send(step):
-        target = lax.rem(me + step, n)
+        target = lax.rem(me + offset(step), n)
         return pltpu.make_async_remote_copy(
             src_ref=slots.at[target],
             dst_ref=received.at[me],
             send_sem=send_sem.at[step],
-            recv_sem=recv_sem.at[step],
+            recv_sem=recv_sem.at[offset(step)],
             device_id=(group, target),
             device_id_type=pl.DeviceIdType.MESH,
         )
 
     def one_step(step, carry):
-        fill(lax.rem(me + step, n))
+        fill(lax.rem(me + offset(step), n))
 
         @pl.when(step > 1)
         def _():
@@ -153,12 +158,13 @@
 
     def finish(step, carry):
         send(step).wait_send()
-        source = lax.rem(me + n - step, n)
+        distance = step
+        source = lax.rem(me + n - distance, n)
         pltpu.make_async_remote_copy(
             src_ref=slots.at[source],
             dst_ref=received.at[source],
             send_sem=send_sem.at[step],
-            recv_sem=recv_sem.at[step],
+            recv_sem=recv_sem.at[distance],
             device_id=(group, source),
             device_id_type=pl.DeviceIdType.MESH,
         ).wait_recv()

time: 73.7 us -> 75.2 us (1.020)
  Pallas kernels: 41.9 us -> 43.3 us
    pallas_call x1, Pallas kernels: 25.2 us -> 26.7 us  [pair_exchange(): pl.pallas_call(pair_exchange_kernel, out_shape=jax.ShapeDtypeStruct((coun...]
where the time goes in v19:
time: 75.2 us; the launch traced here: 74.9 us
  Pallas kernels  43.3 us (58%)
  waiting for transfers between devices  10.4 us (14%)
  other arithmetic  9.28 us (12%)
  starting transfers between devices  6.81 us (9%)
  local copies, waits for them, and re-layouts  3.7 us (5%)
  matrix products  1.25 us (2%)
    pallas_call x1, Pallas kernels, pair_exchange(): pl.pallas_call(pair_exchange_kernel, out_shape=jax.ShapeDtypeStruct((coun...  26.7 us
    pallas_call x1, Pallas kernels, exchange(): pl.pallas_call(functools.partial(exchange_kernel, axis, other_axis, axis_...  13.3 us
    all_to_all x1, waiting for transfers between devices, local(): got = lax.all_to_all(sent, 'chan', split_axis=0, concat_axis=0, tiled=True)  10.4 us
    all_to_all x1, starting transfers between devices, local(): got = lax.all_to_all(sent, 'chan', split_axis=0, concat_axis=0, tiled=True)  6.81 us
    pallas_call x1, Pallas kernels, whiten_chunks(): pl.pallas_call(whiten_kernel, out_shape=jax.ShapeDtypeStruct((chan_count,...  3.29 us
    convert_element_type x1, other arithmetic, table_slice(): sin_part = (-sin_ab * weight).astype(jnp.bfloat16)  2.45 us
    cos x1, other arithmetic, table_slice(): cos_b, sin_b = (jnp.cos(fine)[None, :, :], jnp.sin(fine)[None, :, :])  2.04 us
    reshape x1, other arithmetic, local(): return received.reshape(1, 1, slot_count, pairs, LAGS)  1.98 us
  transfers between devices with their start and end apart: 1, of which 1 were waited for; matrix products, arithmetic and copies ran while one was open for 8% of the time, Pallas kernels for 0%

profile of v19, /device:TPU:1, one launch (start us, length us, event | category | flops | bytes accessed | tf_op | source)
XLA Modules:
  0.0 74.9 jit_solution(17083904619877179507)
XLA Ops:
  0.0 0.0 copy-start.1
  0.0 1.5 %reshape.282.x_ref = bf16[64,8192]{1,0:T(8,128)(2,1)S(1)} reshape(bf16[16,2,2,8192]{3,2,1,0:T(2,128)(2,1)} %param.3) | data formatting | bytes 2097152 | tf_op jit(solution)/shard_map/reshape | solution.py:70
  1.5 0.8 %copy.6.blocks_ref = s32[1,1,18,2]{3,2,1,0:T(8,128)S(1)} copy(s32[1,1,18,2]{2,3,1,0:T(2,128)} %param.4) | data formatting | bytes 288 | tf_op args[1]
  2.3 3.3 %shard_map.37 = bf16[8,65,1024]{2,1,0:T(8,128)(2,1)} custom-call(bf16[64,8192]{1,0:T(8,128)(2,1)S(1)} %reshape.282.x_ref, s32[1,1,18,2]{3,2,1,0:T(8,128)S(1)} %copy.6.blocks_ref), custom_call_target="tpu_custom_call" | custom-call | flops 4194304 | bytes 2097152 | tf_op jit(solution)/shard_map/pallas_call | solution.py:72
  5.5 6.8 %all-to-all-start = ((bf16[8,65,1024]{2,1,0:T(8,128)(2,1)}), bf16[8,65,1024]{2,1,0:T(8,128)(2,1)S(1)}, u32[]{:S(2)}, u32[]{:S(2)}) async-start(bf16[8,65,1024]{2,1,0:T(8,128)(2,1)} %shard_map.37), calls=%async_computation | async-start | bytes 2359296 | tf_op jit(solution)/shard_map/all_to_all | solution.py:292
  12.4 2.0 %fusion.11 = (f32[128,1024]{1,0:T(8,128)S(1)}, f32[128,1024]{1,0:T(8,128)S(1)}) fusion(s32[1024]{0:T(1024)S(1)} %iota_add_fusion.2), kind=kLoop, calls=%fused_computation.21 | loop fusion | flops 1835008 | bytes 1052672 | tf_op jit(solution)/shard_map/cos | solution.py:29
  14.4 0.2 fusion.19
  14.7 0.0 copy-done.1
  14.7 0.2 convert_reduce_fusion
  14.8 1.2 %add_negate_fusion = (f32[8,128,1024]{2,1,0:T(8,128)S(1)}, f32[8,128,1024]{2,1,0:T(8,128)S(1)}) fusion(f32[128,1024]{1,0:T(8,128)S(1)} %get-tuple-element.14, f32[8,1024]{1,0:T(8,128)S(1)} %get-tuple-element.10, f32[128,1024]{1,0:T(8,128)S(1)} %get-tuple-element.13, f32[8,1024]{1,0:T(8,128)S(1)} %get-tuple-element.9), kind=kLoop, calls=%fused_computation.5 | loop fusion | flops 7340032 | bytes 9502720 | tf_op jit(solution)/shard_map/neg | solution.py:35
  16.0 2.4 %fusion = (bf16[1024,1024]{1,0:T(8,128)(2,1)}, bf16[1024,1024]{1,0:T(8,128)(2,1)}) fusion(f32[8,128,1024]{2,1,0:T(8,128)S(1)} %get-tuple-element.7, f32[1024]{0:T(1024)S(1)} %select_multiply_fusion, f32[8,128,1024]{2,1,0:T(8,128)S(1)} %get-tuple-element.8), kind=kLoop, calls=%fused_computation.2 | loop fusion | flops 4194304 | bytes 12587008 | tf_op jit(solution)/shard_map/convert_element_type | solution.py:35
  18.5 10.4 %all-to-all-done.panel = bf16[8,65,1024]{2,1,0:T(8,128)(2,1)S(1)} async-done(((bf16[8,65,1024]{2,1,0:T(8,128)(2,1)}), bf16[8,65,1024]{2,1,0:T(8,128)(2,1)S(1)}, u32[]{:S(2)}, u32[]{:S(2)}) %all-to-all-start) | async-done | bytes 1064992 | tf_op jit(solution)/shard_map/all_to_all | solution.py:292
  28.9 0.0 copy-start
  28.9 0.1 convert_element_type.80
  29.0 0.2 fusion.13
  29.2 0.1 mul.203
  29.3 0.1 eq.78
  29.4 0.1 mul.205
  29.5 0.1 eq.82
  29.6 0.9 %fusion.8 = (bf16[8,72,128]{2,1,0:T(8,128)(2,1)}, bf16[8,72,128]{2,1,0:T(8,128)(2,1)}) fusion(s32[8,72]{1,0:T(8,128)S(1)} %eq.78, s32[8,72]{1,0:T(8,128)S(1)} %eq.82), kind=kLoop, calls=%fused_computation.18 | loop fusion | flops 294912 | bytes 299520 | tf_op jit(solution)/shard_map/convert_element_type | solution.py:304
  30.5 0.0 copy-done
  30.5 26.7 %shard_map.38 = f32[18,4096]{1,0:T(8,128)} custom-call(bf16[8,72,128]{2,1,0:T(8,128)(2,1)} %get-tuple-element.15.left_hot, bf16[8,72,128]{2,1,0:T(8,128)(2,1)} %get-tuple-element.16.right_hot, bf16[8,65,1024]{2,1,0:T(8,128)(2,1)} %copy-done, bf16[1024,1024]{1,0:T(8,128)(2,1)} %get-tuple-element.12.cos_ref, bf16[1024,1024]{1,0:T(8,128)(2,1)} %get-tuple-element.11.sin_ref), custom_call_target="tpu_custom_call" | custom-call | flops 3642753024 | bytes 6438912 | tf_op jit(solution)/shard_map/pallas_call | solution.py:192
  57.3 1.2 %convolution_convert_fusion = bf16[48,4096]{1,0:T(8,128)(2,1)S(1)} fusion(f32[18,4096]{1,0:T(8,128)} %shard_map.38, s32[18]{0:T(128)S(1)} %multiply_add_fusion.1), kind=kOutput, calls=%fused_computation | convolution fusion | flops 7349088 | bytes 688200 | tf_op jit(solution)/shard_map/dot_general | solution.py:316
  58.5 1.0 %convert_element_type.89.x_ref = bf16[16,1,3,4,1024]{4,3,2,1,0:T(4,128)(2,1)} reshape(bf16[48,4096]{1,0:T(8,128)(2,1)S(1)} %convolution_convert_fusion) | data formatting | bytes 786432 | tf_op jit(solution)/shard_map/convert_element_type | solution.py:317
  59.6 13.3 %shard_map.39 = bf16[16,1,3,4,1024]{4,3,2,1,0:T(4,128)(2,1)} custom-call(bf16[16,1,3,4,1024]{4,3,2,1,0:T(4,128)(2,1)} %convert_element_type.89.x_ref), custom_call_target="tpu_custom_call" | custom-call | tf_op jit(solution)/shard_map/pallas_call | solution.py:268
  72.9 2.0 %convert.1 = f32[1,1,48,4,1024]{4,3,2,1,0:T(4,128)} convert(bf16[1,1,48,4,1024]{4,3,2,1,0:T(4,128)(2,1)} %bitcast.16) | non-fusion elementwise | flops 196608 | bytes 1179648 | tf_op jit(solution)/shard_map/reshape | solution.py:319
  (9 shorter events, 0.1 us)
Async XLA Ops:
  0.0 14.7 %copy-start.1 = (s32[1,1,18,1]{2,3,1,0:T(1,128)S(1)}, s32[1,1,18,1]{2,3,1,0:T(1,128)}, u32[]{:S(2)}) copy-start(s32[1,1,18,1]{2,3,1,0:T(1,128)} %param.5) | copy-start | bytes 220
  5.5 23.3 %all-to-all-start = ((bf16[8,65,1024]{2,1,0:T(8,128)(2,1)}), bf16[8,65,1024]{2,1,0:T(8,128)(2,1)S(1)}, u32[]{:S(2)}, u32[]{:S(2)}) async-start(bf16[8,65,1024]{2,1,0:T(8,128)(2,1)} %shard_map.37), calls=%async_computation | async-start | bytes 2359296 | tf_op jit(solution)/shard_map/all_to_all | solution.py:292
  28.9 1.7 %copy-start = (bf16[8,65,1024]{2,1,0:T(8,128)(2,1)}, bf16[8,65,1024]{2,1,0:T(8,128)(2,1)S(1)}, u32[]{:S(2)}) copy-start(bf16[8,65,1024]{2,1,0:T(8,128)(2,1)S(1)} %all-to-all-done.panel) | copy-start | bytes 3194884

commit v20 on v16

--- a/solution.py
+++ b/solution.py
@@ -115,12 +115,6 @@
     me = lax.axis_index("chan")
     group = lax.axis_index("grp")
 
-    barrier = pltpu.get_barrier_semaphore()
-    for step in range(1, n):
-        pl.semaphore_signal(barrier, inc=1, device_id=(group, lax.rem(me + step, n)),
-                            device_id_type=pl.DeviceIdType.MESH)
-    pl.semaphore_wait(barrier, n - 1)
-
     def fill(target):
         slots[target] = pair_rows(left_hot, right_hot, panel, cos_ref, sin_ref, target).astype(slots.dtype)
 
@@ -137,14 +131,17 @@
 
     def one_step(step, carry):
         fill(lax.rem(me + step, n))
-
-        @pl.when(step > 1)
-        def _():
-            send(step - 1).start()
+        send(step - 1).start()
 
         return carry
 
-    lax.fori_loop(1, n, one_step, 0)
+    fill(lax.rem(me + 1, n))
+    barrier = pltpu.get_barrier_semaphore()
+    for step in range(1, n):
+        pl.semaphore_signal(barrier, inc=1, device_id=(group, lax.rem(me + step, n)),
+                            device_id_type=pl.DeviceIdType.MESH)
+    pl.semaphore_wait(barrier, n - 1)
+    lax.fori_loop(2, n, one_step, 0)
     fill(me)
     send(n - 1).start()
     own = pltpu.make_async_copy(slots.at[me], received.at[me], local_sem)

time: 73.7 us -> 73.7 us (level)
  no operation moved by 1% of the time
where the time goes in v20:
time: 73.7 us; the launch traced here: 73.4 us
  Pallas kernels  41.9 us (57%)
  waiting for transfers between devices  10.4 us (14%)
  other arithmetic  9.28 us (13%)
  starting transfers between devices  6.81 us (9%)
  local copies, waits for them, and re-layouts  3.7 us (5%)
  matrix products  1.24 us (2%)
    pallas_call x1, Pallas kernels, pair_exchange(): pl.pallas_call(pair_exchange_kernel, out_shape=jax.ShapeDtypeStruct((coun...  25.3 us
    pallas_call x1, Pallas kernels, exchange(): pl.pallas_call(functools.partial(exchange_kernel, axis, other_axis, axis_...  13.3 us
    all_to_all x1, waiting for transfers between devices, local(): got = lax.all_to_all(sent, 'chan', split_axis=0, concat_axis=0, tiled=True)  10.4 us
    all_to_all x1, starting transfers between devices, local(): got = lax.all_to_all(sent, 'chan', split_axis=0, concat_axis=0, tiled=True)  6.81 us
    pallas_call x1, Pallas kernels, whiten_chunks(): pl.pallas_call(whiten_kernel, out_shape=jax.ShapeDtypeStruct((chan_count,...  3.29 us
    convert_element_type x1, other arithmetic, table_slice(): sin_part = (-sin_ab * weight).astype(jnp.bfloat16)  2.45 us
    cos x1, other arithmetic, table_slice(): cos_b, sin_b = (jnp.cos(fine)[None, :, :], jnp.sin(fine)[None, :, :])  2.04 us
    reshape x1, other arithmetic, local(): return received.reshape(1, 1, slot_count, pairs, LAGS)  1.98 us
  transfers between devices with their start and end apart: 1, of which 1 were waited for; matrix products, arithmetic and copies ran while one was open for 8% of the time, Pallas kernels for 0%

profile of v20, /device:TPU:1, one launch (start us, length us, event | category | flops | bytes accessed | tf_op | source)
XLA Modules:
  0.0 73.4 jit_solution(2450701774829173059)
XLA Ops:
  0.0 0.0 copy-start.1
  0.0 1.5 %reshape.282.x_ref = bf16[64,8192]{1,0:T(8,128)(2,1)S(1)} reshape(bf16[16,2,2,8192]{3,2,1,0:T(2,128)(2,1)} %param.3) | data formatting | bytes 2097152 | tf_op jit(solution)/shard_map/reshape | solution.py:70
  1.5 0.8 %copy.6.blocks_ref = s32[1,1,18,2]{3,2,1,0:T(8,128)S(1)} copy(s32[1,1,18,2]{2,3,1,0:T(2,128)} %param.4) | data formatting | bytes 288 | tf_op args[1]
  2.3 3.3 %shard_map.37 = bf16[8,65,1024]{2,1,0:T(8,128)(2,1)} custom-call(bf16[64,8192]{1,0:T(8,128)(2,1)S(1)} %reshape.282.x_ref, s32[1,1,18,2]{3,2,1,0:T(8,128)S(1)} %copy.6.blocks_ref), custom_call_target="tpu_custom_call" | custom-call | flops 4194304 | bytes 2097152 | tf_op jit(solution)/shard_map/pallas_call | solution.py:72
  5.5 6.8 %all-to-all-start = ((bf16[8,65,1024]{2,1,0:T(8,128)(2,1)}), bf16[8,65,1024]{2,1,0:T(8,128)(2,1)S(1)}, u32[]{:S(2)}, u32[]{:S(2)}) async-start(bf16[8,65,1024]{2,1,0:T(8,128)(2,1)} %shard_map.37), calls=%async_computation | async-start | bytes 2359296 | tf_op jit(solution)/shard_map/all_to_all | solution.py:283
  12.4 2.0 %fusion.11 = (f32[128,1024]{1,0:T(8,128)S(1)}, f32[128,1024]{1,0:T(8,128)S(1)}) fusion(s32[1024]{0:T(1024)S(1)} %iota_add_fusion.2), kind=kLoop, calls=%fused_computation.21 | loop fusion | flops 1835008 | bytes 1052672 | tf_op jit(solution)/shard_map/cos | solution.py:29
  14.4 0.2 fusion.19
  14.7 0.0 copy-done.1
  14.7 0.2 convert_reduce_fusion
  14.8 1.2 %add_negate_fusion = (f32[8,128,1024]{2,1,0:T(8,128)S(1)}, f32[8,128,1024]{2,1,0:T(8,128)S(1)}) fusion(f32[128,1024]{1,0:T(8,128)S(1)} %get-tuple-element.14, f32[8,1024]{1,0:T(8,128)S(1)} %get-tuple-element.10, f32[128,1024]{1,0:T(8,128)S(1)} %get-tuple-element.13, f32[8,1024]{1,0:T(8,128)S(1)} %get-tuple-element.9), kind=kLoop, calls=%fused_computation.5 | loop fusion | flops 7340032 | bytes 9502720 | tf_op jit(solution)/shard_map/neg | solution.py:35
  16.0 2.4 %fusion = (bf16[1024,1024]{1,0:T(8,128)(2,1)}, bf16[1024,1024]{1,0:T(8,128)(2,1)}) fusion(f32[8,128,1024]{2,1,0:T(8,128)S(1)} %get-tuple-element.7, f32[1024]{0:T(1024)S(1)} %select_multiply_fusion, f32[8,128,1024]{2,1,0:T(8,128)S(1)} %get-tuple-element.8), kind=kLoop, calls=%fused_computation.2 | loop fusion | flops 4194304 | bytes 12587008 | tf_op jit(solution)/shard_map/convert_element_type | solution.py:35
  18.5 10.4 %all-to-all-done.panel = bf16[8,65,1024]{2,1,0:T(8,128)(2,1)S(1)} async-done(((bf16[8,65,1024]{2,1,0:T(8,128)(2,1)}), bf16[8,65,1024]{2,1,0:T(8,128)(2,1)S(1)}, u32[]{:S(2)}, u32[]{:S(2)}) %all-to-all-start) | async-done | bytes 1064992 | tf_op jit(solution)/shard_map/all_to_all | solution.py:283
  28.9 0.0 copy-start
  28.9 0.1 convert_element_type.80
  29.0 0.2 fusion.13
  29.2 0.1 mul.203
  29.3 0.1 eq.78
  29.4 0.1 mul.205
  29.5 0.1 eq.82
  29.6 0.9 %fusion.8 = (bf16[8,72,128]{2,1,0:T(8,128)(2,1)}, bf16[8,72,128]{2,1,0:T(8,128)(2,1)}) fusion(s32[8,72]{1,0:T(8,128)S(1)} %eq.78, s32[8,72]{1,0:T(8,128)S(1)} %eq.82), kind=kLoop, calls=%fused_computation.18 | loop fusion | flops 294912 | bytes 299520 | tf_op jit(solution)/shard_map/convert_element_type | solution.py:295
  30.5 0.0 copy-done
  30.6 25.3 %shard_map.38 = f32[18,4096]{1,0:T(8,128)} custom-call(bf16[8,72,128]{2,1,0:T(8,128)(2,1)} %get-tuple-element.15.left_hot, bf16[8,72,128]{2,1,0:T(8,128)(2,1)} %get-tuple-element.16.right_hot, bf16[8,65,1024]{2,1,0:T(8,128)(2,1)} %copy-done, bf16[1024,1024]{1,0:T(8,128)(2,1)} %get-tuple-element.12.cos_ref, bf16[1024,1024]{1,0:T(8,128)(2,1)} %get-tuple-element.11.sin_ref), custom_call_target="tpu_custom_call" | custom-call | flops 3642753024 | bytes 6438912 | tf_op jit(solution)/shard_map/pallas_call | solution.py:183
  55.8 1.2 %convolution_convert_fusion = bf16[48,4096]{1,0:T(8,128)(2,1)S(1)} fusion(f32[18,4096]{1,0:T(8,128)} %shard_map.38, s32[18]{0:T(128)S(1)} %multiply_add_fusion.1), kind=kOutput, calls=%fused_computation | convolution fusion | flops 7349088 | bytes 688200 | tf_op jit(solution)/shard_map/dot_general | solution.py:307
  57.1 1.0 %convert_element_type.89.x_ref = bf16[16,1,3,4,1024]{4,3,2,1,0:T(4,128)(2,1)} reshape(bf16[48,4096]{1,0:T(8,128)(2,1)S(1)} %convolution_convert_fusion) | data formatting | bytes 786432 | tf_op jit(solution)/shard_map/convert_element_type | solution.py:308
  58.1 13.3 %shard_map.39 = bf16[16,1,3,4,1024]{4,3,2,1,0:T(4,128)(2,1)} custom-call(bf16[16,1,3,4,1024]{4,3,2,1,0:T(4,128)(2,1)} %convert_element_type.89.x_ref), custom_call_target="tpu_custom_call" | custom-call | tf_op jit(solution)/shard_map/pallas_call | solution.py:259
  71.5 2.0 %convert.1 = f32[1,1,48,4,1024]{4,3,2,1,0:T(4,128)} convert(bf16[1,1,48,4,1024]{4,3,2,1,0:T(4,128)(2,1)} %bitcast.16) | non-fusion elementwise | flops 196608 | bytes 1179648 | tf_op jit(solution)/shard_map/reshape | solution.py:310
  (9 shorter events, 0.1 us)
Async XLA Ops:
  0.0 14.7 %copy-start.1 = (s32[1,1,18,1]{2,3,1,0:T(1,128)S(1)}, s32[1,1,18,1]{2,3,1,0:T(1,128)}, u32[]{:S(2)}) copy-start(s32[1,1,18,1]{2,3,1,0:T(1,128)} %param.5) | copy-start | bytes 220
  5.5 23.3 %all-to-all-start = ((bf16[8,65,1024]{2,1,0:T(8,128)(2,1)}), bf16[8,65,1024]{2,1,0:T(8,128)(2,1)S(1)}, u32[]{:S(2)}, u32[]{:S(2)}) async-start(bf16[8,65,1024]{2,1,0:T(8,128)(2,1)} %shard_map.37), calls=%async_computation | async-start | bytes 2359296 | tf_op jit(solution)/shard_map/all_to_all | solution.py:283
  28.9 1.7 %copy-start = (bf16[8,65,1024]{2,1,0:T(8,128)(2,1)}, bf16[8,65,1024]{2,1,0:T(8,128)(2,1)S(1)}, u32[]{:S(2)}) copy-start(bf16[8,65,1024]{2,1,0:T(8,128)(2,1)S(1)} %all-to-all-done.panel) | copy-start | bytes 3194884

commit v21 on v16

--- a/solution.py
+++ b/solution.py
@@ -81,8 +81,8 @@
 
 def pair_rows(left_hot, right_hot, panel, cos_ref, sin_ref, target):
     part = cos_ref.shape[0]
-    left = left_hot[target]
-    right = right_hot[target]
+    left = left_hot[0, target]
+    right = left_hot[1, target]
 
     sources = panel.shape[0]
     channels = (panel.shape[1] - 1) // (WINDOWS * 2)
@@ -109,7 +109,7 @@
     return total + jnp.dot(imag_stack, sin_ref[...], preferred_element_type=jnp.float32)
 
 
-def pair_exchange_kernel(left_hot, right_hot, panel, cos_ref, sin_ref, out_ref, slots, received, local_sem,
+def pair_exchange_kernel(left_hot, panel, cos_ref, sin_ref, out_ref, slots, received, local_sem,
                          send_sem, recv_sem):
     n = slots.shape[0]
     me = lax.axis_index("chan")
@@ -122,7 +122,7 @@
     pl.semaphore_wait(barrier, n - 1)
 
     def fill(target):
-        slots[target] = pair_rows(left_hot, right_hot, panel, cos_ref, sin_ref, target).astype(slots.dtype)
+        slots[target] = pair_rows(left_hot, None, panel, cos_ref, sin_ref, target).astype(slots.dtype)
 
     def send(step):
         target = lax.rem(me + step, n)
@@ -177,8 +177,7 @@
 def pair_exchange(left_hot, right_hot, panel, cos_part, sin_part, chan_count, collective):
     rows = left_hot.shape[0]
     count = rows // chan_count
-    left_hot = left_hot.reshape(chan_count, count, -1)
-    right_hot = right_hot.reshape(chan_count, count, -1)
+    hots = jnp.stack([left_hot, right_hot]).reshape(2, chan_count, count, -1)
     part = cos_part.shape[0]
     pairs = BLK * BLK
     vmem = pl.BlockSpec(memory_space=pltpu.VMEM)
@@ -186,7 +185,7 @@
     return pl.pallas_call(
         pair_exchange_kernel,
         out_shape=jax.ShapeDtypeStruct((count // pairs, pairs * LAGS), jnp.float32),
-        in_specs=[vmem] * 5,
+        in_specs=[vmem] * 4,
         out_specs=vmem,
         scratch_shapes=[
             pltpu.VMEM((chan_count, count, LAGS), jnp.bfloat16),
@@ -203,7 +202,7 @@
             transcendentals=0,
             bytes_accessed=panel.size * 2 + 4 * part * LAGS + rows * LAGS * 2,
         ),
-    )(left_hot, right_hot, panel, cos_part, sin_part)
+    )(hots, panel, cos_part, sin_part)
 
 
 def exchange_kernel(axis, other_axis, axis_first, stride, x_ref, out_ref, local_sem, send_sem, recv_sem):
@@ -295,8 +294,9 @@
     channel_ids = jnp.arange(group_channels, dtype=jnp.int32)[None, :]
     left_ch = left_ch.reshape(chan_count, NB_SRC, BLK, BLK).transpose(0, 2, 3, 1)
     right_ch = right_ch.reshape(chan_count, NB_SRC, BLK, BLK).transpose(0, 2, 3, 1)
-    left_hot = (left_ch.reshape(-1, 1) == channel_ids).astype(jnp.bfloat16)
-    right_hot = (right_ch.reshape(-1, 1) == channel_ids).astype(jnp.bfloat16)
+    both = jnp.stack([left_ch.reshape(-1), right_ch.reshape(-1)])[:, :, None] == channel_ids[None]
+    both = both.astype(jnp.bfloat16)
+    left_hot, right_hot = both[0], both[1]
 
     cos_part, sin_part = table_slice(me * part, part)
     corr = pair_exchange(left_hot, right_hot, panel, cos_part, sin_part, chan_count, 0)

time: 73.7 us -> 73.7 us (level)
  no operation moved by 1% of the time
where the time goes in v21:
time: 73.7 us; the launch traced here: 73.3 us
  Pallas kernels  41.8 us (57%)
  waiting for transfers between devices  10.4 us (14%)
  other arithmetic  9.25 us (13%)
  starting transfers between devices  6.81 us (9%)
  local copies, waits for them, and re-layouts  3.7 us (5%)
  matrix products  1.25 us (2%)
    pallas_call x1, Pallas kernels, pair_exchange(): pl.pallas_call(pair_exchange_kernel, out_shape=jax.ShapeDtypeStruct((coun...  25.2 us
    pallas_call x1, Pallas kernels, exchange(): pl.pallas_call(functools.partial(exchange_kernel, axis, other_axis, axis_...  13.3 us
    all_to_all x1, waiting for transfers between devices, local(): got = lax.all_to_all(sent, 'chan', split_axis=0, concat_axis=0, tiled=True)  10.4 us
    all_to_all x1, starting transfers between devices, local(): got = lax.all_to_all(sent, 'chan', split_axis=0, concat_axis=0, tiled=True)  6.81 us
    pallas_call x1, Pallas kernels, whiten_chunks(): pl.pallas_call(whiten_kernel, out_shape=jax.ShapeDtypeStruct((chan_count,...  3.29 us
    convert_element_type x1, other arithmetic, table_slice(): sin_part = (-sin_ab * weight).astype(jnp.bfloat16)  2.45 us
    cos x1, other arithmetic, table_slice(): cos_b, sin_b = (jnp.cos(fine)[None, :, :], jnp.sin(fine)[None, :, :])  2.04 us
    reshape x1, other arithmetic, local(): return received.reshape(1, 1, slot_count, pairs, LAGS)  1.98 us
  transfers between devices with their start and end apart: 1, of which 1 were waited for; matrix products, arithmetic and copies ran while one was open for 8% of the time, Pallas kernels for 0%

profile of v21, /device:TPU:1, one launch (start us, length us, event | category | flops | bytes accessed | tf_op | source)
XLA Modules:
  0.0 73.3 jit_solution(8922881588324731269)
XLA Ops:
  0.0 0.0 copy-start.1
  0.0 1.5 %reshape.268.x_ref = bf16[64,8192]{1,0:T(8,128)(2,1)S(1)} reshape(bf16[16,2,2,8192]{3,2,1,0:T(2,128)(2,1)} %param.3) | data formatting | bytes 2097152 | tf_op jit(solution)/shard_map/reshape | solution.py:70
  1.5 0.8 %copy.6.blocks_ref = s32[1,1,18,2]{3,2,1,0:T(8,128)S(1)} copy(s32[1,1,18,2]{2,3,1,0:T(2,128)} %param.4) | data formatting | bytes 288 | tf_op args[1]
  2.3 3.3 %shard_map.37 = bf16[8,65,1024]{2,1,0:T(8,128)(2,1)} custom-call(bf16[64,8192]{1,0:T(8,128)(2,1)S(1)} %reshape.268.x_ref, s32[1,1,18,2]{3,2,1,0:T(8,128)S(1)} %copy.6.blocks_ref), custom_call_target="tpu_custom_call" | custom-call | flops 4194304 | bytes 2097152 | tf_op jit(solution)/shard_map/pallas_call | solution.py:72
  5.5 6.8 %all-to-all-start = ((bf16[8,65,1024]{2,1,0:T(8,128)(2,1)}), bf16[8,65,1024]{2,1,0:T(8,128)(2,1)S(1)}, u32[]{:S(2)}, u32[]{:S(2)}) async-start(bf16[8,65,1024]{2,1,0:T(8,128)(2,1)} %shard_map.37), calls=%async_computation | async-start | bytes 2359296 | tf_op jit(solution)/shard_map/all_to_all | solution.py:285
  12.4 2.0 %fusion.10 = (f32[128,1024]{1,0:T(8,128)S(1)}, f32[128,1024]{1,0:T(8,128)S(1)}) fusion(s32[1024]{0:T(1024)S(1)} %iota_add_fusion.2), kind=kLoop, calls=%fused_computation.19 | loop fusion | flops 1835008 | bytes 1052672 | tf_op jit(solution)/shard_map/cos | solution.py:29
  14.4 0.2 fusion.18
  14.7 0.0 copy-done.1
  14.7 0.2 convert_reduce_fusion
  14.8 1.2 %add_negate_fusion = (f32[8,128,1024]{2,1,0:T(8,128)S(1)}, f32[8,128,1024]{2,1,0:T(8,128)S(1)}) fusion(f32[128,1024]{1,0:T(8,128)S(1)} %get-tuple-element.14, f32[8,1024]{1,0:T(8,128)S(1)} %get-tuple-element.10, f32[128,1024]{1,0:T(8,128)S(1)} %get-tuple-element.13, f32[8,1024]{1,0:T(8,128)S(1)} %get-tuple-element.9), kind=kLoop, calls=%fused_computation.5 | loop fusion | flops 7340032 | bytes 9502720 | tf_op jit(solution)/shard_map/neg | solution.py:35
  16.0 2.4 %fusion = (bf16[1024,1024]{1,0:T(8,128)(2,1)}, bf16[1024,1024]{1,0:T(8,128)(2,1)}) fusion(f32[8,128,1024]{2,1,0:T(8,128)S(1)} %get-tuple-element.7, f32[1024]{0:T(1024)S(1)} %select_multiply_fusion, f32[8,128,1024]{2,1,0:T(8,128)S(1)} %get-tuple-element.8), kind=kLoop, calls=%fused_computation.2 | loop fusion | flops 4194304 | bytes 12587008 | tf_op jit(solution)/shard_map/convert_element_type | solution.py:35
  18.5 10.4 %all-to-all-done.panel = bf16[8,65,1024]{2,1,0:T(8,128)(2,1)S(1)} async-done(((bf16[8,65,1024]{2,1,0:T(8,128)(2,1)}), bf16[8,65,1024]{2,1,0:T(8,128)(2,1)S(1)}, u32[]{:S(2)}, u32[]{:S(2)}) %all-to-all-start) | async-done | bytes 1064992 | tf_op jit(solution)/shard_map/all_to_all | solution.py:285
  28.9 0.0 copy-start
  28.9 0.1 convert_element_type.76
  29.0 0.2 fusion.13
  29.2 0.1 mul.203
  29.3 0.1 stack.8
  29.4 0.1 mul.205
  29.5 0.1 stack.9
  29.6 0.9 %fusion.2.left_hot = bf16[2,8,72,128]{3,2,1,0:T(8,128)(2,1)} fusion(s32[2,8,72]{2,1,0:T(8,128)S(1)} %pad_add_fusion), kind=kLoop, calls=%fused_computation.11 | loop fusion | flops 294912 | bytes 299520 | tf_op jit(solution)/shard_map/convert_element_type | solution.py:298
  30.5 0.0 copy-done
  30.5 25.2 %shard_map.38 = f32[18,4096]{1,0:T(8,128)} custom-call(bf16[2,8,72,128]{3,2,1,0:T(8,128)(2,1)} %fusion.2.left_hot, bf16[8,65,1024]{2,1,0:T(8,128)(2,1)} %copy-done, bf16[1024,1024]{1,0:T(8,128)(2,1)} %get-tuple-element.12.cos_ref, bf16[1024,1024]{1,0:T(8,128)(2,1)} %get-tuple-element.11.sin_ref), custom_call_target="tpu_custom_call" | custom-call | flops 3642753024 | bytes 6438912 | tf_op jit(solution)/shard_map/pallas_call | solution.py:185
  55.7 1.2 %convolution_convert_fusion = bf16[48,4096]{1,0:T(8,128)(2,1)S(1)} fusion(f32[18,4096]{1,0:T(8,128)} %shard_map.38, s32[18]{0:T(128)S(1)} %multiply_add_fusion.1), kind=kOutput, calls=%fused_computation | convolution fusion | flops 7349088 | bytes 688200 | tf_op jit(solution)/shard_map/dot_general | solution.py:310
  57.0 1.0 %convert_element_type.84.x_ref = bf16[16,1,3,4,1024]{4,3,2,1,0:T(4,128)(2,1)} reshape(bf16[48,4096]{1,0:T(8,128)(2,1)S(1)} %convolution_convert_fusion) | data formatting | bytes 786432 | tf_op jit(solution)/shard_map/convert_element_type | solution.py:311
  58.0 13.3 %shard_map.39 = bf16[16,1,3,4,1024]{4,3,2,1,0:T(4,128)(2,1)} custom-call(bf16[16,1,3,4,1024]{4,3,2,1,0:T(4,128)(2,1)} %convert_element_type.84.x_ref), custom_call_target="tpu_custom_call" | custom-call | tf_op jit(solution)/shard_map/pallas_call | solution.py:261
  71.4 2.0 %convert.1 = f32[1,1,48,4,1024]{4,3,2,1,0:T(4,128)} convert(bf16[1,1,48,4,1024]{4,3,2,1,0:T(4,128)(2,1)} %bitcast.16) | non-fusion elementwise | flops 196608 | bytes 1179648 | tf_op jit(solution)/shard_map/reshape | solution.py:313
  (10 shorter events, 0.1 us)
Async XLA Ops:
  0.0 14.7 %copy-start.1 = (s32[1,1,18,1]{2,3,1,0:T(1,128)S(1)}, s32[1,1,18,1]{2,3,1,0:T(1,128)}, u32[]{:S(2)}) copy-start(s32[1,1,18,1]{2,3,1,0:T(1,128)} %param.5) | copy-start | bytes 220
  5.5 23.3 %all-to-all-start = ((bf16[8,65,1024]{2,1,0:T(8,128)(2,1)}), bf16[8,65,1024]{2,1,0:T(8,128)(2,1)S(1)}, u32[]{:S(2)}, u32[]{:S(2)}) async-start(bf16[8,65,1024]{2,1,0:T(8,128)(2,1)} %shard_map.37), calls=%async_computation | async-start | bytes 2359296 | tf_op jit(solution)/shard_map/all_to_all | solution.py:285
  28.9 1.6 %copy-start = (bf16[8,65,1024]{2,1,0:T(8,128)(2,1)}, bf16[8,65,1024]{2,1,0:T(8,128)(2,1)S(1)}, u32[]{:S(2)}) copy-start(bf16[8,65,1024]{2,1,0:T(8,128)(2,1)S(1)} %all-to-all-done.panel) | copy-start | bytes 3194884

commit v22 on v16

--- a/solution.py
+++ b/solution.py
@@ -258,12 +258,12 @@
 
 def exchange(x, axis, other_axis, axis_first, stride, collective):
     n = x.shape[0]
-    vmem = pl.BlockSpec(memory_space=pltpu.VMEM)
+    anywhere = pl.BlockSpec(memory_space=pl.ANY)
     return pl.pallas_call(
         functools.partial(exchange_kernel, axis, other_axis, axis_first, stride),
         out_shape=jax.ShapeDtypeStruct(x.shape, x.dtype),
-        in_specs=[vmem],
-        out_specs=vmem,
+        in_specs=[anywhere],
+        out_specs=anywhere,
         scratch_shapes=[
             pltpu.SemaphoreType.DMA(()),
             pltpu.SemaphoreType.DMA((n, x.shape[1])),

time: 73.7 us -> 72.3 us (0.981)
  Pallas kernels: 41.9 us -> 40.5 us
    pallas_call x1, Pallas kernels: 13.4 us -> 11.9 us  [exchange(): pl.pallas_call(functools.partial(exchange_kernel, axis, other_axis, axis_...]
where the time goes in v22:
time: 72.3 us; the launch traced here: 72 us
  Pallas kernels  40.5 us (56%)
  waiting for transfers between devices  10.4 us (14%)
  other arithmetic  9.28 us (13%)
  starting transfers between devices  6.81 us (9%)
  local copies, waits for them, and re-layouts  3.7 us (5%)
  matrix products  1.24 us (2%)
    pallas_call x1, Pallas kernels, pair_exchange(): pl.pallas_call(pair_exchange_kernel, out_shape=jax.ShapeDtypeStruct((coun...  25.2 us
    pallas_call x1, Pallas kernels, exchange(): pl.pallas_call(functools.partial(exchange_kernel, axis, other_axis, axis_...  11.9 us
    all_to_all x1, waiting for transfers between devices, local(): got = lax.all_to_all(sent, 'chan', split_axis=0, concat_axis=0, tiled=True)  10.4 us
    all_to_all x1, starting transfers between devices, local(): got = lax.all_to_all(sent, 'chan', split_axis=0, concat_axis=0, tiled=True)  6.81 us
    pallas_call x1, Pallas kernels, whiten_chunks(): pl.pallas_call(whiten_kernel, out_shape=jax.ShapeDtypeStruct((chan_count,...  3.29 us
    convert_element_type x1, other arithmetic, table_slice(): sin_part = (-sin_ab * weight).astype(jnp.bfloat16)  2.45 us
    cos x1, other arithmetic, table_slice(): cos_b, sin_b = (jnp.cos(fine)[None, :, :], jnp.sin(fine)[None, :, :])  2.04 us
    reshape x1, other arithmetic, local(): return received.reshape(1, 1, slot_count, pairs, LAGS)  1.98 us
  transfers between devices with their start and end apart: 1, of which 1 were waited for; matrix products, arithmetic and copies ran while one was open for 8% of the time, Pallas kernels for 0%

profile of v22, /device:TPU:1, one launch (start us, length us, event | category | flops | bytes accessed | tf_op | source)
XLA Modules:
  0.0 72.0 jit_solution(15696912030843749910)
XLA Ops:
  0.0 0.0 copy-start.1
  0.0 1.5 %reshape.282.x_ref = bf16[64,8192]{1,0:T(8,128)(2,1)S(1)} reshape(bf16[16,2,2,8192]{3,2,1,0:T(2,128)(2,1)} %param.3) | data formatting | bytes 2097152 | tf_op jit(solution)/shard_map/reshape | solution.py:70
  1.5 0.8 %copy.6.blocks_ref = s32[1,1,18,2]{3,2,1,0:T(8,128)S(1)} copy(s32[1,1,18,2]{2,3,1,0:T(2,128)} %param.4) | data formatting | bytes 288 | tf_op args[1]
  2.3 3.3 %shard_map.37 = bf16[8,65,1024]{2,1,0:T(8,128)(2,1)} custom-call(bf16[64,8192]{1,0:T(8,128)(2,1)S(1)} %reshape.282.x_ref, s32[1,1,18,2]{3,2,1,0:T(8,128)S(1)} %copy.6.blocks_ref), custom_call_target="tpu_custom_call" | custom-call | flops 4194304 | bytes 2097152 | tf_op jit(solution)/shard_map/pallas_call | solution.py:72
  5.5 6.8 %all-to-all-start = ((bf16[8,65,1024]{2,1,0:T(8,128)(2,1)}), bf16[8,65,1024]{2,1,0:T(8,128)(2,1)S(1)}, u32[]{:S(2)}, u32[]{:S(2)}) async-start(bf16[8,65,1024]{2,1,0:T(8,128)(2,1)} %shard_map.37), calls=%async_computation | async-start | bytes 2359296 | tf_op jit(solution)/shard_map/all_to_all | solution.py:286
  12.4 2.0 %fusion.11 = (f32[128,1024]{1,0:T(8,128)S(1)}, f32[128,1024]{1,0:T(8,128)S(1)}) fusion(s32[1024]{0:T(1024)S(1)} %iota_add_fusion.2), kind=kLoop, calls=%fused_computation.21 | loop fusion | flops 1835008 | bytes 1052672 | tf_op jit(solution)/shard_map/cos | solution.py:29
  14.4 0.2 fusion.19
  14.7 0.0 copy-done.1
  14.7 0.2 convert_reduce_fusion
  14.8 1.2 %add_negate_fusion = (f32[8,128,1024]{2,1,0:T(8,128)S(1)}, f32[8,128,1024]{2,1,0:T(8,128)S(1)}) fusion(f32[128,1024]{1,0:T(8,128)S(1)} %get-tuple-element.14, f32[8,1024]{1,0:T(8,128)S(1)} %get-tuple-element.10, f32[128,1024]{1,0:T(8,128)S(1)} %get-tuple-element.13, f32[8,1024]{1,0:T(8,128)S(1)} %get-tuple-element.9), kind=kLoop, calls=%fused_computation.5 | loop fusion | flops 7340032 | bytes 9502720 | tf_op jit(solution)/shard_map/neg | solution.py:35
  16.0 2.4 %fusion = (bf16[1024,1024]{1,0:T(8,128)(2,1)}, bf16[1024,1024]{1,0:T(8,128)(2,1)}) fusion(f32[8,128,1024]{2,1,0:T(8,128)S(1)} %get-tuple-element.7, f32[1024]{0:T(1024)S(1)} %select_multiply_fusion, f32[8,128,1024]{2,1,0:T(8,128)S(1)} %get-tuple-element.8), kind=kLoop, calls=%fused_computation.2 | loop fusion | flops 4194304 | bytes 12587008 | tf_op jit(solution)/shard_map/convert_element_type | solution.py:35
  18.5 10.4 %all-to-all-done.panel = bf16[8,65,1024]{2,1,0:T(8,128)(2,1)S(1)} async-done(((bf16[8,65,1024]{2,1,0:T(8,128)(2,1)}), bf16[8,65,1024]{2,1,0:T(8,128)(2,1)S(1)}, u32[]{:S(2)}, u32[]{:S(2)}) %all-to-all-start) | async-done | bytes 1064992 | tf_op jit(solution)/shard_map/all_to_all | solution.py:286
  28.9 0.0 copy-start
  28.9 0.1 convert_element_type.80
  29.0 0.2 fusion.13
  29.2 0.1 mul.203
  29.3 0.1 eq.78
  29.4 0.1 mul.205
  29.5 0.1 eq.82
  29.6 0.9 %fusion.8 = (bf16[8,72,128]{2,1,0:T(8,128)(2,1)}, bf16[8,72,128]{2,1,0:T(8,128)(2,1)}) fusion(s32[8,72]{1,0:T(8,128)S(1)} %eq.78, s32[8,72]{1,0:T(8,128)S(1)} %eq.82), kind=kLoop, calls=%fused_computation.18 | loop fusion | flops 294912 | bytes 299520 | tf_op jit(solution)/shard_map/convert_element_type | solution.py:298
  30.5 0.0 copy-done
  30.5 25.2 %shard_map.38 = f32[18,4096]{1,0:T(8,128)} custom-call(bf16[8,72,128]{2,1,0:T(8,128)(2,1)} %get-tuple-element.15.left_hot, bf16[8,72,128]{2,1,0:T(8,128)(2,1)} %get-tuple-element.16.right_hot, bf16[8,65,1024]{2,1,0:T(8,128)(2,1)} %copy-done, bf16[1024,1024]{1,0:T(8,128)(2,1)} %get-tuple-element.12.cos_ref, bf16[1024,1024]{1,0:T(8,128)(2,1)} %get-tuple-element.11.sin_ref), custom_call_target="tpu_custom_call" | custom-call | flops 3642753024 | bytes 6438912 | tf_op jit(solution)/shard_map/pallas_call | solution.py:186
  55.8 1.2 %convolution_convert_fusion = bf16[48,4096]{1,0:T(8,128)(2,1)S(1)} fusion(f32[18,4096]{1,0:T(8,128)} %shard_map.38, s32[18]{0:T(128)S(1)} %multiply_add_fusion.1), kind=kOutput, calls=%fused_computation | convolution fusion | flops 7349088 | bytes 688200 | tf_op jit(solution)/shard_map/dot_general | solution.py:310
  57.0 1.0 %convert_element_type.89.x_ref = bf16[16,1,3,4,1024]{4,3,2,1,0:T(4,128)(2,1)} reshape(bf16[48,4096]{1,0:T(8,128)(2,1)S(1)} %convolution_convert_fusion) | data formatting | bytes 786432 | tf_op jit(solution)/shard_map/convert_element_type | solution.py:311
  58.1 11.9 %shard_map.39 = bf16[16,1,3,4,1024]{4,3,2,1,0:T(4,128)(2,1)} custom-call(bf16[16,1,3,4,1024]{4,3,2,1,0:T(4,128)(2,1)} %convert_element_type.89.x_ref), custom_call_target="tpu_custom_call" | custom-call | tf_op jit(solution)/shard_map/pallas_call | solution.py:262
  70.0 2.0 %convert.1 = f32[1,1,48,4,1024]{4,3,2,1,0:T(4,128)} convert(bf16[1,1,48,4,1024]{4,3,2,1,0:T(4,128)(2,1)} %bitcast.16) | non-fusion elementwise | flops 196608 | bytes 1179648 | tf_op jit(solution)/shard_map/reshape | solution.py:313
  (9 shorter events, 0.1 us)
Async XLA Ops:
  0.0 14.7 %copy-start.1 = (s32[1,1,18,1]{2,3,1,0:T(1,128)S(1)}, s32[1,1,18,1]{2,3,1,0:T(1,128)}, u32[]{:S(2)}) copy-start(s32[1,1,18,1]{2,3,1,0:T(1,128)} %param.5) | copy-start | bytes 220
  5.5 23.3 %all-to-all-start = ((bf16[8,65,1024]{2,1,0:T(8,128)(2,1)}), bf16[8,65,1024]{2,1,0:T(8,128)(2,1)S(1)}, u32[]{:S(2)}, u32[]{:S(2)}) async-start(bf16[8,65,1024]{2,1,0:T(8,128)(2,1)} %shard_map.37), calls=%async_computation | async-start | bytes 2359296 | tf_op jit(solution)/shard_map/all_to_all | solution.py:286
  28.9 1.7 %copy-start = (bf16[8,65,1024]{2,1,0:T(8,128)(2,1)}, bf16[8,65,1024]{2,1,0:T(8,128)(2,1)S(1)}, u32[]{:S(2)}) copy-start(bf16[8,65,1024]{2,1,0:T(8,128)(2,1)S(1)} %all-to-all-done.panel) | copy-start | bytes 3194884
